TPU v7x, 256 devices: a whole 4x4x8 slice. The times are simulated.
256 devices in a mesh: dp: 8 (over y, z_lo), tensor: 32 (over x, z_hi, core).
Axes of the slice: x: 4, y: 4, z: 8 (z_hi: 4, z_lo: 2; z = z_hi * 2 + z_lo), core: 2. Of those that a mesh axis runs over, the one named last changes fastest.
Arguments:
- hidden_in: bfloat16 [6144, 2304], P(('dp', 'tensor')), parts along dimension 0, may hold values from -6 to 6
- attn_gain: bfloat16 [2304], replicated, may hold values from 0.099609375 to 1.8984375
- w_query: bfloat16 [2304, 2048], P(None, 'tensor'), may hold values from -0.125 to 0.125
- w_key: bfloat16 [2304, 2048], P(None, 'tensor'), may hold values from -0.25 to 0.25
- w_value: bfloat16 [2304, 2048], P(None, 'tensor'), may hold values from -0.375 to 0.375
- w_out: bfloat16 [2048, 2304], P('tensor'), may hold values from -0.125 to 0.125
- cache_k: bfloat16 [64, 32, 2048, 64], P('dp', 'tensor'), parts along dimension 0, may hold values from -250 to 250
- cache_v: bfloat16 [64, 32, 2048, 64], P('dp', 'tensor'), parts along dimension 0, may hold values from -16 to 16
- cache_len: int32 [64], P('dp'), parts along dimension 0, may hold values from 1 to 2048, as said below
- ffn_gain: bfloat16 [2304], replicated, may hold values from 0.099609375 to 1.8984375
- router: bfloat16 [2304, 4], replicated, may hold values from -0.375 to 0.375
- routes: int32 [6144, 2], P('dp'), parts along dimension 0, may hold values from 0 to 3, all different within a row; in each aligned block of 768 rows (0 to 767, 768 to 1535, ...) at most 576 rows name the same one
- w_gate_up: bfloat16 [4, 2, 2304, 4096], P(None, None, None, 'tensor'), may hold values from -0.125 to 0.125
- w_down: bfloat16 [4, 4096, 2304], P(None, 'tensor'), may hold values from -0.09375 to 0.09375
Outputs:
- block_out: bfloat16 [6144, 2304], P(('dp', 'tensor')), parts along dimension 0
There are 8 independent parts, one for each index of `dp`. A program takes and returns all parts, laid end to end along the dimension named above; an argument that names none is the same for every part. Nothing has to cross between parts.
Inputs may be any that keep to these rules, and one draw needn't show every extreme that they name: `cache_len`: some request's cache is full in every draw. `routes`: each token names two different experts; no expert is named by more than 576 tokens of the group, and one is named by exactly 576.
All inputs are finite; a program needn't handle non-finite values.
Results may differ from a plain program's by a relative error of at most 0.019.
The roundings to bfloat16 on the way count: a program that leaves them out, or rounds other values in their place, can miss the bound.
Values may be sent and summed in bfloat16 or wider, within the bound.
A program may use at most 128 MiB of HBM per device.

v0:
```python
import jax
import jax.numpy as jnp
from jax import lax
from jax.sharding import PartitionSpec as P

HDIM = 64
REQS = 8
NEW = 96
TOKENS = 768


eps = 1e-05


def rms_scale(rows_in, gain):
    values = rows_in.astype(jnp.float32)
    mean_square = jnp.mean(values * values, axis=-1, keepdims=True)
    return (values * lax.rsqrt(mean_square + eps) * gain.astype(jnp.float32)).astype(jnp.bfloat16)


def rotate(values, positions):
    half_dim = values.shape[-1] // 2
    inverse = 10000.0 ** (-2.0 * jnp.arange(half_dim, dtype=jnp.float32) / values.shape[-1])
    angles = positions.astype(jnp.float32)[:, None] * inverse[None, :]
    cosine = jnp.cos(angles)[:, None, :]
    sine_part = jnp.sin(angles)[:, None, :]
    front = values[..., :half_dim]
    back = values[..., half_dim:]
    return jnp.concatenate(
        [front * cosine - back * sine_part, back * cosine + front * sine_part], axis=-1
    )


def route_weights(logits, routes):
    expert_iota = jnp.arange(logits.shape[1], dtype=jnp.int32)[None, :]
    first_logit = jnp.sum(jnp.where(routes[:, 0:1] == expert_iota, logits, 0.0), axis=1)
    second_logit = jnp.sum(jnp.where(routes[:, 1:2] == expert_iota, logits, 0.0), axis=1)
    first_weight = 1.0 / (1.0 + jnp.exp(second_logit - first_logit))
    second_weight = 1.0 / (1.0 + jnp.exp(first_logit - second_logit))
    return jnp.stack([first_weight, second_weight], axis=1)


def expert_apply(rows_in, gate_up, down_part):
    both = jnp.einsum("td,kdf->ktf", rows_in, gate_up, preferred_element_type=jnp.float32)
    inner = (jax.nn.silu(both[0]) * both[1]).astype(jnp.bfloat16)
    return jnp.dot(inner, down_part, preferred_element_type=jnp.float32)


def attend(query, key_new, value_new, cache_k, cache_v, cache_len):
    cached_scores = (
        jnp.einsum("rhqd,rhkd->rhqk", query, cache_k, preferred_element_type=jnp.float32) * 0.125
    )
    fresh_scores = (
        jnp.einsum("rhqd,rhkd->rhqk", query, key_new, preferred_element_type=jnp.float32) * 0.125
    )
    key_pos = jnp.arange(cache_k.shape[2], dtype=jnp.int32)
    cached_mask = key_pos[None, None, None, :] < cache_len[:, None, None, None]
    new_pos = jnp.arange(query.shape[2], dtype=jnp.int32)
    fresh_mask = (new_pos[:, None] >= new_pos[None, :])[None, None]
    cached_scores = jnp.where(cached_mask, cached_scores, -1e30)
    fresh_scores = jnp.where(fresh_mask, fresh_scores, -1e30)
    peak = jnp.maximum(
        jnp.max(cached_scores, axis=-1, keepdims=True),
        jnp.max(fresh_scores, axis=-1, keepdims=True),
    )
    cached_expo = jnp.exp(cached_scores - peak)
    fresh_expo = jnp.exp(fresh_scores - peak)
    denominator = jnp.sum(cached_expo, axis=-1, keepdims=True) + jnp.sum(
        fresh_expo, axis=-1, keepdims=True
    )
    mixed = jnp.einsum(
        "rhqk,rhkd->rhqd",
        cached_expo.astype(jnp.bfloat16),
        cache_v,
        preferred_element_type=jnp.float32,
    )
    mixed = mixed + jnp.einsum(
        "rhqk,rhkd->rhqd",
        fresh_expo.astype(jnp.bfloat16),
        value_new,
        preferred_element_type=jnp.float32,
    )
    return (mixed / denominator).astype(jnp.bfloat16)


def local(
    hidden_in,
    attn_gain,
    w_query,
    w_key,
    w_value,
    w_out,
    cache_k,
    cache_v,
    cache_len,
    ffn_gain,
    router,
    routes,
    w_gate_up,
    w_down,
):
    width = hidden_in.shape[1]
    head_dev = cache_k.shape[1]
    n_experts = w_gate_up.shape[0]
    whole_in = lax.all_gather(hidden_in, "tensor", axis=0, tiled=True)
    normed = rms_scale(whole_in, attn_gain)
    positions = (cache_len[:, None] + jnp.arange(NEW, dtype=jnp.int32)[None, :]).reshape(-1)

    def project(weight):
        return jnp.dot(normed, weight, preferred_element_type=jnp.float32).reshape(
            TOKENS, head_dev, HDIM
        )

    def by_request(values):
        return values.reshape(REQS, NEW, head_dev, HDIM).transpose(0, 2, 1, 3)

    query = rotate(project(w_query), positions).astype(jnp.bfloat16)
    key_new = rotate(project(w_key), positions).astype(jnp.bfloat16)
    value_new = project(w_value).astype(jnp.bfloat16)
    heads_out = attend(
        by_request(query), by_request(key_new), by_request(value_new), cache_k, cache_v, cache_len
    )
    heads_flat = heads_out.transpose(0, 2, 1, 3).reshape(TOKENS, head_dev * HDIM)
    attn = lax.psum_scatter(
        jnp.dot(heads_flat, w_out, preferred_element_type=jnp.float32).astype(jnp.bfloat16),
        "tensor",
        scatter_dimension=0,
        tiled=True,
    ).astype(jnp.float32)
    middle = (hidden_in.astype(jnp.float32) + attn).astype(jnp.bfloat16)
    normed2 = lax.all_gather(rms_scale(middle, ffn_gain), "tensor", axis=0, tiled=True)
    logits = jnp.dot(normed2, router, preferred_element_type=jnp.float32)
    pair_weights = route_weights(logits, routes)
    running = jnp.zeros((TOKENS, width), jnp.float32)
    for expert in range(n_experts):
        dense_weight = jnp.sum(jnp.where(routes == expert, pair_weights, 0.0), axis=1)
        running = (
            running
            + expert_apply(normed2, w_gate_up[expert], w_down[expert]) * dense_weight[:, None]
        )
    expert_out = lax.psum_scatter(
        running.astype(jnp.bfloat16), "tensor", scatter_dimension=0, tiled=True
    ).astype(jnp.float32)
    return (middle.astype(jnp.float32) + expert_out).astype(jnp.bfloat16)


def solution(mesh):
    in_specs = (
        P(("dp", "tensor"), None),
        P(),
        P(None, "tensor"),
        P(None, "tensor"),
        P(None, "tensor"),
        P("tensor", None),
        P("dp", "tensor", None, None),
        P("dp", "tensor", None, None),
        P("dp"),
        P(),
        P(),
        P("dp", None),
        P(None, None, None, "tensor"),
        P(None, "tensor", None),
    )
    out_specs = P(("dp", "tensor"), None)
    return jax.shard_map(local, mesh=mesh, in_specs=in_specs, out_specs=out_specs, check_vma=False)
```

profile of v0, /device:TPU:22, one launch (start us, length us, event | category | flops | bytes accessed | tf_op | source)
XLA Modules:
  0.0 364.0 jit_solution(10430601139574200619)
XLA Ops:
  6.5 0.7 all-gather.3.cloned.1.call-update
  7.3 0.7 add_convert_fusion.2
  8.1 0.7 convert_element_type.104
  8.8 0.7 iota_compare_fusion
  9.6 62.4 %all-gather.3.cloned.1.call-done = bf16[768,2304]{1,0:T(8,128)(2,1)} async-done(((bf16[24,2304]{1,0:T(8,128)(2,1)}), bf16[768,2304]{1,0:T(8,128)(2,1)}) %all-gather.3.cloned.1.call-update) | async-done | bytes 3538960 | tf_op jit(solution)/shard_map/all_gather | solution.py:105
  71.9 2.9 fusion
  75.0 0.9 fusion.2
  75.9 1.7 copy-done.1
  77.6 1.2 convolution_convert_fusion.1
  79.0 3.3 convolution_bitcast_fusion
  82.4 1.2 convolution_bitcast_fusion.1
  83.6 0.5 fusion.91
  84.7 1.1 fusion.3
  85.8 0.3 fusion.105
  86.2 1.5 fusion.4
  87.7 1.5 fusion.14
  89.8 2.9 convolution_convert_fusion
  92.7 90.5 %reduce-scatter.3.cloned.1.call-done = bf16[24,2304]{1,0:T(8,128)(2,1)} async-done(((bf16[768,2304]{1,0:T(8,128)(2,1)}), bf16[24,2304]{1,0:T(8,128)(2,1)}) %reduce-scatter.3.cloned.1.call-update) | async-done | bytes 110608 | tf_op jit(solution)/shard_map/reduce_scatter | solution.py:124
  183.2 1.0 fusion.60
  184.3 1.6 fusion.62
  186.2 57.6 %all-gather.5.cloned.1.call-done = bf16[768,2304]{1,0:T(8,128)(2,1)} async-done(((bf16[24,2304]{1,0:T(8,128)(2,1)}), bf16[768,2304]{1,0:T(8,128)(2,1)}) %all-gather.5.cloned.1.call-update) | async-done | bytes 3538960 | tf_op jit(solution)/shard_map/all_gather | solution.py:131
  243.8 3.2 select_reduce_fusion.1
  247.1 2.5 fusion.20
  249.6 1.1 fusion.48
  250.8 1.1 fusion.26
  251.9 1.1 fusion.44
  253.0 1.1 fusion.23
  254.1 4.0 %fusion.46 = f32[768,2304]{1,0:T(8,128)} fusion(bf16[4,128,2304]{2,1,0:T(8,128)(2,1)S(1)} %copy-done.5, f32[2,768,128]{2,1,0:T(8,128)S(1)} %fusion.23), kind=kOutput, calls=%fused_computation.48 | convolution fusion | flops 453574656 | bytes 8454144 | tf_op jit(solution)/shard_map/dot_general | solution.py:46
  258.1 1.1 fusion.29
  259.2 6.1 %add_convert_fusion = bf16[768,2304]{1,0:T(8,128)(2,1)} fusion(f32[768,2304]{1,0:T(8,128)S(1)} %fusion.44, f32[768,2304]{1,0:T(8,128)} %fusion.46, f32[768,2304]{1,0:T(8,128)S(1)} %fusion.48, f32[768]{0:T(1024)S(1)} %get-tuple-element.7, f32[768]{0:T(1024)S(1)} %get-tuple-element.8, f32[768]{0:T(1024)S(1)} %get-tuple-element.6, ...), kind=kOutput, calls=%fused_computation.5 | convolution fusion | flops 467730432 | bytes 26165248 | tf_op jit(solution)/shard_map/dot_general | solution.py:46
  265.3 90.6 %reduce-scatter.5.cloned.1.call-done = bf16[24,2304]{1,0:T(8,128)(2,1)} async-done(((bf16[768,2304]{1,0:T(8,128)(2,1)}), bf16[24,2304]{1,0:T(8,128)(2,1)}) %reduce-scatter.5.cloned.1.call-update) | async-done | bytes 110608 | tf_op jit(solution)/shard_map/reduce_scatter | solution.py:141
  355.9 1.6 fusion.63
  (69 shorter events, 2.1 us)
Async XLA Ops:
  6.5 78.1 %copy-start = (bf16[8,1,2048,64]{2,3,1,0:T(8,128)(2,1)S(1)}, bf16[8,1,2048,64]{2,3,1,0:T(8,128)(2,1)}, u32[]{:S(2)}) copy-start(bf16[8,1,2048,64]{2,3,1,0:T(8,128)(2,1)} %param.20) | copy-start | bytes 6291460
  6.5 65.4 %all-gather.3.cloned.1.call-start = ((), (), s32[]{:S(2)}) async-start(), calls=%async_computation.2 | async-start | bytes 3649536 | tf_op jit(solution)/shard_map/all_gather | solution.py:105
  7.3 176.0 %reduce-scatter.3.cloned.1.call-start = ((), (), s32[]{:S(2)}) async-start(), calls=%async_computation.3 | async-start | bytes 3649536 | tf_op jit(solution)/shard_map/reduce_scatter | solution.py:124
  71.9 3.1 copy-start.3
  75.0 2.6 copy-start.8
  75.9 1.8 copy-start.1
  77.6 1.4 copy-start.9
  78.8 3.6 copy-start.10
  79.0 3.4 copy-start.2
  86.1 1.6 copy-start.15
  87.7 2.0 copy-start.11
  89.7 3.0 copy-start.14
  89.7 93.5 %copy-start.6 = (bf16[24,2304]{1,0:T(8,128)(2,1)S(1)}, bf16[24,2304]{1,0:T(8,128)(2,1)}, u32[]{:S(2)}) copy-start(bf16[24,2304]{1,0:T(8,128)(2,1)} %param.14) | copy-start | bytes 331780
  89.8 96.4 %copy-start.12 = (s32[768,2]{0,1:T(2,128)S(1)}, s32[768,2]{0,1:T(2,128)}, u32[]{:S(2)}) copy-start(s32[768,2]{0,1:T(2,128)} %param.25) | copy-start | bytes 18436
  89.8 154.0 %copy-start.13 = (bf16[2304,4]{0,1:T(4,128)(2,1)S(1)}, bf16[2304,4]{0,1:T(4,128)(2,1)}, u32[]{:S(2)}) copy-start(bf16[2304,4]{0,1:T(4,128)(2,1)} %param.24) | copy-start | bytes 55300
  92.7 151.1 %all-gather.5.cloned.1.call-start = ((), (), s32[]{:S(2)}) async-start(), calls=%async_computation.4 | async-start | bytes 3649536 | tf_op jit(solution)/shard_map/all_gather | solution.py:131
  185.9 170.0 %reduce-scatter.5.cloned.1.call-start = ((), (), s32[]{:S(2)}) async-start(), calls=%async_computation.5 | async-start | bytes 3649536 | tf_op jit(solution)/shard_map/reduce_scatter | solution.py:141
  243.8 3.3 copy-start.4
  247.0 2.5 copy-start.5
  247.0 3.6 slice-start
  249.6 1.2 slice-start.1
  265.3 90.6 %copy-start.7 = (bf16[24,2304]{1,0:T(8,128)(2,1)S(1)}, bf16[24,2304]{1,0:T(8,128)(2,1)}, u32[]{:S(2)}) copy-start(bf16[24,2304]{1,0:T(8,128)(2,1)} %reduce-scatter.3.cloned.1.call-done) | copy-start | bytes 331780
Sparse Core Ops, SparseCore 0:
  10.0 61.9 all-gather.2
  92.8 90.3 reduce-scatter.2
  186.0 57.6 all-gather.4
  265.4 90.4 reduce-scatter.4
where the time goes:
time: 366 us; the launch traced here: 364 us
  waiting for transfers between devices  302 us (83%)
  matrix products  32.9 us (9%)
  between operations  13.6 us (4%)
  other arithmetic  12.4 us (3%)
    reduce_scatter x1, waiting for transfers between devices, local(): lax.psum_scatter(running.astype(jnp.bfloat16), 'tensor', scatter_dimensio...  90.6 us
    reduce_scatter x1, waiting for transfers between devices, local(): lax.psum_scatter(jnp.dot(heads_flat, w_out, preferred_element_type=jnp.fl...  90.5 us
    all_gather x1, waiting for transfers between devices, local(): whole_in = lax.all_gather(hidden_in, 'tensor', axis=0, tiled=True)  62.4 us
    all_gather x1, waiting for transfers between devices, local(): lax.all_gather(rms_scale(middle, ffn_gain), 'tensor', axis=0, tiled=True)  57.6 us
    dot_general x4, matrix products, expert_apply(): return jnp.dot(inner, down_part, preferred_element_type=jnp.float32)  12.3 us
  transfers between devices with their start and end apart: 4, of which 4 were waited for; matrix products, arithmetic and copies ran while one was open for 1% of the time, Pallas kernels for 0%

commit v1 on v0

--- a/solution.py
+++ b/solution.py
@@ -1,6 +1,7 @@
 import jax
 import jax.numpy as jnp
 from jax import lax
+from jax.sharding import Mesh
 from jax.sharding import PartitionSpec as P
 
 HDIM = 64
@@ -8,6 +9,9 @@
 NEW = 96
 TOKENS = 768
 
+SUB = (("x", 4), ("zh", 4), ("core", 2))
+TENSOR = tuple(name for name, _ in SUB)
+SIZE = dict(SUB)
 
 eps = 1e-05
 
@@ -81,6 +85,65 @@
         preferred_element_type=jnp.float32,
     )
     return (mixed / denominator).astype(jnp.bfloat16)
+
+
+def shifts(axis, step):
+    n = SIZE[axis]
+    return [(i, (i + step) % n) for i in range(n)]
+
+
+def gather_stage(rows, axis):
+    n = SIZE[axis]
+    me = lax.axis_index(axis)
+    blk = rows.shape[0]
+    out = jnp.zeros((n * blk,) + rows.shape[1:], rows.dtype)
+    out = lax.dynamic_update_slice_in_dim(out, rows, me * blk, axis=0)
+    for step in range(1, n):
+        got = lax.ppermute(rows, axis, shifts(axis, step))
+        out = lax.dynamic_update_slice_in_dim(out, got, ((me - step) % n) * blk, axis=0)
+    return out
+
+
+def scatter_stage(rows, axis):
+    n = SIZE[axis]
+    me = lax.axis_index(axis)
+    chunks = rows.reshape((n, rows.shape[0] // n) + rows.shape[1:])
+    total = lax.dynamic_index_in_dim(chunks, me, axis=0, keepdims=False).astype(jnp.float32)
+    for step in range(1, n):
+        send = lax.dynamic_index_in_dim(chunks, (me + step) % n, axis=0, keepdims=False)
+        got = lax.ppermute(send.astype(jnp.bfloat16), axis, shifts(axis, step))
+        total = total + got.astype(jnp.float32)
+    return total
+
+
+def gather_rows(rows):
+    rows = gather_stage(rows, "zh")
+    rows = gather_stage(rows, "x")
+    return gather_stage(rows, "core")
+
+
+def scatter_rows(rows):
+    rows = scatter_stage(rows, "core")
+    rows = scatter_stage(rows.astype(jnp.bfloat16), "x")
+    return scatter_stage(rows.astype(jnp.bfloat16), "zh")
+
+
+def to_request_order(values):
+    nx, nz, nc = SIZE["x"], SIZE["zh"], SIZE["core"]
+    blk = TOKENS // (nx * nz * nc)
+    tail = values.shape[1:]
+    values = values.reshape((nc, nx, nz, blk) + tail)
+    values = jnp.moveaxis(values, 0, 2)
+    return values.reshape((TOKENS,) + tail)
+
+
+def from_request_order(values):
+    nx, nz, nc = SIZE["x"], SIZE["zh"], SIZE["core"]
+    blk = TOKENS // (nx * nz * nc)
+    tail = values.shape[1:]
+    values = values.reshape((nx, nz, nc, blk) + tail)
+    values = jnp.moveaxis(values, 2, 0)
+    return values.reshape((TOKENS,) + tail)
 
 
 def local(
@@ -102,9 +165,10 @@
     width = hidden_in.shape[1]
     head_dev = cache_k.shape[1]
     n_experts = w_gate_up.shape[0]
-    whole_in = lax.all_gather(hidden_in, "tensor", axis=0, tiled=True)
+    whole_in = gather_rows(hidden_in)
     normed = rms_scale(whole_in, attn_gain)
     positions = (cache_len[:, None] + jnp.arange(NEW, dtype=jnp.int32)[None, :]).reshape(-1)
+    positions = from_request_order(positions)
 
     def project(weight):
         return jnp.dot(normed, weight, preferred_element_type=jnp.float32).reshape(
@@ -112,6 +176,7 @@
         )
 
     def by_request(values):
+        values = to_request_order(values)
         return values.reshape(REQS, NEW, head_dev, HDIM).transpose(0, 2, 1, 3)
 
     query = rotate(project(w_query), positions).astype(jnp.bfloat16)
@@ -120,16 +185,14 @@
     heads_out = attend(
         by_request(query), by_request(key_new), by_request(value_new), cache_k, cache_v, cache_len
     )
-    heads_flat = heads_out.transpose(0, 2, 1, 3).reshape(TOKENS, head_dev * HDIM)
-    attn = lax.psum_scatter(
-        jnp.dot(heads_flat, w_out, preferred_element_type=jnp.float32).astype(jnp.bfloat16),
-        "tensor",
-        scatter_dimension=0,
-        tiled=True,
-    ).astype(jnp.float32)
+    heads_flat = from_request_order(heads_out.transpose(0, 2, 1, 3).reshape(TOKENS, head_dev * HDIM))
+    attn = scatter_rows(
+        jnp.dot(heads_flat, w_out, preferred_element_type=jnp.float32).astype(jnp.bfloat16)
+    )
     middle = (hidden_in.astype(jnp.float32) + attn).astype(jnp.bfloat16)
-    normed2 = lax.all_gather(rms_scale(middle, ffn_gain), "tensor", axis=0, tiled=True)
+    normed2 = gather_rows(rms_scale(middle, ffn_gain))
     logits = jnp.dot(normed2, router, preferred_element_type=jnp.float32)
+    routes = from_request_order(routes)
     pair_weights = route_weights(logits, routes)
     running = jnp.zeros((TOKENS, width), jnp.float32)
     for expert in range(n_experts):
@@ -138,28 +201,29 @@
             running
             + expert_apply(normed2, w_gate_up[expert], w_down[expert]) * dense_weight[:, None]
         )
-    expert_out = lax.psum_scatter(
-        running.astype(jnp.bfloat16), "tensor", scatter_dimension=0, tiled=True
-    ).astype(jnp.float32)
+    expert_out = scatter_rows(running.astype(jnp.bfloat16))
     return (middle.astype(jnp.float32) + expert_out).astype(jnp.bfloat16)
 
 
 def solution(mesh):
+    dp = mesh.shape["dp"]
+    fine = Mesh(mesh.devices.reshape((dp,) + tuple(n for _, n in SUB)), ("dp",) + TENSOR)
+    rows = ("dp",) + TENSOR
     in_specs = (
-        P(("dp", "tensor"), None),
+        P(rows, None),
         P(),
-        P(None, "tensor"),
-        P(None, "tensor"),
-        P(None, "tensor"),
-        P("tensor", None),
-        P("dp", "tensor", None, None),
-        P("dp", "tensor", None, None),
+        P(None, TENSOR),
+        P(None, TENSOR),
+        P(None, TENSOR),
+        P(TENSOR, None),
+        P("dp", TENSOR, None, None),
+        P("dp", TENSOR, None, None),
         P("dp"),
         P(),
         P(),
         P("dp", None),
-        P(None, None, None, "tensor"),
-        P(None, "tensor", None),
-    )
-    out_specs = P(("dp", "tensor"), None)
-    return jax.shard_map(local, mesh=mesh, in_specs=in_specs, out_specs=out_specs, check_vma=False)
+        P(None, None, None, TENSOR),
+        P(None, TENSOR, None),
+    )
+    out_specs = P(rows, None)
+    return jax.shard_map(local, mesh=fine, in_specs=in_specs, out_specs=out_specs, check_vma=False)

time: 366 us -> 231 us (0.63)
  the two profiles are of different devices: /device:TPU:22 before, /device:TPU:40 now
where the time goes in v1:
time: 231 us; the launch traced here: 226 us
  waiting for transfers between devices  118 us (51%)
  starting transfers between devices  48.2 us (21%)
  matrix products  30 us (13%)
  local copies, waits for them, and re-layouts  18.9 us (8%)
  other arithmetic  9.66 us (4%)
    ppermute x14, waiting for transfers between devices, scatter_stage(): got = lax.ppermute(send.astype(jnp.bfloat16), axis, shifts(axis, step))  62.9 us
    ppermute x14, waiting for transfers between devices, gather_stage(): got = lax.ppermute(rows, axis, shifts(axis, step))  55.3 us
    ppermute x14, starting transfers between devices, gather_stage(): got = lax.ppermute(rows, axis, shifts(axis, step))  26.7 us
    ppermute x14, starting transfers between devices, scatter_stage(): got = lax.ppermute(send.astype(jnp.bfloat16), axis, shifts(axis, step))  21.5 us
    dot_general x4, matrix products, expert_apply(): return jnp.dot(inner, down_part, preferred_element_type=jnp.float32)  12.3 us
    dot_general x4, matrix products, expert_apply(): jnp.einsum('td,kdf->ktf', rows_in, gate_up, preferred_element_type=jnp.fl...  6.68 us
    dynamic_update_slice x14, local copies, waits for them, and re-layouts, gather_stage(): lax.dynamic_update_slice_in_dim(out, got, (me - step) % n * blk, axis=0)  5.94 us
    dot_general x3, matrix products, project(): jnp.dot(normed, weight, preferred_element_type=jnp.float32)  5.73 us
  transfers between devices with their start and end apart: 28, of which 21 were waited for; matrix products, arithmetic and copies ran while one was open for 4% of the time, Pallas kernels for 0%

profile of v1, /device:TPU:40, one launch (start us, length us, event | category | flops | bytes accessed | tf_op | source)
XLA Modules:
  0.0 226.1 jit_solution(18387178674458039177)
XLA Ops:
  0.0 3.3 %collective-permute-start = (bf16[24,2304]{1,0:T(8,128)(2,1)}, bf16[24,2304]{1,0:T(8,128)(2,1)S(1)}, u32[]{:S(2)}, u32[]{:S(2)}) collective-permute-start(bf16[24,2304]{1,0:T(8,128)(2,1)} %param.14), channel_id=1, source_target_pairs={{0,2},{2,4},{4,6},{6,0},{1,3},{3,5},{5,7},{7,1},{8,10},{10,12},{12... | collective-permute-start | bytes 331784 | tf_op jit(solution)/shard_map/ppermute | solution.py:102
  5.6 4.9 %collective-permute-start.1 = (bf16[24,2304]{1,0:T(8,128)(2,1)}, bf16[24,2304]{1,0:T(8,128)(2,1)S(1)}, u32[]{:S(2)}, u32[]{:S(2)}) collective-permute-start(bf16[24,2304]{1,0:T(8,128)(2,1)} %param.14), channel_id=1, source_target_pairs={{0,4},{2,6},{4,0},{6,2},{1,5},{3,7},{5,1},{7,3},{8,12},{10,14},{12... | collective-permute-start | bytes 331784 | tf_op jit(solution)/shard_map/ppermute | solution.py:102
  11.6 8.2 %collective-permute-done.1 = bf16[24,2304]{1,0:T(8,128)(2,1)S(1)} collective-permute-done((bf16[24,2304]{1,0:T(8,128)(2,1)}, bf16[24,2304]{1,0:T(8,128)(2,1)S(1)}, u32[]{:S(2)}, u32[]{:S(2)}) %collective-permute-start.1) | collective-permute-done | bytes 110624 | tf_op jit(solution)/shard_map/ppermute | solution.py:102
  27.1 6.1 %collective-permute-done.3 = bf16[96,2304]{1,0:T(8,128)(2,1)S(1)} collective-permute-done((bf16[96,2304]{1,0:T(8,128)(2,1)S(1)}, bf16[96,2304]{1,0:T(8,128)(2,1)S(1)}, u32[]{:S(2)}, u32[]{:S(2)}) %collective-permute-start.3) | collective-permute-done | bytes 442400 | tf_op jit(solution)/shard_map/ppermute | solution.py:102
  34.0 9.0 %collective-permute-done.4 = bf16[96,2304]{1,0:T(8,128)(2,1)S(1)} collective-permute-done((bf16[96,2304]{1,0:T(8,128)(2,1)S(1)}, bf16[96,2304]{1,0:T(8,128)(2,1)S(1)}, u32[]{:S(2)}, u32[]{:S(2)}) %collective-permute-start.4) | collective-permute-done | bytes 442400 | tf_op jit(solution)/shard_map/ppermute | solution.py:102
  55.6 3.3 %convolution_bitcast_fusion = f32[768,1,64]{0,2,1:T(8,128)S(1)} fusion(bf16[768,2304]{1,0:T(8,128)(2,1)} %copy-done.2, bf16[2304,64]{0,1:T(8,128)(2,1)S(1)} %copy-done.8), kind=kOutput, calls=%fused_computation.48 | convolution fusion | flops 226492416 | bytes 4030464 | tf_op jit(solution)/shard_map/dot_general | solution.py:174
  69.8 3.7 %collective-permute-done.7 = bf16[384,2304]{1,0:T(8,128)(2,1)} collective-permute-done((bf16[384,2304]{1,0:T(8,128)(2,1)S(1)}, bf16[384,2304]{1,0:T(8,128)(2,1)}, u32[]{:S(2)}, u32[]{:S(2)}) %collective-permute-start.7) | collective-permute-done | bytes 1769504 | tf_op jit(solution)/shard_map/ppermute | solution.py:114
  73.5 2.4 %fusion.7 = bf16[384,2304]{1,0:T(8,128)(2,1)S(1)} fusion(bf16[384,2304]{1,0:T(8,128)(2,1)} %collective-permute-done.7, bf16[2,384,2304]{2,1,0:T(8,128)(2,1)} %bitcast.172, s32[]{:T(128)S(6)} %select_n.223), kind=kLoop, calls=%fused_computation.15 | loop fusion | flops 3538944 | bytes 5308420 | tf_op jit(solution)/shard_map/convert_element_type | solution.py:127
  80.4 11.1 %collective-permute-done.8 = bf16[96,2304]{1,0:T(8,128)(2,1)S(1)} collective-permute-done((bf16[96,2304]{1,0:T(8,128)(2,1)}, bf16[96,2304]{1,0:T(8,128)(2,1)S(1)}, u32[]{:S(2)}, u32[]{:S(2)}) %collective-permute-start.8) | collective-permute-done | bytes 442400 | tf_op jit(solution)/shard_map/ppermute | solution.py:114
  91.5 8.1 %collective-permute-done.10 = bf16[96,2304]{1,0:T(8,128)(2,1)S(1)} collective-permute-done((bf16[96,2304]{1,0:T(8,128)(2,1)}, bf16[96,2304]{1,0:T(8,128)(2,1)S(1)}, u32[]{:S(2)}, u32[]{:S(2)}) %collective-permute-start.10) | collective-permute-done | bytes 442400 | tf_op jit(solution)/shard_map/ppermute | solution.py:114
  101.7 4.1 %collective-permute-start.13 = (bf16[24,2304]{1,0:T(8,128)(2,1)S(1)}, bf16[24,2304]{1,0:T(8,128)(2,1)S(1)}, u32[]{:S(2)}, u32[]{:S(2)}) collective-permute-start(bf16[24,2304]{1,0:T(8,128)(2,1)S(1)} %get-tuple-element.27), channel_id=1, source_target_pairs={{0,6},{2,0},{4,2},{6,4},{1,7},{3,1},{5,3},{7,5},{8,14},{10,8},{12,... | collective-permute-start | bytes 331784 | tf_op jit(solution)/shard_map/ppermute | solution.py:114
  105.8 3.0 %collective-permute-start.12 = (bf16[24,2304]{1,0:T(8,128)(2,1)S(1)}, bf16[24,2304]{1,0:T(8,128)(2,1)S(1)}, u32[]{:S(2)}, u32[]{:S(2)}) collective-permute-start(bf16[24,2304]{1,0:T(8,128)(2,1)S(1)} %get-tuple-element.28), channel_id=1, source_target_pairs={{0,4},{2,6},{4,0},{6,2},{1,5},{3,7},{5,1},{7,3},{8,12},{10,14},{12... | collective-permute-start | bytes 331784 | tf_op jit(solution)/shard_map/ppermute | solution.py:114
  108.8 4.5 %collective-permute-done.11 = bf16[24,2304]{1,0:T(8,128)(2,1)S(1)} collective-permute-done((bf16[24,2304]{1,0:T(8,128)(2,1)S(1)}, bf16[24,2304]{1,0:T(8,128)(2,1)S(1)}, u32[]{:S(2)}, u32[]{:S(2)}) %collective-permute-start.11) | collective-permute-done | bytes 110624 | tf_op jit(solution)/shard_map/ppermute | solution.py:114
  113.4 3.3 %collective-permute-done.12 = bf16[24,2304]{1,0:T(8,128)(2,1)S(1)} collective-permute-done((bf16[24,2304]{1,0:T(8,128)(2,1)S(1)}, bf16[24,2304]{1,0:T(8,128)(2,1)S(1)}, u32[]{:S(2)}, u32[]{:S(2)}) %collective-permute-start.12) | collective-permute-done | bytes 110624 | tf_op jit(solution)/shard_map/ppermute | solution.py:114
  117.1 2.6 %collective-permute-start.15 = (bf16[24,2304]{1,0:T(8,128)(2,1)S(1)}, bf16[24,2304]{1,0:T(8,128)(2,1)S(1)}, u32[]{:S(2)}, u32[]{:S(2)}) collective-permute-start(bf16[24,2304]{1,0:T(8,128)(2,1)S(1)} %get-tuple-element.14), channel_id=1, source_target_pairs={{0,4},{2,6},{4,0},{6,2},{1,5},{3,7},{5,1},{7,3},{8,12},{10,14},{12... | collective-permute-start | bytes 331784 | tf_op jit(solution)/shard_map/ppermute | solution.py:102
  119.7 4.0 %collective-permute-start.16 = (bf16[24,2304]{1,0:T(8,128)(2,1)S(1)}, bf16[24,2304]{1,0:T(8,128)(2,1)S(1)}, u32[]{:S(2)}, u32[]{:S(2)}) collective-permute-start(bf16[24,2304]{1,0:T(8,128)(2,1)S(1)} %get-tuple-element.14), channel_id=1, source_target_pairs={{0,6},{2,0},{4,2},{6,4},{1,7},{3,1},{5,3},{7,5},{8,14},{10,8},{12,... | collective-permute-start | bytes 331784 | tf_op jit(solution)/shard_map/ppermute | solution.py:102
  123.8 4.8 %collective-permute-done.14 = bf16[24,2304]{1,0:T(8,128)(2,1)S(1)} collective-permute-done((bf16[24,2304]{1,0:T(8,128)(2,1)S(1)}, bf16[24,2304]{1,0:T(8,128)(2,1)S(1)}, u32[]{:S(2)}, u32[]{:S(2)}) %collective-permute-start.14) | collective-permute-done | bytes 110624 | tf_op jit(solution)/shard_map/ppermute | solution.py:102
  128.7 3.7 %collective-permute-done.16 = bf16[24,2304]{1,0:T(8,128)(2,1)S(1)} collective-permute-done((bf16[24,2304]{1,0:T(8,128)(2,1)S(1)}, bf16[24,2304]{1,0:T(8,128)(2,1)S(1)}, u32[]{:S(2)}, u32[]{:S(2)}) %collective-permute-start.16) | collective-permute-done | bytes 110624 | tf_op jit(solution)/shard_map/ppermute | solution.py:102
  133.3 2.4 %collective-permute-start.19 = (bf16[96,2304]{1,0:T(8,128)(2,1)S(1)}, bf16[96,2304]{1,0:T(8,128)(2,1)S(1)}, u32[]{:S(2)}, u32[]{:S(2)}) collective-permute-start(bf16[96,2304]{1,0:T(8,128)(2,1)S(1)} %constant_dynamic-update-slice_fusion.6), channel_id=1, source_target_pairs={{0,24},{8,0},{16,8},{24,16},{1,25},{9,1},{17,9},{25,17},{2,26},{10... | collective-permute-start | bytes 1327112 | tf_op jit(solution)/shard_map/ppermute | solution.py:102
  136.0 19.1 %collective-permute-done.17 = bf16[96,2304]{1,0:T(8,128)(2,1)S(1)} collective-permute-done((bf16[96,2304]{1,0:T(8,128)(2,1)S(1)}, bf16[96,2304]{1,0:T(8,128)(2,1)S(1)}, u32[]{:S(2)}, u32[]{:S(2)}) %collective-permute-start.17) | collective-permute-done | bytes 442400 | tf_op jit(solution)/shard_map/ppermute | solution.py:102
  156.3 3.1 %collective-permute-done.20 = bf16[384,2304]{1,0:T(8,128)(2,1)} collective-permute-done((bf16[384,2304]{1,0:T(8,128)(2,1)S(1)}, bf16[384,2304]{1,0:T(8,128)(2,1)}, u32[]{:S(2)}, u32[]{:S(2)}) %collective-permute-start.20) | collective-permute-done | bytes 1769504 | tf_op jit(solution)/shard_map/ppermute | solution.py:102
  161.1 2.5 %fusion.25 = f32[2,768,128]{2,1,0:T(8,128)S(1)} fusion(bf16[768,2304]{1,0:T(8,128)(2,1)S(1)} %constant_dynamic-update-slice_fusion, bf16[4,2,2304,128]{3,2,1,0:T(8,128)(2,1)} %param.26), kind=kOutput, calls=%fused_computation.32 | convolution fusion | flops 905969664 | bytes 5505024 | tf_op jit(solution)/shard_map/td,kdf->ktf/dot_general | solution.py:48
  169.7 2.3 %fusion.56 = f32[768,2304]{1,0:T(8,128)S(1)} fusion(bf16[4,128,2304]{2,1,0:T(8,128)(2,1)} %param.27, f32[2,768,128]{2,1,0:T(8,128)S(1)} %fusion.22), kind=kOutput, calls=%fused_computation.64 | convolution fusion | flops 453574656 | bytes 8454144 | tf_op jit(solution)/shard_map/dot_general | solution.py:50
  173.2 4.0 %fusion.54 = f32[768,2304]{1,0:T(8,128)} fusion(bf16[4,128,2304]{2,1,0:T(8,128)(2,1)S(1)} %copy-done.5, f32[2,768,128]{2,1,0:T(8,128)S(1)} %fusion.25), kind=kOutput, calls=%fused_computation.62 | convolution fusion | flops 453574656 | bytes 8454144 | tf_op jit(solution)/shard_map/dot_general | solution.py:50
  177.1 5.0 %add_convert_fusion = bf16[768,2304]{1,0:T(8,128)(2,1)S(1)} fusion(f32[768,2304]{1,0:T(8,128)S(1)} %fusion.52, f32[768,2304]{1,0:T(8,128)} %fusion.54, f32[768,2304]{1,0:T(8,128)S(1)} %fusion.56, f32[768]{0:T(1024)S(1)} %mul.275, f32[768]{0:T(1024)S(1)} %mul.270, f32[768]{0:T(1024)S(1)} %mul.265, f32[768]{0:T(1024)S(1)} %mul.260, ...), kind=kOutput, calls=%fused_computation.5 | convolution fusion | flops 467730432 | bytes 26161152 | tf_op jit(solution)/shard_map/dot_general | solution.py:50
  182.5 3.6 %collective-permute-done.21 = bf16[384,2304]{1,0:T(8,128)(2,1)S(1)} collective-permute-done((bf16[384,2304]{1,0:T(8,128)(2,1)S(1)}, bf16[384,2304]{1,0:T(8,128)(2,1)S(1)}, u32[]{:S(2)}, u32[]{:S(2)}) %collective-permute-start.21) | collective-permute-done | bytes 1769504 | tf_op jit(solution)/shard_map/ppermute | solution.py:114
  187.5 2.4 %collective-permute-start.24 = (bf16[96,2304]{1,0:T(8,128)(2,1)S(1)}, bf16[96,2304]{1,0:T(8,128)(2,1)S(1)}, u32[]{:S(2)}, u32[]{:S(2)}) collective-permute-start(bf16[96,2304]{1,0:T(8,128)(2,1)S(1)} %get-tuple-element.18), channel_id=1, source_target_pairs={{0,24},{8,0},{16,8},{24,16},{1,25},{9,1},{17,9},{25,17},{2,26},{10... | collective-permute-start | bytes 1327112 | tf_op jit(solution)/shard_map/ppermute | solution.py:114
  191.3 8.9 %collective-permute-done.22 = bf16[96,2304]{1,0:T(8,128)(2,1)S(1)} collective-permute-done((bf16[96,2304]{1,0:T(8,128)(2,1)S(1)}, bf16[96,2304]{1,0:T(8,128)(2,1)S(1)}, u32[]{:S(2)}, u32[]{:S(2)}) %collective-permute-start.22) | collective-permute-done | bytes 442400 | tf_op jit(solution)/shard_map/ppermute | solution.py:114
  200.1 8.8 %collective-permute-done.24 = bf16[96,2304]{1,0:T(8,128)(2,1)S(1)} collective-permute-done((bf16[96,2304]{1,0:T(8,128)(2,1)S(1)}, bf16[96,2304]{1,0:T(8,128)(2,1)S(1)}, u32[]{:S(2)}, u32[]{:S(2)}) %collective-permute-start.24) | collective-permute-done | bytes 442400 | tf_op jit(solution)/shard_map/ppermute | solution.py:114
  211.0 4.1 %collective-permute-start.27 = (bf16[24,2304]{1,0:T(8,128)(2,1)S(1)}, bf16[24,2304]{1,0:T(8,128)(2,1)S(1)}, u32[]{:S(2)}, u32[]{:S(2)}) collective-permute-start(bf16[24,2304]{1,0:T(8,128)(2,1)S(1)} %get-tuple-element.24), channel_id=1, source_target_pairs={{0,6},{2,0},{4,2},{6,4},{1,7},{3,1},{5,3},{7,5},{8,14},{10,8},{12,... | collective-permute-start | bytes 331784 | tf_op jit(solution)/shard_map/ppermute | solution.py:114
  218.0 3.9 %collective-permute-done.27 = bf16[24,2304]{1,0:T(8,128)(2,1)S(1)} collective-permute-done((bf16[24,2304]{1,0:T(8,128)(2,1)S(1)}, bf16[24,2304]{1,0:T(8,128)(2,1)S(1)}, u32[]{:S(2)}, u32[]{:S(2)}) %collective-permute-start.27) | collective-permute-done | bytes 110624 | tf_op jit(solution)/shard_map/ppermute | solution.py:114
  221.9 3.2 %collective-permute-done.26 = bf16[24,2304]{1,0:T(8,128)(2,1)S(1)} collective-permute-done((bf16[24,2304]{1,0:T(8,128)(2,1)S(1)}, bf16[24,2304]{1,0:T(8,128)(2,1)S(1)}, u32[]{:S(2)}, u32[]{:S(2)}) %collective-permute-start.26) | collective-permute-done | bytes 110624 | tf_op jit(solution)/shard_map/ppermute | solution.py:114
  (172 shorter events, 61.5 us)
Async XLA Ops:
  0.0 61.9 %copy-start = (bf16[8,1,2048,64]{2,3,1,0:T(8,128)(2,1)S(1)}, bf16[8,1,2048,64]{2,3,1,0:T(8,128)(2,1)}, u32[]{:S(2)}) copy-start(bf16[8,1,2048,64]{2,3,1,0:T(8,128)(2,1)} %param.20) | copy-start | bytes 6291460
  0.0 45.1 %copy-start.16 = (s32[8]{0:T(128)S(1)}, s32[8]{0:T(128)}, u32[]{:S(2)}) copy-start(s32[8]{0:T(128)} %param.22) | copy-start | bytes 100
  0.0 45.5 %copy-start.14 = (bf16[2304]{0:T(1024)(128)(2,1)S(1)}, bf16[2304]{0:T(1024)(128)(2,1)}, u32[]{:S(2)}) copy-start(bf16[2304]{0:T(1024)(128)(2,1)} %param.15) | copy-start | bytes 13828
  0.0 11.6 %collective-permute-start = (bf16[24,2304]{1,0:T(8,128)(2,1)}, bf16[24,2304]{1,0:T(8,128)(2,1)S(1)}, u32[]{:S(2)}, u32[]{:S(2)}) collective-permute-start(bf16[24,2304]{1,0:T(8,128)(2,1)} %param.14), channel_id=1, source_target_pairs={{0,2},{2,4},{4,6},{6,0},{1,3},{3,5},{5,7},{7,1},{8,10},{10,12},{12... | collective-permute-start | bytes 331784 | tf_op jit(solution)/shard_map/ppermute | solution.py:102
  3.4 16.4 %collective-permute-start.2 = (bf16[24,2304]{1,0:T(8,128)(2,1)}, bf16[24,2304]{1,0:T(8,128)(2,1)S(1)}, u32[]{:S(2)}, u32[]{:S(2)}) collective-permute-start(bf16[24,2304]{1,0:T(8,128)(2,1)} %param.14), channel_id=1, source_target_pairs={{0,6},{2,0},{4,2},{6,4},{1,7},{3,1},{5,3},{7,5},{8,14},{10,8},{12,... | collective-permute-start | bytes 331784 | tf_op jit(solution)/shard_map/ppermute | solution.py:102
  5.6 14.2 %collective-permute-start.1 = (bf16[24,2304]{1,0:T(8,128)(2,1)}, bf16[24,2304]{1,0:T(8,128)(2,1)S(1)}, u32[]{:S(2)}, u32[]{:S(2)}) collective-permute-start(bf16[24,2304]{1,0:T(8,128)(2,1)} %param.14), channel_id=1, source_target_pairs={{0,4},{2,6},{4,0},{6,2},{1,5},{3,7},{5,1},{7,3},{8,12},{10,14},{12... | collective-permute-start | bytes 331784 | tf_op jit(solution)/shard_map/ppermute | solution.py:102
  19.8 13.3 %collective-permute-start.3 = (bf16[96,2304]{1,0:T(8,128)(2,1)S(1)}, bf16[96,2304]{1,0:T(8,128)(2,1)S(1)}, u32[]{:S(2)}, u32[]{:S(2)}) collective-permute-start(bf16[96,2304]{1,0:T(8,128)(2,1)S(1)} %constant_dynamic-update-slice_fusion.16), channel_id=1, source_target_pairs={{0,8},{8,16},{16,24},{24,0},{1,9},{9,17},{17,25},{25,1},{2,10},{10... | collective-permute-start | bytes 1327112 | tf_op jit(solution)/shard_map/ppermute | solution.py:102
  21.4 22.3 %collective-permute-start.5 = (bf16[96,2304]{1,0:T(8,128)(2,1)S(1)}, bf16[96,2304]{1,0:T(8,128)(2,1)S(1)}, u32[]{:S(2)}, u32[]{:S(2)}) collective-permute-start(bf16[96,2304]{1,0:T(8,128)(2,1)S(1)} %constant_dynamic-update-slice_fusion.16), channel_id=1, source_target_pairs={{0,24},{8,0},{16,8},{24,16},{1,25},{9,1},{17,9},{25,17},{2,26},{10... | collective-permute-start | bytes 1327112 | tf_op jit(solution)/shard_map/ppermute | solution.py:102
  23.1 19.8 %collective-permute-start.4 = (bf16[96,2304]{1,0:T(8,128)(2,1)S(1)}, bf16[96,2304]{1,0:T(8,128)(2,1)S(1)}, u32[]{:S(2)}, u32[]{:S(2)}) collective-permute-start(bf16[96,2304]{1,0:T(8,128)(2,1)S(1)} %constant_dynamic-update-slice_fusion.16), channel_id=1, source_target_pairs={{0,16},{8,24},{16,0},{24,8},{1,17},{9,25},{17,1},{25,9},{2,18},{10... | collective-permute-start | bytes 1327112 | tf_op jit(solution)/shard_map/ppermute | solution.py:102
  44.5 4.5 %collective-permute-start.6 = (bf16[384,2304]{1,0:T(8,128)(2,1)}, bf16[384,2304]{1,0:T(8,128)(2,1)}, u32[]{:S(2)}, u32[]{:S(2)}) collective-permute-start(bf16[384,2304]{1,0:T(8,128)(2,1)} %constant_dynamic-update-slice_fusion.12), channel_id=1, source_target_pairs={{0,1},{1,0},{2,3},{3,2},{4,5},{5,4},{6,7},{7,6},{8,9},{9,8},{10,11... | collective-permute-start | bytes 5308424 | tf_op jit(solution)/shard_map/ppermute | solution.py:102
  69.6 3.9 %collective-permute-start.7 = (bf16[384,2304]{1,0:T(8,128)(2,1)S(1)}, bf16[384,2304]{1,0:T(8,128)(2,1)}, u32[]{:S(2)}, u32[]{:S(2)}) collective-permute-start(bf16[384,2304]{1,0:T(8,128)(2,1)S(1)} %dynamic-slice_bitcast_fusion.1), channel_id=1, source_target_pairs={{0,1},{1,0},{2,3},{3,2},{4,5},{5,4},{6,7},{7,6},{8,9},{9,8},{10,11... | collective-permute-start | bytes 5308424 | tf_op jit(solution)/shard_map/ppermute | solution.py:114
  75.9 40.8 %copy-start.6 = (bf16[24,2304]{1,0:T(8,128)(2,1)S(1)}, bf16[24,2304]{1,0:T(8,128)(2,1)}, u32[]{:S(2)}) copy-start(bf16[24,2304]{1,0:T(8,128)(2,1)} %param.14) | copy-start | bytes 331780
  76.9 14.6 %collective-permute-start.8 = (bf16[96,2304]{1,0:T(8,128)(2,1)}, bf16[96,2304]{1,0:T(8,128)(2,1)S(1)}, u32[]{:S(2)}, u32[]{:S(2)}) collective-permute-start(bf16[96,2304]{1,0:T(8,128)(2,1)} %get-tuple-element.20), channel_id=1, source_target_pairs={{0,8},{8,16},{16,24},{24,0},{1,9},{9,17},{17,25},{25,1},{2,10},{10... | collective-permute-start | bytes 1327112 | tf_op jit(solution)/shard_map/ppermute | solution.py:114
  78.2 21.4 %collective-permute-start.10 = (bf16[96,2304]{1,0:T(8,128)(2,1)}, bf16[96,2304]{1,0:T(8,128)(2,1)S(1)}, u32[]{:S(2)}, u32[]{:S(2)}) collective-permute-start(bf16[96,2304]{1,0:T(8,128)(2,1)} %get-tuple-element.21), channel_id=1, source_target_pairs={{0,24},{8,0},{16,8},{24,16},{1,25},{9,1},{17,9},{25,17},{2,26},{10... | collective-permute-start | bytes 1327112 | tf_op jit(solution)/shard_map/ppermute | solution.py:114
  80.3 20.0 %collective-permute-start.9 = (bf16[96,2304]{1,0:T(8,128)(2,1)S(1)}, bf16[96,2304]{1,0:T(8,128)(2,1)}, u32[]{:S(2)}, u32[]{:S(2)}) collective-permute-start(bf16[96,2304]{1,0:T(8,128)(2,1)S(1)} %get-tuple-element.22), channel_id=1, source_target_pairs={{0,16},{8,24},{16,0},{24,8},{1,17},{9,25},{17,1},{25,9},{2,18},{10... | collective-permute-start | bytes 1327112 | tf_op jit(solution)/shard_map/ppermute | solution.py:114
  101.6 11.7 %collective-permute-start.11 = (bf16[24,2304]{1,0:T(8,128)(2,1)S(1)}, bf16[24,2304]{1,0:T(8,128)(2,1)S(1)}, u32[]{:S(2)}, u32[]{:S(2)}) collective-permute-start(bf16[24,2304]{1,0:T(8,128)(2,1)S(1)} %get-tuple-element.26), channel_id=1, source_target_pairs={{0,2},{2,4},{4,6},{6,0},{1,3},{3,5},{5,7},{7,1},{8,10},{10,12},{12... | collective-permute-start | bytes 331784 | tf_op jit(solution)/shard_map/ppermute | solution.py:114
  101.7 11.7 %collective-permute-start.13 = (bf16[24,2304]{1,0:T(8,128)(2,1)S(1)}, bf16[24,2304]{1,0:T(8,128)(2,1)S(1)}, u32[]{:S(2)}, u32[]{:S(2)}) collective-permute-start(bf16[24,2304]{1,0:T(8,128)(2,1)S(1)} %get-tuple-element.27), channel_id=1, source_target_pairs={{0,6},{2,0},{4,2},{6,4},{1,7},{3,1},{5,3},{7,5},{8,14},{10,8},{12,... | collective-permute-start | bytes 331784 | tf_op jit(solution)/shard_map/ppermute | solution.py:114
  105.8 10.9 %collective-permute-start.12 = (bf16[24,2304]{1,0:T(8,128)(2,1)S(1)}, bf16[24,2304]{1,0:T(8,128)(2,1)S(1)}, u32[]{:S(2)}, u32[]{:S(2)}) collective-permute-start(bf16[24,2304]{1,0:T(8,128)(2,1)S(1)} %get-tuple-element.28), channel_id=1, source_target_pairs={{0,4},{2,6},{4,0},{6,2},{1,5},{3,7},{5,1},{7,3},{8,12},{10,14},{12... | collective-permute-start | bytes 331784 | tf_op jit(solution)/shard_map/ppermute | solution.py:114
  117.1 11.6 %collective-permute-start.14 = (bf16[24,2304]{1,0:T(8,128)(2,1)S(1)}, bf16[24,2304]{1,0:T(8,128)(2,1)S(1)}, u32[]{:S(2)}, u32[]{:S(2)}) collective-permute-start(bf16[24,2304]{1,0:T(8,128)(2,1)S(1)} %get-tuple-element.14), channel_id=1, source_target_pairs={{0,2},{2,4},{4,6},{6,0},{1,3},{3,5},{5,7},{7,1},{8,10},{10,12},{12... | collective-permute-start | bytes 331784 | tf_op jit(solution)/shard_map/ppermute | solution.py:102
  117.1 11.5 %collective-permute-start.15 = (bf16[24,2304]{1,0:T(8,128)(2,1)S(1)}, bf16[24,2304]{1,0:T(8,128)(2,1)S(1)}, u32[]{:S(2)}, u32[]{:S(2)}) collective-permute-start(bf16[24,2304]{1,0:T(8,128)(2,1)S(1)} %get-tuple-element.14), channel_id=1, source_target_pairs={{0,4},{2,6},{4,0},{6,2},{1,5},{3,7},{5,1},{7,3},{8,12},{10,14},{12... | collective-permute-start | bytes 331784 | tf_op jit(solution)/shard_map/ppermute | solution.py:102
  119.7 12.6 %collective-permute-start.16 = (bf16[24,2304]{1,0:T(8,128)(2,1)S(1)}, bf16[24,2304]{1,0:T(8,128)(2,1)S(1)}, u32[]{:S(2)}, u32[]{:S(2)}) collective-permute-start(bf16[24,2304]{1,0:T(8,128)(2,1)S(1)} %get-tuple-element.14), channel_id=1, source_target_pairs={{0,6},{2,0},{4,2},{6,4},{1,7},{3,1},{5,3},{7,5},{8,14},{10,8},{12,... | collective-permute-start | bytes 331784 | tf_op jit(solution)/shard_map/ppermute | solution.py:102
  132.3 22.8 %collective-permute-start.17 = (bf16[96,2304]{1,0:T(8,128)(2,1)S(1)}, bf16[96,2304]{1,0:T(8,128)(2,1)S(1)}, u32[]{:S(2)}, u32[]{:S(2)}) collective-permute-start(bf16[96,2304]{1,0:T(8,128)(2,1)S(1)} %constant_dynamic-update-slice_fusion.6), channel_id=1, source_target_pairs={{0,8},{8,16},{16,24},{24,0},{1,9},{9,17},{17,25},{25,1},{2,10},{10... | collective-permute-start | bytes 1327112 | tf_op jit(solution)/shard_map/ppermute | solution.py:102
  133.3 21.9 %collective-permute-start.19 = (bf16[96,2304]{1,0:T(8,128)(2,1)S(1)}, bf16[96,2304]{1,0:T(8,128)(2,1)S(1)}, u32[]{:S(2)}, u32[]{:S(2)}) collective-permute-start(bf16[96,2304]{1,0:T(8,128)(2,1)S(1)} %constant_dynamic-update-slice_fusion.6), channel_id=1, source_target_pairs={{0,24},{8,0},{16,8},{24,16},{1,25},{9,1},{17,9},{25,17},{2,26},{10... | collective-permute-start | bytes 1327112 | tf_op jit(solution)/shard_map/ppermute | solution.py:102
  135.7 19.5 %collective-permute-start.18 = (bf16[96,2304]{1,0:T(8,128)(2,1)S(1)}, bf16[96,2304]{1,0:T(8,128)(2,1)S(1)}, u32[]{:S(2)}, u32[]{:S(2)}) collective-permute-start(bf16[96,2304]{1,0:T(8,128)(2,1)S(1)} %constant_dynamic-update-slice_fusion.6), channel_id=1, source_target_pairs={{0,16},{8,24},{16,0},{24,8},{1,17},{9,25},{17,1},{25,9},{2,18},{10... | collective-permute-start | bytes 1327112 | tf_op jit(solution)/shard_map/ppermute | solution.py:102
  155.3 4.1 %collective-permute-start.20 = (bf16[384,2304]{1,0:T(8,128)(2,1)S(1)}, bf16[384,2304]{1,0:T(8,128)(2,1)}, u32[]{:S(2)}, u32[]{:S(2)}) collective-permute-start(bf16[384,2304]{1,0:T(8,128)(2,1)S(1)} %constant_dynamic-update-slice_fusion.2), channel_id=1, source_target_pairs={{0,1},{1,0},{2,3},{3,2},{4,5},{5,4},{6,7},{7,6},{8,9},{9,8},{10,11... | collective-permute-start | bytes 5308424 | tf_op jit(solution)/shard_map/ppermute | solution.py:102
  182.2 3.8 %collective-permute-start.21 = (bf16[384,2304]{1,0:T(8,128)(2,1)S(1)}, bf16[384,2304]{1,0:T(8,128)(2,1)S(1)}, u32[]{:S(2)}, u32[]{:S(2)}) collective-permute-start(bf16[384,2304]{1,0:T(8,128)(2,1)S(1)} %dynamic-slice_bitcast_fusion), channel_id=1, source_target_pairs={{0,1},{1,0},{2,3},{3,2},{4,5},{5,4},{6,7},{7,6},{8,9},{9,8},{10,11... | collective-permute-start | bytes 5308424 | tf_op jit(solution)/shard_map/ppermute | solution.py:114
  186.6 13.5 %collective-permute-start.22 = (bf16[96,2304]{1,0:T(8,128)(2,1)S(1)}, bf16[96,2304]{1,0:T(8,128)(2,1)S(1)}, u32[]{:S(2)}, u32[]{:S(2)}) collective-permute-start(bf16[96,2304]{1,0:T(8,128)(2,1)S(1)} %get-tuple-element.17), channel_id=1, source_target_pairs={{0,8},{8,16},{16,24},{24,0},{1,9},{9,17},{17,25},{25,1},{2,10},{10... | collective-permute-start | bytes 1327112 | tf_op jit(solution)/shard_map/ppermute | solution.py:114
  187.5 21.4 %collective-permute-start.24 = (bf16[96,2304]{1,0:T(8,128)(2,1)S(1)}, bf16[96,2304]{1,0:T(8,128)(2,1)S(1)}, u32[]{:S(2)}, u32[]{:S(2)}) collective-permute-start(bf16[96,2304]{1,0:T(8,128)(2,1)S(1)} %get-tuple-element.18), channel_id=1, source_target_pairs={{0,24},{8,0},{16,8},{24,16},{1,25},{9,1},{17,9},{25,17},{2,26},{10... | collective-permute-start | bytes 1327112 | tf_op jit(solution)/shard_map/ppermute | solution.py:114
  190.0 20.7 %collective-permute-start.23 = (bf16[96,2304]{1,0:T(8,128)(2,1)S(1)}, bf16[96,2304]{1,0:T(8,128)(2,1)S(1)}, u32[]{:S(2)}, u32[]{:S(2)}) collective-permute-start(bf16[96,2304]{1,0:T(8,128)(2,1)S(1)} %get-tuple-element.19), channel_id=1, source_target_pairs={{0,16},{8,24},{16,0},{24,8},{1,17},{9,25},{17,1},{25,9},{2,18},{10... | collective-permute-start | bytes 1327112 | tf_op jit(solution)/shard_map/ppermute | solution.py:114
  210.9 7.1 %collective-permute-start.25 = (bf16[24,2304]{1,0:T(8,128)(2,1)S(1)}, bf16[24,2304]{1,0:T(8,128)(2,1)S(1)}, u32[]{:S(2)}, u32[]{:S(2)}) collective-permute-start(bf16[24,2304]{1,0:T(8,128)(2,1)S(1)} %get-tuple-element.23), channel_id=1, source_target_pairs={{0,2},{2,4},{4,6},{6,0},{1,3},{3,5},{5,7},{7,1},{8,10},{10,12},{12... | collective-permute-start | bytes 331784 | tf_op jit(solution)/shard_map/ppermute | solution.py:114
  211.0 10.9 %collective-permute-start.27 = (bf16[24,2304]{1,0:T(8,128)(2,1)S(1)}, bf16[24,2304]{1,0:T(8,128)(2,1)S(1)}, u32[]{:S(2)}, u32[]{:S(2)}) collective-permute-start(bf16[24,2304]{1,0:T(8,128)(2,1)S(1)} %get-tuple-element.24), channel_id=1, source_target_pairs={{0,6},{2,0},{4,2},{6,4},{1,7},{3,1},{5,3},{7,5},{8,14},{10,8},{12,... | collective-permute-start | bytes 331784 | tf_op jit(solution)/shard_map/ppermute | solution.py:114
  215.2 10.0 %collective-permute-start.26 = (bf16[24,2304]{1,0:T(8,128)(2,1)S(1)}, bf16[24,2304]{1,0:T(8,128)(2,1)S(1)}, u32[]{:S(2)}, u32[]{:S(2)}) collective-permute-start(bf16[24,2304]{1,0:T(8,128)(2,1)S(1)} %get-tuple-element.25), channel_id=1, source_target_pairs={{0,4},{2,6},{4,0},{6,2},{1,5},{3,7},{5,1},{7,3},{8,12},{10,14},{12... | collective-permute-start | bytes 331784 | tf_op jit(solution)/shard_map/ppermute | solution.py:114
  (16 other events, 143.8 us)

commit v2 on v1

--- a/solution.py
+++ b/solution.py
@@ -1,6 +1,8 @@
 import jax
 import jax.numpy as jnp
 from jax import lax
+from jax.experimental import pallas as pl
+from jax.experimental.pallas import tpu as pltpu
 from jax.sharding import Mesh
 from jax.sharding import PartitionSpec as P
 
@@ -116,10 +118,106 @@
     return total
 
 
+def gather_kernel(own_ref, out_ref, send_sem, recv_sem, local_sem):
+    nx, nz = SIZE["x"], SIZE["zh"]
+    dp = lax.axis_index("dp")
+    x = lax.axis_index("x")
+    z = lax.axis_index("zh")
+    c = lax.axis_index("core")
+    mesh_id = pl.DeviceIdType.MESH
+    z_peers = [(dp, x, (z + s) % nz, c) for s in range(1, nz)]
+    z_from = [(z + nz - s) % nz for s in range(1, nz)]
+    x_peers = [(dp, (x + s) % nx, z, c) for s in range(1, nx)]
+    x_from = [(x + nx - s) % nx for s in range(1, nx)]
+    sibling = (dp, x, z, 1 - c)
+    barrier = pltpu.get_barrier_semaphore()
+    for peer in z_peers + x_peers + [sibling]:
+        pl.semaphore_signal(barrier, 1, device_id=peer, device_id_type=mesh_id)
+    pl.semaphore_wait(barrier, len(z_peers) + len(x_peers) + 1)
+    local = pltpu.make_async_copy(own_ref, out_ref.at[c, x, z], local_sem.at[0])
+    local.start()
+    sent = []
+    for k, peer in enumerate(z_peers):
+        copy = pltpu.make_async_remote_copy(
+            src_ref=own_ref,
+            dst_ref=out_ref.at[c, x, z],
+            send_sem=send_sem.at[k],
+            recv_sem=recv_sem.at[k],
+            device_id=peer,
+            device_id_type=mesh_id,
+        )
+        copy.start()
+        sent.append(copy)
+    local.wait()
+    for k, src in enumerate(z_from):
+        pltpu.make_async_remote_copy(
+            src_ref=own_ref,
+            dst_ref=out_ref.at[c, x, src],
+            send_sem=send_sem.at[k],
+            recv_sem=recv_sem.at[k],
+            device_id=z_peers[k],
+            device_id_type=mesh_id,
+        ).wait_recv()
+    base = len(z_peers)
+    for k, peer in enumerate(x_peers):
+        copy = pltpu.make_async_remote_copy(
+            src_ref=out_ref.at[c, x],
+            dst_ref=out_ref.at[c, x],
+            send_sem=send_sem.at[base + k],
+            recv_sem=recv_sem.at[base + k],
+            device_id=peer,
+            device_id_type=mesh_id,
+        )
+        copy.start()
+        sent.append(copy)
+    for k, src in enumerate(x_from):
+        pltpu.make_async_remote_copy(
+            src_ref=out_ref.at[c, x],
+            dst_ref=out_ref.at[c, src],
+            send_sem=send_sem.at[base + k],
+            recv_sem=recv_sem.at[base + k],
+            device_id=x_peers[k],
+            device_id_type=mesh_id,
+        ).wait_recv()
+    last = base + len(x_peers)
+    copy = pltpu.make_async_remote_copy(
+        src_ref=out_ref.at[c],
+        dst_ref=out_ref.at[c],
+        send_sem=send_sem.at[last],
+        recv_sem=recv_sem.at[last],
+        device_id=sibling,
+        device_id_type=mesh_id,
+    )
+    copy.start()
+    sent.append(copy)
+    pltpu.make_async_remote_copy(
+        src_ref=out_ref.at[c],
+        dst_ref=out_ref.at[1 - c],
+        send_sem=send_sem.at[last],
+        recv_sem=recv_sem.at[last],
+        device_id=sibling,
+        device_id_type=mesh_id,
+    ).wait_recv()
+    for copy in sent:
+        copy.wait_send()
+
+
 def gather_rows(rows):
-    rows = gather_stage(rows, "zh")
-    rows = gather_stage(rows, "x")
-    return gather_stage(rows, "core")
+    nx, nz, nc = SIZE["x"], SIZE["zh"], SIZE["core"]
+    links = (nz - 1) + (nx - 1) + 1
+    out = pl.pallas_call(
+        gather_kernel,
+        out_shape=jax.ShapeDtypeStruct((nc, nx, nz) + rows.shape, rows.dtype),
+        in_specs=[pl.BlockSpec(memory_space=pltpu.VMEM)],
+        out_specs=pl.BlockSpec(memory_space=pltpu.VMEM),
+        scratch_shapes=[
+            pltpu.SemaphoreType.DMA((links,)),
+            pltpu.SemaphoreType.DMA((links,)),
+            pltpu.SemaphoreType.DMA((1,)),
+        ],
+        compiler_params=pltpu.CompilerParams(collective_id=0, has_side_effects=True),
+    )(rows)
+    return out.reshape((nc * nx * nz * rows.shape[0],) + rows.shape[1:])
 
 
 def scatter_rows(rows):

time: 231 us -> 228 us (0.987)
  the two profiles are of different devices: /device:TPU:40 before, /device:TPU:22 now
where the time goes in v2:
time: 228 us; the launch traced here: 227 us
  Pallas kernels  75.2 us (33%)
  waiting for transfers between devices  66.3 us (29%)
  matrix products  32.4 us (14%)
  starting transfers between devices  29.1 us (13%)
  other arithmetic  14.7 us (6%)
  local copies, waits for them, and re-layouts  8.27 us (4%)
    pallas_call x2, Pallas kernels, gather_rows(): pl.pallas_call(gather_kernel, out_shape=jax.ShapeDtypeStruct((nc, nx, nz)...  75.2 us
    ppermute x14, waiting for transfers between devices, scatter_stage(): got = lax.ppermute(send.astype(jnp.bfloat16), axis, shifts(axis, step))  66.3 us
    ppermute x14, starting transfers between devices, scatter_stage(): got = lax.ppermute(send.astype(jnp.bfloat16), axis, shifts(axis, step))  29.1 us
    dot_general x4, matrix products, expert_apply(): return jnp.dot(inner, down_part, preferred_element_type=jnp.float32)  12.4 us
    dot_general x4, matrix products, expert_apply(): jnp.einsum('td,kdf->ktf', rows_in, gate_up, preferred_element_type=jnp.fl...  9.03 us
    dot_general x3, matrix products, project(): jnp.dot(normed, weight, preferred_element_type=jnp.float32)  5.72 us
  transfers between devices with their start and end apart: 14, of which 12 were waited for; matrix products, arithmetic and copies ran while one was open for 0% of the time, Pallas kernels for 0%

profile of v2, /device:TPU:22, one launch (start us, length us, event | category | flops | bytes accessed | tf_op | source)
XLA Modules:
  0.0 226.7 jit_solution(3338882272355538074)
XLA Ops:
  2.7 42.8 %shard_map.136 = bf16[2,4,4,24,2304]{4,3,2,1,0:T(8,128)(2,1)} custom-call(bf16[24,2304]{1,0:T(8,128)(2,1)} %own_ref.1), custom_call_target="tpu_custom_call" | custom-call | tf_op jit(solution)/shard_map/pallas_call | solution.py:208
  45.6 2.8 %multiply_reduce_fusion = f32[2,4,4,24]{3,2,1,0:T(4,128)S(1)} fusion(bf16[2,4,4,24,2304]{4,3,2,1,0:T(8,128)(2,1)} %shard_map.136), kind=kLoop, calls=%fused_computation.4 | loop fusion | flops 5307648 | bytes 3542016 | tf_op jit(solution)/shard_map/reduce_sum | solution.py:23
  48.4 2.9 %fusion.1 = bf16[768,2304]{1,0:T(8,128)(2,1)S(1)} fusion(f32[2304]{0:T(1024)S(1)} %convert_element_type.205, f32[768]{0:T(1024)S(1)} %rsqrt.20, bf16[2,4,4,24,2304]{4,3,2,1,0:T(8,128)(2,1)} %shard_map.136), kind=kLoop, calls=%fused_computation.2 | loop fusion | flops 7077888 | bytes 7090176 | tf_op jit(solution)/shard_map/convert_element_type | solution.py:24
  51.4 1.7 copy-done.2
  54.5 3.3 %convolution_bitcast_fusion.4 = f32[768,1,64]{0,2,1:T(8,128)S(1)} fusion(bf16[768,2304]{1,0:T(8,128)(2,1)} %copy-done.2, bf16[2304,64]{0,1:T(8,128)(2,1)S(1)} %copy-done.9), kind=kOutput, calls=%fused_computation.39 | convolution fusion | flops 226492416 | bytes 4030464 | tf_op jit(solution)/shard_map/dot_general | solution.py:272
  63.6 1.5 fusion.7
  66.7 1.7 copy-done.5
  69.0 3.4 %collective-permute-done = bf16[384,2304]{1,0:T(8,128)(2,1)} collective-permute-done((bf16[384,2304]{1,0:T(8,128)(2,1)S(1)}, bf16[384,2304]{1,0:T(8,128)(2,1)}, u32[]{:S(2)}, u32[]{:S(2)}) %collective-permute-start) | collective-permute-done | bytes 1769504 | tf_op jit(solution)/shard_map/ppermute | solution.py:116
  72.5 2.4 %fusion.6 = bf16[384,2304]{1,0:T(8,128)(2,1)S(1)} fusion(bf16[384,2304]{1,0:T(8,128)(2,1)} %collective-permute-done, bf16[2,384,2304]{2,1,0:T(8,128)(2,1)} %bitcast.173, s32[]{:T(128)S(6)} %select_n.124), kind=kLoop, calls=%fused_computation.14 | loop fusion | flops 3538944 | bytes 5308420 | tf_op jit(solution)/shard_map/convert_element_type | solution.py:225
  76.0 1.5 collective-permute-start.1
  79.5 9.7 %collective-permute-done.1 = bf16[96,2304]{1,0:T(8,128)(2,1)S(1)} collective-permute-done((bf16[96,2304]{1,0:T(8,128)(2,1)}, bf16[96,2304]{1,0:T(8,128)(2,1)S(1)}, u32[]{:S(2)}, u32[]{:S(2)}) %collective-permute-start.1) | collective-permute-done | bytes 442400 | tf_op jit(solution)/shard_map/ppermute | solution.py:116
  89.3 11.3 %collective-permute-done.3 = bf16[96,2304]{1,0:T(8,128)(2,1)S(1)} collective-permute-done((bf16[96,2304]{1,0:T(8,128)(2,1)}, bf16[96,2304]{1,0:T(8,128)(2,1)S(1)}, u32[]{:S(2)}, u32[]{:S(2)}) %collective-permute-start.3) | collective-permute-done | bytes 442400 | tf_op jit(solution)/shard_map/ppermute | solution.py:116
  100.9 4.8 %collective-permute-start.4 = (bf16[24,2304]{1,0:T(8,128)(2,1)S(1)}, bf16[24,2304]{1,0:T(8,128)(2,1)S(1)}, u32[]{:S(2)}, u32[]{:S(2)}) collective-permute-start(bf16[24,2304]{1,0:T(8,128)(2,1)S(1)} %get-tuple-element.24), channel_id=1, source_target_pairs={{0,2},{2,4},{4,6},{6,0},{1,3},{3,5},{5,7},{7,1},{8,10},{10,12},{12... | collective-permute-start | bytes 331784 | tf_op jit(solution)/shard_map/ppermute | solution.py:116
  105.6 2.2 collective-permute-start.6
  107.8 2.6 %collective-permute-start.5 = (bf16[24,2304]{1,0:T(8,128)(2,1)S(1)}, bf16[24,2304]{1,0:T(8,128)(2,1)S(1)}, u32[]{:S(2)}, u32[]{:S(2)}) collective-permute-start(bf16[24,2304]{1,0:T(8,128)(2,1)S(1)} %get-tuple-element.26), channel_id=1, source_target_pairs={{0,4},{2,6},{4,0},{6,2},{1,5},{3,7},{5,1},{7,3},{8,12},{10,14},{12... | collective-permute-start | bytes 331784 | tf_op jit(solution)/shard_map/ppermute | solution.py:116
  110.4 1.5 collective-permute-done.4
  113.0 5.4 %collective-permute-done.5 = bf16[24,2304]{1,0:T(8,128)(2,1)S(1)} collective-permute-done((bf16[24,2304]{1,0:T(8,128)(2,1)S(1)}, bf16[24,2304]{1,0:T(8,128)(2,1)S(1)}, u32[]{:S(2)}, u32[]{:S(2)}) %collective-permute-start.5) | collective-permute-done | bytes 110624 | tf_op jit(solution)/shard_map/ppermute | solution.py:116
  119.3 32.4 %shard_map.137 = bf16[2,4,4,24,2304]{4,3,2,1,0:T(8,128)(2,1)} custom-call(bf16[24,2304]{1,0:T(8,128)(2,1)} %fusion.49.own_ref), custom_call_target="tpu_custom_call" | custom-call | tf_op jit(solution)/shard_map/pallas_call | solution.py:208
  151.8 4.4 %convolution_bitcast_fusion = f32[2,768,128]{2,1,0:T(8,128)} fusion(bf16[768,2304,1]{1,0,2:T(8,128)(2,1)} %bitcast.167, bf16[4,2,2304,128]{3,2,1,0:T(8,128)(2,1)} %param.26), kind=kOutput, calls=%fused_computation.22 | convolution fusion | flops 905969664 | bytes 5505024 | tf_op jit(solution)/shard_map/td,kdf->ktf/dot_general | solution.py:50
  156.2 2.4 %convolution_bitcast_fusion.1 = f32[2,768,128]{2,1,0:T(8,128)S(1)} fusion(bf16[768,2304,1]{1,0,2:T(8,128)(2,1)S(1)} %bitcast.168, bf16[4,2,2304,128]{3,2,1,0:T(8,128)(2,1)} %param.26), kind=kOutput, calls=%fused_computation.23 | convolution fusion | flops 905969664 | bytes 5505024 | tf_op jit(solution)/shard_map/td,kdf->ktf/dot_general | solution.py:50
  162.8 2.3 %fusion.35 = f32[768,2304]{1,0:T(8,128)S(1)} fusion(bf16[4,128,2304]{2,1,0:T(8,128)(2,1)} %param.27, f32[2,768,128]{2,1,0:T(8,128)S(1)} %convolution_bitcast_fusion.3), kind=kOutput, calls=%fused_computation.55 | convolution fusion | flops 453574656 | bytes 8454144 | tf_op jit(solution)/shard_map/dot_general | solution.py:52
  166.2 4.0 %fusion.31 = f32[768,2304]{1,0:T(8,128)} fusion(bf16[4,128,2304]{2,1,0:T(8,128)(2,1)S(1)} %copy-done.6, f32[2,768,128]{2,1,0:T(8,128)S(1)} %convolution_bitcast_fusion.1), kind=kOutput, calls=%fused_computation.51 | convolution fusion | flops 453574656 | bytes 8454144 | tf_op jit(solution)/shard_map/dot_general | solution.py:52
  170.2 5.0 %add_convert_fusion = bf16[768,2304]{1,0:T(8,128)(2,1)S(1)} fusion(f32[768,2304]{1,0:T(8,128)} %fusion.31, f32[768,2304]{1,0:T(8,128)S(1)} %fusion.33, f32[768,2304]{1,0:T(8,128)S(1)} %fusion.35, f32[768]{0:T(1024)S(1)} %mul.226, f32[768]{0:T(1024)S(1)} %mul.221, f32[768]{0:T(1024)S(1)} %mul.216, f32[768]{0:T(1024)S(1)} %mul.211, ...), kind=kOutput, calls=%fused_computation.3 | convolution fusion | flops 467730432 | bytes 26161152 | tf_op jit(solution)/shard_map/dot_general | solution.py:52
  175.9 3.3 %collective-permute-done.7 = bf16[384,2304]{1,0:T(8,128)(2,1)S(1)} collective-permute-done((bf16[384,2304]{1,0:T(8,128)(2,1)S(1)}, bf16[384,2304]{1,0:T(8,128)(2,1)S(1)}, u32[]{:S(2)}, u32[]{:S(2)}) %collective-permute-start.7) | collective-permute-done | bytes 1769504 | tf_op jit(solution)/shard_map/ppermute | solution.py:116
  179.8 3.6 %collective-permute-start.8 = (bf16[96,2304]{1,0:T(8,128)(2,1)S(1)}, bf16[96,2304]{1,0:T(8,128)(2,1)S(1)}, u32[]{:S(2)}, u32[]{:S(2)}) collective-permute-start(bf16[96,2304]{1,0:T(8,128)(2,1)S(1)} %get-tuple-element.15), channel_id=1, source_target_pairs={{0,8},{8,16},{16,24},{24,0},{1,9},{9,17},{17,25},{25,1},{2,10},{10... | collective-permute-start | bytes 1327112 | tf_op jit(solution)/shard_map/ppermute | solution.py:116
  183.4 1.6 collective-permute-start.9
  185.0 17.9 %collective-permute-done.8 = bf16[96,2304]{1,0:T(8,128)(2,1)S(1)} collective-permute-done((bf16[96,2304]{1,0:T(8,128)(2,1)S(1)}, bf16[96,2304]{1,0:T(8,128)(2,1)S(1)}, u32[]{:S(2)}, u32[]{:S(2)}) %collective-permute-start.8) | collective-permute-done | bytes 442400 | tf_op jit(solution)/shard_map/ppermute | solution.py:116
  202.9 3.4 %collective-permute-done.10 = bf16[96,2304]{1,0:T(8,128)(2,1)S(1)} collective-permute-done((bf16[96,2304]{1,0:T(8,128)(2,1)S(1)}, bf16[96,2304]{1,0:T(8,128)(2,1)S(1)}, u32[]{:S(2)}, u32[]{:S(2)}) %collective-permute-start.10) | collective-permute-done | bytes 442400 | tf_op jit(solution)/shard_map/ppermute | solution.py:116
  206.6 6.5 %collective-permute-start.11 = (bf16[24,2304]{1,0:T(8,128)(2,1)S(1)}, bf16[24,2304]{1,0:T(8,128)(2,1)S(1)}, u32[]{:S(2)}, u32[]{:S(2)}) collective-permute-start(bf16[24,2304]{1,0:T(8,128)(2,1)S(1)} %get-tuple-element.21), channel_id=1, source_target_pairs={{0,2},{2,4},{4,6},{6,0},{1,3},{3,5},{5,7},{7,1},{8,10},{10,12},{12... | collective-permute-start | bytes 331784 | tf_op jit(solution)/shard_map/ppermute | solution.py:116
  214.5 2.3 %collective-permute-start.12 = (bf16[24,2304]{1,0:T(8,128)(2,1)S(1)}, bf16[24,2304]{1,0:T(8,128)(2,1)S(1)}, u32[]{:S(2)}, u32[]{:S(2)}) collective-permute-start(bf16[24,2304]{1,0:T(8,128)(2,1)S(1)} %get-tuple-element.23), channel_id=1, source_target_pairs={{0,4},{2,6},{4,0},{6,2},{1,5},{3,7},{5,1},{7,3},{8,12},{10,14},{12... | collective-permute-start | bytes 331784 | tf_op jit(solution)/shard_map/ppermute | solution.py:116
  217.1 2.3 %collective-permute-done.13 = bf16[24,2304]{1,0:T(8,128)(2,1)S(1)} collective-permute-done((bf16[24,2304]{1,0:T(8,128)(2,1)S(1)}, bf16[24,2304]{1,0:T(8,128)(2,1)S(1)}, u32[]{:S(2)}, u32[]{:S(2)}) %collective-permute-start.13) | collective-permute-done | bytes 110624 | tf_op jit(solution)/shard_map/ppermute | solution.py:116
  219.4 6.5 %collective-permute-done.12 = bf16[24,2304]{1,0:T(8,128)(2,1)S(1)} collective-permute-done((bf16[24,2304]{1,0:T(8,128)(2,1)S(1)}, bf16[24,2304]{1,0:T(8,128)(2,1)S(1)}, u32[]{:S(2)}, u32[]{:S(2)}) %collective-permute-start.12) | collective-permute-done | bytes 110624 | tf_op jit(solution)/shard_map/ppermute | solution.py:116
  (120 shorter events, 26.3 us)
Async XLA Ops:
  0.0 60.9 %copy-start = (bf16[8,1,2048,64]{2,3,1,0:T(8,128)(2,1)S(1)}, bf16[8,1,2048,64]{2,3,1,0:T(8,128)(2,1)}, u32[]{:S(2)}) copy-start(bf16[8,1,2048,64]{2,3,1,0:T(8,128)(2,1)} %param.20) | copy-start | bytes 6291460
  48.4 4.7 %copy-start.8 = (bf16[2304,64]{0,1:T(8,128)(2,1)S(1)}, bf16[2304,64]{0,1:T(8,128)(2,1)}, u32[]{:S(2)}) copy-start(bf16[2304,64]{0,1:T(8,128)(2,1)} %param.18) | copy-start | bytes 884740
  51.4 1.7 copy-start.2
  53.1 1.4 copy-start.9
  54.3 3.6 %copy-start.10 = (bf16[2304,64]{0,1:T(8,128)(2,1)S(1)}, bf16[2304,64]{0,1:T(8,128)(2,1)}, u32[]{:S(2)}) copy-start(bf16[2304,64]{0,1:T(8,128)(2,1)} %param.16) | copy-start | bytes 884740
  54.5 3.4 %copy-start.3 = (bf16[768,2304]{1,0:T(8,128)(2,1)S(1)}, bf16[768,2304]{1,0:T(8,128)(2,1)}, u32[]{:S(2)}) copy-start(bf16[768,2304]{1,0:T(8,128)(2,1)} %copy-done.2) | copy-start | bytes 10616836
  62.0 1.6 copy-start.16
  63.6 2.0 copy-start.11
  66.7 1.7 copy-start.5
  68.5 3.9 %collective-permute-start = (bf16[384,2304]{1,0:T(8,128)(2,1)S(1)}, bf16[384,2304]{1,0:T(8,128)(2,1)}, u32[]{:S(2)}, u32[]{:S(2)}) collective-permute-start(bf16[384,2304]{1,0:T(8,128)(2,1)S(1)} %dynamic-slice_bitcast_fusion.1), channel_id=1, source_target_pairs={{0,1},{1,0},{2,3},{3,2},{4,5},{5,4},{6,7},{7,6},{8,9},{9,8},{10,11... | collective-permute-start | bytes 5308424 | tf_op jit(solution)/shard_map/ppermute | solution.py:116
  69.0 10.3 %copy-start.15 = (bf16[2304]{0:T(1024)(128)(2,1)S(1)}, bf16[2304]{0:T(1024)(128)(2,1)}, u32[]{:S(2)}) copy-start(bf16[2304]{0:T(1024)(128)(2,1)} %param.23) | copy-start | bytes 13828
  69.0 10.3 %copy-start.14 = (s32[768,2]{0,1:T(2,128)S(1)}, s32[768,2]{0,1:T(2,128)}, u32[]{:S(2)}) copy-start(s32[768,2]{0,1:T(2,128)} %param.25) | copy-start | bytes 18436
  74.9 43.5 %copy-start.7 = (bf16[24,2304]{1,0:T(8,128)(2,1)S(1)}, bf16[24,2304]{1,0:T(8,128)(2,1)}, u32[]{:S(2)}) copy-start(bf16[24,2304]{1,0:T(8,128)(2,1)} %own_ref.1) | copy-start | bytes 331780
  76.0 13.3 %collective-permute-start.1 = (bf16[96,2304]{1,0:T(8,128)(2,1)}, bf16[96,2304]{1,0:T(8,128)(2,1)S(1)}, u32[]{:S(2)}, u32[]{:S(2)}) collective-permute-start(bf16[96,2304]{1,0:T(8,128)(2,1)} %get-tuple-element.18), channel_id=1, source_target_pairs={{0,8},{8,16},{16,24},{24,0},{1,9},{9,17},{17,25},{25,1},{2,10},{10... | collective-permute-start | bytes 1327112 | tf_op jit(solution)/shard_map/ppermute | solution.py:116
  77.5 23.1 %collective-permute-start.3 = (bf16[96,2304]{1,0:T(8,128)(2,1)}, bf16[96,2304]{1,0:T(8,128)(2,1)S(1)}, u32[]{:S(2)}, u32[]{:S(2)}) collective-permute-start(bf16[96,2304]{1,0:T(8,128)(2,1)} %get-tuple-element.19), channel_id=1, source_target_pairs={{0,24},{8,0},{16,8},{24,16},{1,25},{9,1},{17,9},{25,17},{2,26},{10... | collective-permute-start | bytes 1327112 | tf_op jit(solution)/shard_map/ppermute | solution.py:116
  78.0 22.6 %collective-permute-start.2 = (bf16[96,2304]{1,0:T(8,128)(2,1)}, bf16[96,2304]{1,0:T(8,128)(2,1)S(1)}, u32[]{:S(2)}, u32[]{:S(2)}) collective-permute-start(bf16[96,2304]{1,0:T(8,128)(2,1)} %get-tuple-element.20), channel_id=1, source_target_pairs={{0,16},{8,24},{16,0},{24,8},{1,17},{9,25},{17,1},{25,9},{2,18},{10... | collective-permute-start | bytes 1327112 | tf_op jit(solution)/shard_map/ppermute | solution.py:116
  100.9 11.1 %collective-permute-start.4 = (bf16[24,2304]{1,0:T(8,128)(2,1)S(1)}, bf16[24,2304]{1,0:T(8,128)(2,1)S(1)}, u32[]{:S(2)}, u32[]{:S(2)}) collective-permute-start(bf16[24,2304]{1,0:T(8,128)(2,1)S(1)} %get-tuple-element.24), channel_id=1, source_target_pairs={{0,2},{2,4},{4,6},{6,0},{1,3},{3,5},{5,7},{7,1},{8,10},{10,12},{12... | collective-permute-start | bytes 331784 | tf_op jit(solution)/shard_map/ppermute | solution.py:116
  105.6 7.4 %collective-permute-start.6 = (bf16[24,2304]{1,0:T(8,128)(2,1)S(1)}, bf16[24,2304]{1,0:T(8,128)(2,1)S(1)}, u32[]{:S(2)}, u32[]{:S(2)}) collective-permute-start(bf16[24,2304]{1,0:T(8,128)(2,1)S(1)} %get-tuple-element.25), channel_id=1, source_target_pairs={{0,6},{2,0},{4,2},{6,4},{1,7},{3,1},{5,3},{7,5},{8,14},{10,8},{12,... | collective-permute-start | bytes 331784 | tf_op jit(solution)/shard_map/ppermute | solution.py:116
  107.8 10.5 %collective-permute-start.5 = (bf16[24,2304]{1,0:T(8,128)(2,1)S(1)}, bf16[24,2304]{1,0:T(8,128)(2,1)S(1)}, u32[]{:S(2)}, u32[]{:S(2)}) collective-permute-start(bf16[24,2304]{1,0:T(8,128)(2,1)S(1)} %get-tuple-element.26), channel_id=1, source_target_pairs={{0,4},{2,6},{4,0},{6,2},{1,5},{3,7},{5,1},{7,3},{8,12},{10,14},{12... | collective-permute-start | bytes 331784 | tf_op jit(solution)/shard_map/ppermute | solution.py:116
  151.8 4.5 %copy-start.4 = (bf16[2,4,4,24,2304]{4,3,2,1,0:T(8,128)(2,1)S(1)}, bf16[2,4,4,24,2304]{4,3,2,1,0:T(8,128)(2,1)}, u32[]{:S(2)}) copy-start(bf16[2,4,4,24,2304]{4,3,2,1,0:T(8,128)(2,1)} %shard_map.137) | copy-start | bytes 10616836
  151.8 6.9 %slice-start = ((s8[4718592]{0:T(1024)(128)(4,1)}), s8[4194304]{0:T(1024)(128)(4,1)S(1)}, s32[]{:S(2)}) async-start(s8[4718592]{0:T(1024)(128)(4,1)} %bitcast.198), calls=%async_computation | async-start | bytes 8388608
  156.2 2.4 %slice-start.1 = ((s8[4718592]{0:T(1024)(128)(4,1)}), s8[524288]{0:T(1024)(128)(4,1)S(1)}, s32[]{:S(2)}) async-start(s8[4718592]{0:T(1024)(128)(4,1)} %bitcast.198), calls=%async_computation.1 | async-start | bytes 1048576
  162.8 2.3 %copy-start.6 = (bf16[4,128,2304]{2,1,0:T(8,128)(2,1)S(1)}, bf16[4,128,2304]{2,1,0:T(8,128)(2,1)}, u32[]{:S(2)}) copy-start(bf16[4,128,2304]{2,1,0:T(8,128)(2,1)} %param.27) | copy-start | bytes 7077892
  166.2 4.0 %copy-start.12 = (f32[2,768,128]{2,1,0:T(8,128)S(1)}, f32[2,768,128]{2,1,0:T(8,128)}, u32[]{:S(2)}) copy-start(f32[2,768,128]{2,1,0:T(8,128)} %convolution_bitcast_fusion) | copy-start | bytes 2359300
  175.4 3.8 %collective-permute-start.7 = (bf16[384,2304]{1,0:T(8,128)(2,1)S(1)}, bf16[384,2304]{1,0:T(8,128)(2,1)S(1)}, u32[]{:S(2)}, u32[]{:S(2)}) collective-permute-start(bf16[384,2304]{1,0:T(8,128)(2,1)S(1)} %dynamic-slice_bitcast_fusion), channel_id=1, source_target_pairs={{0,1},{1,0},{2,3},{3,2},{4,5},{5,4},{6,7},{7,6},{8,9},{9,8},{10,11... | collective-permute-start | bytes 5308424 | tf_op jit(solution)/shard_map/ppermute | solution.py:116
  179.2 47.5 %copy-start.1 = (bf16[8,1,2048,64]{2,3,1,0:T(8,128)(2,1)S(1)}, bf16[8,1,2048,64]{2,3,1,0:T(8,128)(2,1)}, u32[]{:S(2)}) copy-start(bf16[8,1,2048,64]{2,3,1,0:T(8,128)(2,1)} %param.20) | copy-start | bytes 6291460
  179.8 23.1 %collective-permute-start.8 = (bf16[96,2304]{1,0:T(8,128)(2,1)S(1)}, bf16[96,2304]{1,0:T(8,128)(2,1)S(1)}, u32[]{:S(2)}, u32[]{:S(2)}) collective-permute-start(bf16[96,2304]{1,0:T(8,128)(2,1)S(1)} %get-tuple-element.15), channel_id=1, source_target_pairs={{0,8},{8,16},{16,24},{24,0},{1,9},{9,17},{17,25},{25,1},{2,10},{10... | collective-permute-start | bytes 1327112 | tf_op jit(solution)/shard_map/ppermute | solution.py:116
  183.4 22.9 %collective-permute-start.10 = (bf16[96,2304]{1,0:T(8,128)(2,1)S(1)}, bf16[96,2304]{1,0:T(8,128)(2,1)S(1)}, u32[]{:S(2)}, u32[]{:S(2)}) collective-permute-start(bf16[96,2304]{1,0:T(8,128)(2,1)S(1)} %get-tuple-element.16), channel_id=1, source_target_pairs={{0,24},{8,0},{16,8},{24,16},{1,25},{9,1},{17,9},{25,17},{2,26},{10... | collective-permute-start | bytes 1327112 | tf_op jit(solution)/shard_map/ppermute | solution.py:116
  183.4 22.9 %collective-permute-start.9 = (bf16[96,2304]{1,0:T(8,128)(2,1)S(1)}, bf16[96,2304]{1,0:T(8,128)(2,1)S(1)}, u32[]{:S(2)}, u32[]{:S(2)}) collective-permute-start(bf16[96,2304]{1,0:T(8,128)(2,1)S(1)} %get-tuple-element.17), channel_id=1, source_target_pairs={{0,16},{8,24},{16,0},{24,8},{1,17},{9,25},{17,1},{25,9},{2,18},{10... | collective-permute-start | bytes 1327112 | tf_op jit(solution)/shard_map/ppermute | solution.py:116
  206.6 10.6 %collective-permute-start.11 = (bf16[24,2304]{1,0:T(8,128)(2,1)S(1)}, bf16[24,2304]{1,0:T(8,128)(2,1)S(1)}, u32[]{:S(2)}, u32[]{:S(2)}) collective-permute-start(bf16[24,2304]{1,0:T(8,128)(2,1)S(1)} %get-tuple-element.21), channel_id=1, source_target_pairs={{0,2},{2,4},{4,6},{6,0},{1,3},{3,5},{5,7},{7,1},{8,10},{10,12},{12... | collective-permute-start | bytes 331784 | tf_op jit(solution)/shard_map/ppermute | solution.py:116
  213.1 6.4 %collective-permute-start.13 = (bf16[24,2304]{1,0:T(8,128)(2,1)S(1)}, bf16[24,2304]{1,0:T(8,128)(2,1)S(1)}, u32[]{:S(2)}, u32[]{:S(2)}) collective-permute-start(bf16[24,2304]{1,0:T(8,128)(2,1)S(1)} %get-tuple-element.22), channel_id=1, source_target_pairs={{0,6},{2,0},{4,2},{6,4},{1,7},{3,1},{5,3},{7,5},{8,14},{10,8},{12,... | collective-permute-start | bytes 331784 | tf_op jit(solution)/shard_map/ppermute | solution.py:116
  214.5 11.5 %collective-permute-start.12 = (bf16[24,2304]{1,0:T(8,128)(2,1)S(1)}, bf16[24,2304]{1,0:T(8,128)(2,1)S(1)}, u32[]{:S(2)}, u32[]{:S(2)}) collective-permute-start(bf16[24,2304]{1,0:T(8,128)(2,1)S(1)} %get-tuple-element.23), channel_id=1, source_target_pairs={{0,4},{2,6},{4,0},{6,2},{1,5},{3,7},{5,1},{7,3},{8,12},{10,14},{12... | collective-permute-start | bytes 331784 | tf_op jit(solution)/shard_map/ppermute | solution.py:116
  (1 other events, 1.1 us)

commit v3 on v2

--- a/solution.py
+++ b/solution.py
@@ -220,10 +220,85 @@
     return out.reshape((nc * nx * nz * rows.shape[0],) + rows.shape[1:])
 
 
+def scatter_kernel(part_ref, out_ref, got_c, sum_c, got_x, sum_x, got_z, send_sem, recv_sem):
+    nx, nz = SIZE["x"], SIZE["zh"]
+    dp = lax.axis_index("dp")
+    x = lax.axis_index("x")
+    z = lax.axis_index("zh")
+    c = lax.axis_index("core")
+    mesh_id = pl.DeviceIdType.MESH
+    sibling = (dp, x, z, 1 - c)
+    x_peers = [(dp, (x + s) % nx, z, c) for s in range(1, nx)]
+    z_peers = [(dp, x, (z + s) % nz, c) for s in range(1, nz)]
+    barrier = pltpu.get_barrier_semaphore()
+    for peer in [sibling] + x_peers + z_peers:
+        pl.semaphore_signal(barrier, 1, device_id=peer, device_id_type=mesh_id)
+    pl.semaphore_wait(barrier, 1 + len(x_peers) + len(z_peers))
+    sent = []
+
+    def exchange(src, dst, k, peer):
+        copy = pltpu.make_async_remote_copy(
+            src_ref=src,
+            dst_ref=dst,
+            send_sem=send_sem.at[k],
+            recv_sem=recv_sem.at[k],
+            device_id=peer,
+            device_id_type=mesh_id,
+        )
+        copy.start()
+        sent.append(copy)
+        return copy
+
+    exchange(part_ref.at[1 - c], got_c, 0, sibling).wait_recv()
+    sum_c[...] = (
+        part_ref[c].astype(jnp.float32) + got_c[...].astype(jnp.float32)
+    ).astype(sum_c.dtype)
+    copies = [
+        exchange(sum_c.at[(x + s) % nx], got_x.at[s - 1], s, x_peers[s - 1]) for s in range(1, nx)
+    ]
+    for copy in copies:
+        copy.wait_recv()
+    total = sum_c[x].astype(jnp.float32)
+    for k in range(nx - 1):
+        total = total + got_x[k].astype(jnp.float32)
+    sum_x[...] = total.astype(sum_x.dtype)
+    base = nx - 1
+    copies = [
+        exchange(sum_x.at[(z + s) % nz], got_z.at[s - 1], base + s, z_peers[s - 1])
+        for s in range(1, nz)
+    ]
+    for copy in copies:
+        copy.wait_recv()
+    total = sum_x[z].astype(jnp.float32)
+    for k in range(nz - 1):
+        total = total + got_z[k].astype(jnp.float32)
+    out_ref[...] = total
+    for copy in sent:
+        copy.wait_send()
+
+
 def scatter_rows(rows):
-    rows = scatter_stage(rows, "core")
-    rows = scatter_stage(rows.astype(jnp.bfloat16), "x")
-    return scatter_stage(rows.astype(jnp.bfloat16), "zh")
+    nx, nz, nc = SIZE["x"], SIZE["zh"], SIZE["core"]
+    blk = rows.shape[0] // (nx * nz * nc)
+    tail = rows.shape[1:]
+    part = rows.reshape((nc, nx, nz, blk) + tail)
+    links = 1 + (nx - 1) + (nz - 1)
+    return pl.pallas_call(
+        scatter_kernel,
+        out_shape=jax.ShapeDtypeStruct((blk,) + tail, jnp.float32),
+        in_specs=[pl.BlockSpec(memory_space=pltpu.VMEM)],
+        out_specs=pl.BlockSpec(memory_space=pltpu.VMEM),
+        scratch_shapes=[
+            pltpu.VMEM((nx, nz, blk) + tail, rows.dtype),
+            pltpu.VMEM((nx, nz, blk) + tail, rows.dtype),
+            pltpu.VMEM((nx - 1, nz, blk) + tail, rows.dtype),
+            pltpu.VMEM((nz, blk) + tail, rows.dtype),
+            pltpu.VMEM((nz - 1, blk) + tail, rows.dtype),
+            pltpu.SemaphoreType.DMA((links,)),
+            pltpu.SemaphoreType.DMA((links,)),
+        ],
+        compiler_params=pltpu.CompilerParams(collective_id=1, has_side_effects=True),
+    )(part)
 
 
 def to_request_order(values):

time: 228 us -> 232 us (1.018)
  Pallas kernels: 75.2 us -> 174 us
  waiting for transfers between devices: 66.3 us -> 0 us
  starting transfers between devices: 29.1 us -> 0 us
  matrix products: 32.4 us -> 35.2 us
    pallas_call x0 -> x2, Pallas kernels: none -> 91.9 us  [scatter_rows(): pl.pallas_call(scatter_kernel, out_shape=jax.ShapeDtypeStruct((blk,) + ta...]
    ppermute x14 -> x0, waiting for transfers between devices: 66.3 us -> none  [scatter_stage(): got = lax.ppermute(send.astype(jnp.bfloat16), axis, shifts(axis, step))]
    ppermute x14 -> x0, starting transfers between devices: 29.1 us -> none  [scatter_stage(): got = lax.ppermute(send.astype(jnp.bfloat16), axis, shifts(axis, step))]
    pallas_call x2, Pallas kernels: 75.2 us -> 82.3 us  [gather_rows(): pl.pallas_call(gather_kernel, out_shape=jax.ShapeDtypeStruct((nc, nx, nz)...]
    convert_element_type x4 -> x0, other arithmetic: 3.35 us -> none  [the longest x2 2.91 us: scatter_rows(): rows = scatter_stage(rows.astype(jnp.bfloat16), 'x')]
  transfers between devices with their start and end apart: 14 -> 0, of which waited for: 12 -> 0; matrix products, arithmetic and copies ran while one was open for 0% -> 0% of each run, Pallas kernels for 0% -> 0%
where the time goes in v3:
time: 232 us; the launch traced here: 230 us
  Pallas kernels  174 us (75%)
  matrix products  35.2 us (15%)
  other arithmetic  13.8 us (6%)
  local copies, waits for them, and re-layouts  6.25 us (3%)
    pallas_call x2, Pallas kernels, scatter_rows(): pl.pallas_call(scatter_kernel, out_shape=jax.ShapeDtypeStruct((blk,) + ta...  91.9 us
    pallas_call x2, Pallas kernels, gather_rows(): pl.pallas_call(gather_kernel, out_shape=jax.ShapeDtypeStruct((nc, nx, nz)...  82.3 us
    dot_general x4, matrix products, expert_apply(): return jnp.dot(inner, down_part, preferred_element_type=jnp.float32)  12.3 us
    dot_general x4, matrix products, expert_apply(): jnp.einsum('td,kdf->ktf', rows_in, gate_up, preferred_element_type=jnp.fl...  8.16 us
    dot_general x3, matrix products, project(): jnp.dot(normed, weight, preferred_element_type=jnp.float32)  5.72 us

profile of v3, /device:TPU:22, one launch (start us, length us, event | category | flops | bytes accessed | tf_op | source)
XLA Modules:
  0.0 230.0 jit_solution(10051511728630859877)
XLA Ops:
  0.0 0.9 add.141
  1.3 0.7 convert_element_type.115
  2.0 0.7 convert_element_type.126
  2.7 0.7 iota_compare_fusion
  3.4 0.8 reshape.454
  4.4 43.0 %shard_map.136 = bf16[2,4,4,24,2304]{4,3,2,1,0:T(8,128)(2,1)} custom-call(bf16[24,2304]{1,0:T(8,128)(2,1)} %own_ref.1), custom_call_target="tpu_custom_call" | custom-call | tf_op jit(solution)/shard_map/pallas_call | solution.py:208
  47.4 2.8 %multiply_reduce_fusion = f32[2,4,4,24]{3,2,1,0:T(4,128)S(1)} fusion(bf16[2,4,4,24,2304]{4,3,2,1,0:T(8,128)(2,1)} %shard_map.136), kind=kLoop, calls=%fused_computation.4 | loop fusion | flops 5307648 | bytes 3542016 | tf_op jit(solution)/shard_map/reduce_sum | solution.py:23
  50.3 2.9 %fusion.1 = bf16[768,2304]{1,0:T(8,128)(2,1)S(1)} fusion(f32[2304]{0:T(1024)S(1)} %convert_element_type.115, f32[768]{0:T(1024)S(1)} %rsqrt.20, bf16[2,4,4,24,2304]{4,3,2,1,0:T(8,128)(2,1)} %shard_map.136), kind=kLoop, calls=%fused_computation.2 | loop fusion | flops 7077888 | bytes 7090176 | tf_op jit(solution)/shard_map/convert_element_type | solution.py:24
  53.2 1.7 copy-done.1
  54.9 1.2 convolution_convert_fusion.1
  56.4 3.3 %convolution_bitcast_fusion.4 = f32[768,1,64]{0,2,1:T(8,128)S(1)} fusion(bf16[768,2304]{1,0:T(8,128)(2,1)} %copy-done.1, bf16[2304,64]{0,1:T(8,128)(2,1)S(1)} %copy-done.7), kind=kOutput, calls=%fused_computation.33 | convolution fusion | flops 226492416 | bytes 4030464 | tf_op jit(solution)/shard_map/dot_general | solution.py:347
  59.7 1.2 convolution_bitcast_fusion.5
  62.7 1.1 fusion.2
  63.9 1.5 fusion.3
  65.4 1.5 fusion.5
  67.4 2.8 %convolution_convert_fusion = bf16[768,2304]{1,0:T(8,128)(2,1)} fusion(bf16[768,64]{1,0:T(8,128)(2,1)S(1)} %bitcast.125, bf16[64,2304]{1,0:T(8,128)(2,1)S(1)} %copy-done.9), kind=kOutput, calls=%fused_computation.8 | convolution fusion | flops 228261888 | bytes 3932160 | tf_op jit(solution)/shard_map/dot_general | solution.py:363
  70.2 47.2 %shard_map.137 = f32[24,2304]{1,0:T(8,128)} custom-call(bf16[2,4,4,24,2304]{4,3,2,1,0:T(8,128)(2,1)} %bitcast.121), custom_call_target="tpu_custom_call" | custom-call | tf_op jit(solution)/shard_map/pallas_call | solution.py:286
  117.4 1.1 fusion.39
  118.5 0.7 fusion.41.own_ref
  119.3 39.4 %shard_map.138 = bf16[2,4,4,24,2304]{4,3,2,1,0:T(8,128)(2,1)} custom-call(bf16[24,2304]{1,0:T(8,128)(2,1)} %fusion.41.own_ref), custom_call_target="tpu_custom_call" | custom-call | tf_op jit(solution)/shard_map/pallas_call | solution.py:208
  158.6 3.1 %select_reduce_fusion = (f32[768]{0:T(1024)S(1)}, f32[768]{0:T(1024)S(1)}) fusion(s32[768]{0:T(1024)S(1)} %get-tuple-element.11, s32[768]{0:T(1024)S(1)} %get-tuple-element.12, bf16[768,2304]{1,0:T(8,128)(2,1)} %bitcast.116, bf16[2304,4]{0,1:T(4,128)(2,1)S(1)} %copy-done.10), kind=kOutput, calls=%fused_computation.105 | convolution fusion | flops 14172672 | bytes 3569664 | tf_op jit(solution)/shard_map/dot_general | solution.py:367
  162.5 3.6 %convolution_bitcast_fusion = f32[2,768,128]{2,1,0:T(8,128)S(1)} fusion(bf16[768,2304,1]{1,0,2:T(8,128)(2,1)} %bitcast.117, bf16[4,2,2304,128]{3,2,1,0:T(8,128)(2,1)} %param.26), kind=kOutput, calls=%fused_computation.16 | convolution fusion | flops 905969664 | bytes 5505024 | tf_op jit(solution)/shard_map/td,kdf->ktf/dot_general | solution.py:50
  166.1 2.4 %convolution_bitcast_fusion.1 = f32[2,768,128]{2,1,0:T(8,128)S(1)} fusion(bf16[768,2304,1]{1,0,2:T(8,128)(2,1)S(1)} %bitcast.118, bf16[4,2,2304,128]{3,2,1,0:T(8,128)(2,1)} %param.26), kind=kOutput, calls=%fused_computation.17 | convolution fusion | flops 905969664 | bytes 5505024 | tf_op jit(solution)/shard_map/td,kdf->ktf/dot_general | solution.py:50
  168.6 1.1 convolution_bitcast_fusion.2
  169.7 1.1 convolution_bitcast_fusion.3
  170.8 0.6 copy-done.4
  171.4 1.1 fusion.27
  172.4 1.1 fusion.25
  173.5 4.0 %fusion.23 = f32[768,2304]{1,0:T(8,128)} fusion(bf16[4,128,2304]{2,1,0:T(8,128)(2,1)S(1)} %copy-done.4, f32[2,768,128]{2,1,0:T(8,128)S(1)} %convolution_bitcast_fusion.1), kind=kOutput, calls=%fused_computation.37 | convolution fusion | flops 453574656 | bytes 8454144 | tf_op jit(solution)/shard_map/dot_general | solution.py:52
  177.5 6.1 %add_convert_fusion = bf16[768,2304]{1,0:T(8,128)(2,1)} fusion(f32[768,2304]{1,0:T(8,128)} %fusion.23, f32[768,2304]{1,0:T(8,128)S(1)} %fusion.25, f32[768,2304]{1,0:T(8,128)S(1)} %fusion.27, f32[768]{0:T(1024)S(1)} %mul.226, f32[768]{0:T(1024)S(1)} %mul.221, f32[768]{0:T(1024)S(1)} %mul.216, f32[768]{0:T(1024)S(1)} %mul.211, ...), kind=kOutput, calls=%fused_computation.3 | convolution fusion | flops 467730432 | bytes 26165248 | tf_op jit(solution)/shard_map/dot_general | solution.py:52
  183.6 44.7 %shard_map.139 = f32[24,2304]{1,0:T(8,128)} custom-call(bf16[2,4,4,24,2304]{4,3,2,1,0:T(8,128)(2,1)} %bitcast.122), custom_call_target="tpu_custom_call" | custom-call | tf_op jit(solution)/shard_map/pallas_call | solution.py:286
  228.3 1.6 fusion.42
  (74 shorter events, 3.8 us)
Async XLA Ops:
  0.0 62.7 %copy-start = (bf16[8,1,2048,64]{2,3,1,0:T(8,128)(2,1)S(1)}, bf16[8,1,2048,64]{2,3,1,0:T(8,128)(2,1)}, u32[]{:S(2)}) copy-start(bf16[8,1,2048,64]{2,3,1,0:T(8,128)(2,1)} %param.20) | copy-start | bytes 6291460
  50.2 4.7 %copy-start.6 = (bf16[2304,64]{0,1:T(8,128)(2,1)S(1)}, bf16[2304,64]{0,1:T(8,128)(2,1)}, u32[]{:S(2)}) copy-start(bf16[2304,64]{0,1:T(8,128)(2,1)} %param.18) | copy-start | bytes 884740
  53.2 1.8 copy-start.1
  54.9 1.4 copy-start.7
  56.1 3.6 %copy-start.8 = (bf16[2304,64]{0,1:T(8,128)(2,1)S(1)}, bf16[2304,64]{0,1:T(8,128)(2,1)}, u32[]{:S(2)}) copy-start(bf16[2304,64]{0,1:T(8,128)(2,1)} %param.16) | copy-start | bytes 884740
  56.3 3.4 %copy-start.2 = (bf16[768,2304]{1,0:T(8,128)(2,1)S(1)}, bf16[768,2304]{1,0:T(8,128)(2,1)}, u32[]{:S(2)}) copy-start(bf16[768,2304]{1,0:T(8,128)(2,1)} %copy-done.1) | copy-start | bytes 10616836
  63.8 1.6 copy-start.11
  65.4 2.0 copy-start.9
  67.4 50.0 %copy-start.5 = (bf16[24,2304]{1,0:T(8,128)(2,1)S(1)}, bf16[24,2304]{1,0:T(8,128)(2,1)}, u32[]{:S(2)}) copy-start(bf16[24,2304]{1,0:T(8,128)(2,1)} %own_ref.1) | copy-start | bytes 331780
  70.2 88.4 %copy-start.10 = (bf16[2304,4]{0,1:T(4,128)(2,1)S(1)}, bf16[2304,4]{0,1:T(4,128)(2,1)}, u32[]{:S(2)}) copy-start(bf16[2304,4]{0,1:T(4,128)(2,1)} %param.24) | copy-start | bytes 55300
  162.5 3.6 %copy-start.3 = (bf16[2,4,4,24,2304]{4,3,2,1,0:T(8,128)(2,1)S(1)}, bf16[2,4,4,24,2304]{4,3,2,1,0:T(8,128)(2,1)}, u32[]{:S(2)}) copy-start(bf16[2,4,4,24,2304]{4,3,2,1,0:T(8,128)(2,1)} %shard_map.138) | copy-start | bytes 10616836
  162.5 6.0 %slice-start = ((s8[4718592]{0:T(1024)(128)(4,1)}), s8[4194304]{0:T(1024)(128)(4,1)S(1)}, s32[]{:S(2)}) async-start(s8[4718592]{0:T(1024)(128)(4,1)} %bitcast.137), calls=%async_computation | async-start | bytes 8388608
  166.1 2.5 %slice-start.1 = ((s8[4718592]{0:T(1024)(128)(4,1)}), s8[524288]{0:T(1024)(128)(4,1)S(1)}, s32[]{:S(2)}) async-start(s8[4718592]{0:T(1024)(128)(4,1)} %bitcast.137), calls=%async_computation.1 | async-start | bytes 1048576
  169.7 1.7 copy-start.4

commit v4 on v1

--- a/solution.py
+++ b/solution.py
@@ -1,6 +1,8 @@
 import jax
 import jax.numpy as jnp
 from jax import lax
+from jax.experimental import pallas as pl
+from jax.experimental.pallas import tpu as pltpu
 from jax.sharding import Mesh
 from jax.sharding import PartitionSpec as P
 
@@ -116,16 +118,188 @@
     return total
 
 
+def ring_peers(axis):
+    here = {name: lax.axis_index(name) for name in ("dp",) + TENSOR}
+    n = SIZE[axis]
+    me = here[axis]
+
+    def at(member):
+        return tuple(member if name == axis else here[name] for name in ("dp",) + TENSOR)
+
+    return me, n, at((me + 1) % n), at((me + n - 1) % n)
+
+
+def halves(ref):
+    half = ref.shape[-1] // 2
+    return ref.at[..., pl.ds(0, half)], ref.at[..., pl.ds(half, half)]
+
+
+def remote(src, dst, send_sem, recv_sem, peer):
+    return pltpu.make_async_remote_copy(
+        src_ref=src,
+        dst_ref=dst,
+        send_sem=send_sem,
+        recv_sem=recv_sem,
+        device_id=peer,
+        device_id_type=pl.DeviceIdType.MESH,
+    )
+
+
+def ring_gather(slot, first, axis, send_sem, recv_sem, sent):
+    me, n, right, left = ring_peers(axis)
+    opposite = (me + 2) % n
+    for k, peer in ((0, right), (1, left)):
+        copy = remote(first, slot(me), send_sem.at[k], recv_sem.at[k], peer)
+        copy.start()
+        sent.append(copy)
+    remote(first, slot((me + n - 1) % n), send_sem.at[0], recv_sem.at[0], left).wait_recv()
+    copy = remote(
+        halves(slot((me + n - 1) % n))[0], halves(slot((me + n - 1) % n))[0],
+        send_sem.at[2], recv_sem.at[2], right,
+    )
+    copy.start()
+    sent.append(copy)
+    remote(first, slot((me + 1) % n), send_sem.at[1], recv_sem.at[1], right).wait_recv()
+    copy = remote(
+        halves(slot((me + 1) % n))[1], halves(slot((me + 1) % n))[1],
+        send_sem.at[3], recv_sem.at[3], left,
+    )
+    copy.start()
+    sent.append(copy)
+    lo, hi = halves(slot(opposite))
+    remote(lo, lo, send_sem.at[2], recv_sem.at[2], left).wait_recv()
+    remote(hi, hi, send_sem.at[3], recv_sem.at[3], right).wait_recv()
+
+
+def gather_kernel(own_ref, out_ref, send_sem, recv_sem, local_sem):
+    x = lax.axis_index("x")
+    z = lax.axis_index("zh")
+    c = lax.axis_index("core")
+    _, _, z_right, z_left = ring_peers("zh")
+    _, _, x_right, x_left = ring_peers("x")
+    _, _, sibling, _ = ring_peers("core")
+    barrier = pltpu.get_barrier_semaphore()
+    for peer in (z_right, z_left, x_right, x_left, sibling):
+        pl.semaphore_signal(barrier, 1, device_id=peer, device_id_type=pl.DeviceIdType.MESH)
+    pl.semaphore_wait(barrier, 5)
+    local = pltpu.make_async_copy(own_ref, out_ref.at[c, x, z], local_sem.at[0])
+    local.start()
+    sent = []
+    ring_gather(lambda i: out_ref.at[c, x, i], own_ref, "zh", send_sem.at[0:4], recv_sem.at[0:4], sent)
+    local.wait()
+    ring_gather(lambda i: out_ref.at[c, i], out_ref.at[c, x], "x", send_sem.at[4:8], recv_sem.at[4:8], sent)
+    copy = remote(out_ref.at[c], out_ref.at[c], send_sem.at[8], recv_sem.at[8], sibling)
+    copy.start()
+    sent.append(copy)
+    remote(out_ref.at[c], out_ref.at[1 - c], send_sem.at[8], recv_sem.at[8], sibling).wait_recv()
+    for copy in sent:
+        copy.wait_send()
+
+
 def gather_rows(rows):
-    rows = gather_stage(rows, "zh")
-    rows = gather_stage(rows, "x")
-    return gather_stage(rows, "core")
+    nx, nz, nc = SIZE["x"], SIZE["zh"], SIZE["core"]
+    links = 9
+    out = pl.pallas_call(
+        gather_kernel,
+        out_shape=jax.ShapeDtypeStruct((nc, nx, nz) + rows.shape, rows.dtype),
+        in_specs=[pl.BlockSpec(memory_space=pltpu.VMEM)],
+        out_specs=pl.BlockSpec(memory_space=pltpu.VMEM),
+        scratch_shapes=[
+            pltpu.SemaphoreType.DMA((links,)),
+            pltpu.SemaphoreType.DMA((links,)),
+            pltpu.SemaphoreType.DMA((1,)),
+        ],
+        compiler_params=pltpu.CompilerParams(collective_id=0, has_side_effects=True),
+    )(rows)
+    return out.reshape((nc * nx * nz * rows.shape[0],) + rows.shape[1:])
+
+
+def ring_scatter(chunk, axis, buffers, send_sem, recv_sem, sent):
+    me, n, right, left = ring_peers(axis)
+    got_lo, got_hi, to_right, to_left, from_left, from_right = buffers
+    lo, hi = halves(chunk((me + 2) % n))
+    for k, src, dst, peer in ((0, lo, got_lo, right), (1, hi, got_hi, left)):
+        copy = remote(src, dst, send_sem.at[k], recv_sem.at[k], peer)
+        copy.start()
+        sent.append(copy)
+    half = to_right.shape[-1] // 2
+    remote(lo, got_lo, send_sem.at[0], recv_sem.at[0], left).wait_recv()
+    ahead = chunk((me + 1) % n)
+    to_right[..., :half] = (
+        ahead[..., :half].astype(jnp.float32) + got_lo[...].astype(jnp.float32)
+    ).astype(to_right.dtype)
+    to_right[..., half:] = ahead[..., half:]
+    copy = remote(to_right, from_left, send_sem.at[2], recv_sem.at[2], right)
+    copy.start()
+    sent.append(copy)
+    remote(hi, got_hi, send_sem.at[1], recv_sem.at[1], right).wait_recv()
+    behind = chunk((me + n - 1) % n)
+    to_left[..., :half] = behind[..., :half]
+    to_left[..., half:] = (
+        behind[..., half:].astype(jnp.float32) + got_hi[...].astype(jnp.float32)
+    ).astype(to_left.dtype)
+    copy = remote(to_left, from_right, send_sem.at[3], recv_sem.at[3], left)
+    copy.start()
+    sent.append(copy)
+    remote(to_right, from_left, send_sem.at[2], recv_sem.at[2], left).wait_recv()
+    remote(to_left, from_right, send_sem.at[3], recv_sem.at[3], right).wait_recv()
+    return (
+        chunk(me)[...].astype(jnp.float32)
+        + from_left[...].astype(jnp.float32)
+        + from_right[...].astype(jnp.float32)
+    )
+
+
+def scatter_kernel(part_ref, out_ref, got_c, sum_c, x_bufs, sum_x, z_bufs, send_sem, recv_sem):
+    c = lax.axis_index("core")
+    _, _, z_right, z_left = ring_peers("zh")
+    _, _, x_right, x_left = ring_peers("x")
+    _, _, sibling, _ = ring_peers("core")
+    barrier = pltpu.get_barrier_semaphore()
+    for peer in (sibling, x_right, x_left, z_right, z_left):
+        pl.semaphore_signal(barrier, 1, device_id=peer, device_id_type=pl.DeviceIdType.MESH)
+    pl.semaphore_wait(barrier, 5)
+    sent = []
+    copy = remote(part_ref.at[1 - c], got_c, send_sem.at[0], recv_sem.at[0], sibling)
+    copy.start()
+    sent.append(copy)
+    copy.wait_recv()
+    sum_c[...] = (
+        part_ref[c].astype(jnp.float32) + got_c[...].astype(jnp.float32)
+    ).astype(sum_c.dtype)
+    x_bufs = [x_bufs.at[0, 0], x_bufs.at[0, 1]] + [x_bufs.at[1, k] for k in range(4)]
+    x_bufs = [x_bufs[0].at[..., pl.ds(0, x_bufs[0].shape[-1] // 2)], x_bufs[1].at[..., pl.ds(0, x_bufs[1].shape[-1] // 2)]] + x_bufs[2:]
+    total = ring_scatter(lambda i: sum_c.at[i], "x", x_bufs, send_sem.at[1:5], recv_sem.at[1:5], sent)
+    sum_x[...] = total.astype(sum_x.dtype)
+    z_bufs = [z_bufs.at[0, 0], z_bufs.at[0, 1]] + [z_bufs.at[1, k] for k in range(4)]
+    z_bufs = [z_bufs[0].at[..., pl.ds(0, z_bufs[0].shape[-1] // 2)], z_bufs[1].at[..., pl.ds(0, z_bufs[1].shape[-1] // 2)]] + z_bufs[2:]
+    out_ref[...] = ring_scatter(lambda i: sum_x.at[i], "zh", z_bufs, send_sem.at[5:9], recv_sem.at[5:9], sent)
+    for copy in sent:
+        copy.wait_send()
 
 
 def scatter_rows(rows):
-    rows = scatter_stage(rows, "core")
-    rows = scatter_stage(rows.astype(jnp.bfloat16), "x")
-    return scatter_stage(rows.astype(jnp.bfloat16), "zh")
+    nx, nz, nc = SIZE["x"], SIZE["zh"], SIZE["core"]
+    blk = rows.shape[0] // (nx * nz * nc)
+    tail = rows.shape[1:]
+    part = rows.reshape((nc, nx, nz, blk) + tail)
+    links = 9
+    return pl.pallas_call(
+        scatter_kernel,
+        out_shape=jax.ShapeDtypeStruct((blk,) + tail, jnp.float32),
+        in_specs=[pl.BlockSpec(memory_space=pltpu.VMEM)],
+        out_specs=pl.BlockSpec(memory_space=pltpu.VMEM),
+        scratch_shapes=[
+            pltpu.VMEM((nx, nz, blk) + tail, rows.dtype),
+            pltpu.VMEM((nx, nz, blk) + tail, rows.dtype),
+            pltpu.VMEM((2, 4, nz, blk) + tail, rows.dtype),
+            pltpu.VMEM((nz, blk) + tail, rows.dtype),
+            pltpu.VMEM((2, 4, blk) + tail, rows.dtype),
+            pltpu.SemaphoreType.DMA((links,)),
+            pltpu.SemaphoreType.DMA((links,)),
+        ],
+        compiler_params=pltpu.CompilerParams(collective_id=1, has_side_effects=True),
+    )(part)
 
 
 def to_request_order(values):

time: 231 us -> 214 us (0.926)
  the two profiles are of different devices: /device:TPU:40 before, /device:TPU:22 now
where the time goes in v4:
time: 214 us; the launch traced here: 211 us
  Pallas kernels  155 us (72%)
  matrix products  35.2 us (16%)
  other arithmetic  13.8 us (6%)
  local copies, waits for them, and re-layouts  6.25 us (3%)
    pallas_call x2, Pallas kernels, scatter_rows(): pl.pallas_call(scatter_kernel, out_shape=jax.ShapeDtypeStruct((blk,) + ta...  77.8 us
    pallas_call x2, Pallas kernels, gather_rows(): pl.pallas_call(gather_kernel, out_shape=jax.ShapeDtypeStruct((nc, nx, nz)...  77.2 us
    dot_general x4, matrix products, expert_apply(): return jnp.dot(inner, down_part, preferred_element_type=jnp.float32)  12.3 us
    dot_general x4, matrix products, expert_apply(): jnp.einsum('td,kdf->ktf', rows_in, gate_up, preferred_element_type=jnp.fl...  8.16 us
    dot_general x3, matrix products, project(): jnp.dot(normed, weight, preferred_element_type=jnp.float32)  5.73 us

profile of v4, /device:TPU:22, one launch (start us, length us, event | category | flops | bytes accessed | tf_op | source)
XLA Modules:
  0.0 210.8 jit_solution(16552464009275235380)
XLA Ops:
  0.0 0.9 add.141
  1.3 0.7 convert_element_type.115
  2.0 0.7 convert_element_type.126
  2.7 0.7 iota_compare_fusion
  3.4 0.8 reshape.454
  4.4 40.4 %shard_map.136 = bf16[2,4,4,24,2304]{4,3,2,1,0:T(8,128)(2,1)} custom-call(bf16[24,2304]{1,0:T(8,128)(2,1)} %own_ref.1), custom_call_target="tpu_custom_call" | custom-call | tf_op jit(solution)/shard_map/pallas_call | solution.py:202
  44.8 2.8 %multiply_reduce_fusion = f32[2,4,4,24]{3,2,1,0:T(4,128)S(1)} fusion(bf16[2,4,4,24,2304]{4,3,2,1,0:T(8,128)(2,1)} %shard_map.136), kind=kLoop, calls=%fused_computation.4 | loop fusion | flops 5307648 | bytes 3542016 | tf_op jit(solution)/shard_map/reduce_sum | solution.py:23
  47.7 2.9 %fusion.1 = bf16[768,2304]{1,0:T(8,128)(2,1)S(1)} fusion(f32[2304]{0:T(1024)S(1)} %convert_element_type.115, f32[768]{0:T(1024)S(1)} %rsqrt.20, bf16[2,4,4,24,2304]{4,3,2,1,0:T(8,128)(2,1)} %shard_map.136), kind=kLoop, calls=%fused_computation.2 | loop fusion | flops 7077888 | bytes 7090176 | tf_op jit(solution)/shard_map/convert_element_type | solution.py:24
  50.6 1.7 copy-done.1
  52.4 1.2 convolution_convert_fusion.1
  53.8 3.3 %convolution_bitcast_fusion.4 = f32[768,1,64]{0,2,1:T(8,128)S(1)} fusion(bf16[768,2304]{1,0:T(8,128)(2,1)} %copy-done.1, bf16[2304,64]{0,1:T(8,128)(2,1)S(1)} %copy-done.7), kind=kOutput, calls=%fused_computation.33 | convolution fusion | flops 226492416 | bytes 4030464 | tf_op jit(solution)/shard_map/dot_general | solution.py:348
  57.2 1.2 convolution_bitcast_fusion.5
  60.1 1.1 fusion.2
  61.4 1.5 fusion.3
  62.9 1.5 fusion.5
  64.9 2.8 %convolution_convert_fusion = bf16[768,2304]{1,0:T(8,128)(2,1)} fusion(bf16[768,64]{1,0:T(8,128)(2,1)S(1)} %bitcast.125, bf16[64,2304]{1,0:T(8,128)(2,1)S(1)} %copy-done.9), kind=kOutput, calls=%fused_computation.8 | convolution fusion | flops 228261888 | bytes 3932160 | tf_op jit(solution)/shard_map/dot_general | solution.py:364
  67.7 38.2 %shard_map.137 = f32[24,2304]{1,0:T(8,128)} custom-call(bf16[2,4,4,24,2304]{4,3,2,1,0:T(8,128)(2,1)} %bitcast.121), custom_call_target="tpu_custom_call" | custom-call | tf_op jit(solution)/shard_map/pallas_call | solution.py:287
  105.9 1.1 fusion.39
  107.0 0.7 fusion.41.own_ref
  107.8 36.8 %shard_map.138 = bf16[2,4,4,24,2304]{4,3,2,1,0:T(8,128)(2,1)} custom-call(bf16[24,2304]{1,0:T(8,128)(2,1)} %fusion.41.own_ref), custom_call_target="tpu_custom_call" | custom-call | tf_op jit(solution)/shard_map/pallas_call | solution.py:202
  144.6 3.1 %select_reduce_fusion = (f32[768]{0:T(1024)S(1)}, f32[768]{0:T(1024)S(1)}) fusion(s32[768]{0:T(1024)S(1)} %get-tuple-element.11, s32[768]{0:T(1024)S(1)} %get-tuple-element.12, bf16[768,2304]{1,0:T(8,128)(2,1)} %bitcast.116, bf16[2304,4]{0,1:T(4,128)(2,1)S(1)} %copy-done.10), kind=kOutput, calls=%fused_computation.105 | convolution fusion | flops 14172672 | bytes 3569664 | tf_op jit(solution)/shard_map/dot_general | solution.py:368
  148.5 3.6 %convolution_bitcast_fusion = f32[2,768,128]{2,1,0:T(8,128)S(1)} fusion(bf16[768,2304,1]{1,0,2:T(8,128)(2,1)} %bitcast.117, bf16[4,2,2304,128]{3,2,1,0:T(8,128)(2,1)} %param.26), kind=kOutput, calls=%fused_computation.16 | convolution fusion | flops 905969664 | bytes 5505024 | tf_op jit(solution)/shard_map/td,kdf->ktf/dot_general | solution.py:50
  152.1 2.4 %convolution_bitcast_fusion.1 = f32[2,768,128]{2,1,0:T(8,128)S(1)} fusion(bf16[768,2304,1]{1,0,2:T(8,128)(2,1)S(1)} %bitcast.118, bf16[4,2,2304,128]{3,2,1,0:T(8,128)(2,1)} %param.26), kind=kOutput, calls=%fused_computation.17 | convolution fusion | flops 905969664 | bytes 5505024 | tf_op jit(solution)/shard_map/td,kdf->ktf/dot_general | solution.py:50
  154.5 1.1 convolution_bitcast_fusion.2
  155.6 1.1 convolution_bitcast_fusion.3
  156.7 0.6 copy-done.4
  157.3 1.1 fusion.27
  158.4 1.1 fusion.25
  159.5 4.0 %fusion.23 = f32[768,2304]{1,0:T(8,128)} fusion(bf16[4,128,2304]{2,1,0:T(8,128)(2,1)S(1)} %copy-done.4, f32[2,768,128]{2,1,0:T(8,128)S(1)} %convolution_bitcast_fusion.1), kind=kOutput, calls=%fused_computation.37 | convolution fusion | flops 453574656 | bytes 8454144 | tf_op jit(solution)/shard_map/dot_general | solution.py:52
  163.5 6.1 %add_convert_fusion = bf16[768,2304]{1,0:T(8,128)(2,1)} fusion(f32[768,2304]{1,0:T(8,128)} %fusion.23, f32[768,2304]{1,0:T(8,128)S(1)} %fusion.25, f32[768,2304]{1,0:T(8,128)S(1)} %fusion.27, f32[768]{0:T(1024)S(1)} %mul.226, f32[768]{0:T(1024)S(1)} %mul.221, f32[768]{0:T(1024)S(1)} %mul.216, f32[768]{0:T(1024)S(1)} %mul.211, ...), kind=kOutput, calls=%fused_computation.3 | convolution fusion | flops 467730432 | bytes 26165248 | tf_op jit(solution)/shard_map/dot_general | solution.py:52
  169.6 39.6 %shard_map.139 = f32[24,2304]{1,0:T(8,128)} custom-call(bf16[2,4,4,24,2304]{4,3,2,1,0:T(8,128)(2,1)} %bitcast.122), custom_call_target="tpu_custom_call" | custom-call | tf_op jit(solution)/shard_map/pallas_call | solution.py:287
  209.2 1.6 fusion.42
  (74 shorter events, 3.8 us)
Async XLA Ops:
  0.0 60.1 %copy-start = (bf16[8,1,2048,64]{2,3,1,0:T(8,128)(2,1)S(1)}, bf16[8,1,2048,64]{2,3,1,0:T(8,128)(2,1)}, u32[]{:S(2)}) copy-start(bf16[8,1,2048,64]{2,3,1,0:T(8,128)(2,1)} %param.20) | copy-start | bytes 6291460
  47.7 4.7 %copy-start.6 = (bf16[2304,64]{0,1:T(8,128)(2,1)S(1)}, bf16[2304,64]{0,1:T(8,128)(2,1)}, u32[]{:S(2)}) copy-start(bf16[2304,64]{0,1:T(8,128)(2,1)} %param.18) | copy-start | bytes 884740
  50.6 1.8 copy-start.1
  52.4 1.4 copy-start.7
  53.6 3.6 %copy-start.8 = (bf16[2304,64]{0,1:T(8,128)(2,1)S(1)}, bf16[2304,64]{0,1:T(8,128)(2,1)}, u32[]{:S(2)}) copy-start(bf16[2304,64]{0,1:T(8,128)(2,1)} %param.16) | copy-start | bytes 884740
  53.8 3.4 %copy-start.2 = (bf16[768,2304]{1,0:T(8,128)(2,1)S(1)}, bf16[768,2304]{1,0:T(8,128)(2,1)}, u32[]{:S(2)}) copy-start(bf16[768,2304]{1,0:T(8,128)(2,1)} %copy-done.1) | copy-start | bytes 10616836
  61.3 1.6 copy-start.11
  62.9 2.0 copy-start.9
  64.9 41.1 %copy-start.5 = (bf16[24,2304]{1,0:T(8,128)(2,1)S(1)}, bf16[24,2304]{1,0:T(8,128)(2,1)}, u32[]{:S(2)}) copy-start(bf16[24,2304]{1,0:T(8,128)(2,1)} %own_ref.1) | copy-start | bytes 331780
  67.7 76.9 %copy-start.10 = (bf16[2304,4]{0,1:T(4,128)(2,1)S(1)}, bf16[2304,4]{0,1:T(4,128)(2,1)}, u32[]{:S(2)}) copy-start(bf16[2304,4]{0,1:T(4,128)(2,1)} %param.24) | copy-start | bytes 55300
  148.4 3.6 %copy-start.3 = (bf16[2,4,4,24,2304]{4,3,2,1,0:T(8,128)(2,1)S(1)}, bf16[2,4,4,24,2304]{4,3,2,1,0:T(8,128)(2,1)}, u32[]{:S(2)}) copy-start(bf16[2,4,4,24,2304]{4,3,2,1,0:T(8,128)(2,1)} %shard_map.138) | copy-start | bytes 10616836
  148.5 6.0 %slice-start = ((s8[4718592]{0:T(1024)(128)(4,1)}), s8[4194304]{0:T(1024)(128)(4,1)S(1)}, s32[]{:S(2)}) async-start(s8[4718592]{0:T(1024)(128)(4,1)} %bitcast.137), calls=%async_computation | async-start | bytes 8388608
  152.1 2.5 %slice-start.1 = ((s8[4718592]{0:T(1024)(128)(4,1)}), s8[524288]{0:T(1024)(128)(4,1)S(1)}, s32[]{:S(2)}) async-start(s8[4718592]{0:T(1024)(128)(4,1)} %bitcast.137), calls=%async_computation.1 | async-start | bytes 1048576
  155.6 1.7 copy-start.4

commit v5 on v4

--- a/solution.py
+++ b/solution.py
@@ -1,3 +1,5 @@
+import functools
+
 import jax
 import jax.numpy as jnp
 from jax import lax
@@ -250,23 +252,27 @@
     )
 
 
-def scatter_kernel(part_ref, out_ref, got_c, sum_c, x_bufs, sum_x, z_bufs, send_sem, recv_sem):
+def scatter_kernel(with_core, part_ref, out_ref, got_c, sum_c, x_bufs, sum_x, z_bufs, send_sem, recv_sem):
     c = lax.axis_index("core")
     _, _, z_right, z_left = ring_peers("zh")
     _, _, x_right, x_left = ring_peers("x")
     _, _, sibling, _ = ring_peers("core")
     barrier = pltpu.get_barrier_semaphore()
-    for peer in (sibling, x_right, x_left, z_right, z_left):
+    peers = ((sibling,) if with_core else ()) + (x_right, x_left, z_right, z_left)
+    for peer in peers:
         pl.semaphore_signal(barrier, 1, device_id=peer, device_id_type=pl.DeviceIdType.MESH)
-    pl.semaphore_wait(barrier, 5)
+    pl.semaphore_wait(barrier, len(peers))
     sent = []
-    copy = remote(part_ref.at[1 - c], got_c, send_sem.at[0], recv_sem.at[0], sibling)
-    copy.start()
-    sent.append(copy)
-    copy.wait_recv()
-    sum_c[...] = (
-        part_ref[c].astype(jnp.float32) + got_c[...].astype(jnp.float32)
-    ).astype(sum_c.dtype)
+    if with_core:
+        copy = remote(part_ref.at[1 - c], got_c, send_sem.at[0], recv_sem.at[0], sibling)
+        copy.start()
+        sent.append(copy)
+        copy.wait_recv()
+        sum_c[...] = (
+            part_ref[c].astype(jnp.float32) + got_c[...].astype(jnp.float32)
+        ).astype(sum_c.dtype)
+    else:
+        sum_c = part_ref
     x_bufs = [x_bufs.at[0, 0], x_bufs.at[0, 1]] + [x_bufs.at[1, k] for k in range(4)]
     x_bufs = [x_bufs[0].at[..., pl.ds(0, x_bufs[0].shape[-1] // 2)], x_bufs[1].at[..., pl.ds(0, x_bufs[1].shape[-1] // 2)]] + x_bufs[2:]
     total = ring_scatter(lambda i: sum_c.at[i], "x", x_bufs, send_sem.at[1:5], recv_sem.at[1:5], sent)
@@ -278,14 +284,15 @@
         copy.wait_send()
 
 
-def scatter_rows(rows):
+def scatter_rows(rows, with_core=True):
     nx, nz, nc = SIZE["x"], SIZE["zh"], SIZE["core"]
-    blk = rows.shape[0] // (nx * nz * nc)
+    halves_in = nc if with_core else 1
+    blk = rows.shape[0] // (nx * nz * halves_in)
     tail = rows.shape[1:]
-    part = rows.reshape((nc, nx, nz, blk) + tail)
+    part = rows.reshape(((nc,) if with_core else ()) + (nx, nz, blk) + tail)
     links = 9
     return pl.pallas_call(
-        scatter_kernel,
+        functools.partial(scatter_kernel, with_core),
         out_shape=jax.ShapeDtypeStruct((blk,) + tail, jnp.float32),
         in_specs=[pl.BlockSpec(memory_space=pltpu.VMEM)],
         out_specs=pl.BlockSpec(memory_space=pltpu.VMEM),
@@ -298,7 +305,9 @@
             pltpu.SemaphoreType.DMA((links,)),
             pltpu.SemaphoreType.DMA((links,)),
         ],
-        compiler_params=pltpu.CompilerParams(collective_id=1, has_side_effects=True),
+        compiler_params=pltpu.CompilerParams(
+            collective_id=1 if with_core else 2, has_side_effects=True
+        ),
     )(part)
 
 
@@ -360,8 +369,19 @@
         by_request(query), by_request(key_new), by_request(value_new), cache_k, cache_v, cache_len
     )
     heads_flat = from_request_order(heads_out.transpose(0, 2, 1, 3).reshape(TOKENS, head_dev * HDIM))
+    core = lax.axis_index("core")
+    by_core = heads_flat.reshape(SIZE["core"], TOKENS // SIZE["core"], head_dev * HDIM)
+    mine = lax.dynamic_index_in_dim(by_core, core, axis=0, keepdims=False)
+    theirs = lax.dynamic_index_in_dim(by_core, 1 - core, axis=0, keepdims=False)
+    swap = [(0, 1), (1, 0)]
+    from_sibling = lax.ppermute(theirs, "core", swap)
+    w_out_sibling = lax.ppermute(w_out, "core", swap)
     attn = scatter_rows(
-        jnp.dot(heads_flat, w_out, preferred_element_type=jnp.float32).astype(jnp.bfloat16)
+        (
+            jnp.dot(mine, w_out, preferred_element_type=jnp.float32)
+            + jnp.dot(from_sibling, w_out_sibling, preferred_element_type=jnp.float32)
+        ).astype(jnp.bfloat16),
+        with_core=False,
     )
     middle = (hidden_in.astype(jnp.float32) + attn).astype(jnp.bfloat16)
     normed2 = gather_rows(rms_scale(middle, ffn_gain))

time: 214 us -> 208 us (0.972); the launches traced: 211 us -> 208 us
  transfers between devices with their start and end apart: 0 -> 2, of which waited for: 0 -> 0; matrix products, arithmetic and copies ran while one was open for 0% -> 10% of each run, Pallas kernels for 0% -> 20%
where the time goes in v5:
time: 208 us
  Pallas kernels  154 us (74%)
  matrix products  35 us (17%)
  other arithmetic  13.1 us (6%)
  local copies, waits for them, and re-layouts  5.02 us (2%)
    pallas_call x2, Pallas kernels, gather_rows(): pl.pallas_call(gather_kernel, out_shape=jax.ShapeDtypeStruct((nc, nx, nz)...  77.3 us
    pallas_call x2, Pallas kernels, scatter_rows(): pl.pallas_call(functools.partial(scatter_kernel, with_core), out_shape=ja...  76.4 us
    dot_general x4, matrix products, expert_apply(): return jnp.dot(inner, down_part, preferred_element_type=jnp.float32)  13.6 us
    dot_general x4, matrix products, expert_apply(): jnp.einsum('td,kdf->ktf', rows_in, gate_up, preferred_element_type=jnp.fl...  9.03 us
    dot_general x3, matrix products, project(): jnp.dot(normed, weight, preferred_element_type=jnp.float32)  5.72 us
  transfers between devices with their start and end apart: 2, of which 0 were waited for; matrix products, arithmetic and copies ran while one was open for 10% of the time, Pallas kernels for 20%

profile of v5, /device:TPU:22, one launch (start us, length us, event | category | flops | bytes accessed | tf_op | source)
XLA Modules:
  0.0 208.1 jit_solution(2882891239574543985)
XLA Ops:
  0.1 0.9 add.152
  0.9 0.7 iota_compare_fusion
  2.1 0.7 convert_element_type.115
  2.8 40.9 %shard_map.136 = bf16[2,4,4,24,2304]{4,3,2,1,0:T(8,128)(2,1)} custom-call(bf16[24,2304]{1,0:T(8,128)(2,1)} %own_ref.1), custom_call_target="tpu_custom_call" | custom-call | tf_op jit(solution)/shard_map/pallas_call | solution.py:204
  43.7 2.8 %multiply_reduce_fusion = f32[2,4,4,24]{3,2,1,0:T(4,128)S(1)} fusion(bf16[2,4,4,24,2304]{4,3,2,1,0:T(8,128)(2,1)} %shard_map.136), kind=kLoop, calls=%fused_computation.4 | loop fusion | flops 5307648 | bytes 3542016 | tf_op jit(solution)/shard_map/reduce_sum | solution.py:25
  46.6 2.9 %fusion.1 = bf16[768,2304]{1,0:T(8,128)(2,1)S(1)} fusion(f32[2304]{0:T(1024)S(1)} %convert_element_type.115, f32[768]{0:T(1024)S(1)} %rsqrt.20, bf16[2,4,4,24,2304]{4,3,2,1,0:T(8,128)(2,1)} %shard_map.136), kind=kLoop, calls=%fused_computation.2 | loop fusion | flops 7077888 | bytes 7090176 | tf_op jit(solution)/shard_map/convert_element_type | solution.py:26
  49.5 1.7 copy-done.2
  51.2 1.2 convolution_convert_fusion
  52.7 3.3 %convolution_bitcast_fusion.4 = f32[768,1,64]{0,2,1:T(8,128)S(1)} fusion(bf16[768,2304]{1,0:T(8,128)(2,1)} %copy-done.2, bf16[2304,64]{0,1:T(8,128)(2,1)S(1)} %copy-done.8), kind=kOutput, calls=%fused_computation.34 | convolution fusion | flops 226492416 | bytes 4030464 | tf_op jit(solution)/shard_map/dot_general | solution.py:357
  56.0 1.2 convolution_bitcast_fusion.5
  57.2 0.5 fusion.67
  59.0 1.1 fusion.2
  60.2 1.5 fusion.3
  61.8 1.5 fusion.6
  63.8 0.7 collective-permute-start
  64.7 0.6 fusion.70
  65.4 1.8 fusion.5
  67.2 33.0 %shard_map.137 = f32[24,2304]{1,0:T(8,128)} custom-call(bf16[4,4,24,2304]{3,2,1,0:T(8,128)(2,1)} %bitcast.128), custom_call_target="tpu_custom_call" | custom-call | tf_op jit(solution)/shard_map/pallas_call | solution.py:294
  100.2 1.1 fusion.40
  101.3 0.7 fusion.42.own_ref
  102.0 36.4 %shard_map.138 = bf16[2,4,4,24,2304]{4,3,2,1,0:T(8,128)(2,1)} custom-call(bf16[24,2304]{1,0:T(8,128)(2,1)} %fusion.42.own_ref), custom_call_target="tpu_custom_call" | custom-call | tf_op jit(solution)/shard_map/pallas_call | solution.py:204
  138.4 4.4 %convolution_bitcast_fusion = f32[2,768,128]{2,1,0:T(8,128)} fusion(bf16[768,2304,1]{1,0,2:T(8,128)(2,1)} %bitcast.122, bf16[4,2,2304,128]{3,2,1,0:T(8,128)(2,1)} %param.26), kind=kOutput, calls=%fused_computation.17 | convolution fusion | flops 905969664 | bytes 5505024 | tf_op jit(solution)/shard_map/td,kdf->ktf/dot_general | solution.py:52
  142.9 2.4 %convolution_bitcast_fusion.1 = f32[2,768,128]{2,1,0:T(8,128)S(1)} fusion(bf16[768,2304,1]{1,0,2:T(8,128)(2,1)S(1)} %bitcast.123, bf16[4,2,2304,128]{3,2,1,0:T(8,128)(2,1)} %param.26), kind=kOutput, calls=%fused_computation.18 | convolution fusion | flops 905969664 | bytes 5505024 | tf_op jit(solution)/shard_map/td,kdf->ktf/dot_general | solution.py:52
  145.3 1.1 convolution_bitcast_fusion.2
  146.4 1.1 convolution_bitcast_fusion.3
  147.5 1.1 select_reduce_fusion
  149.4 2.3 %fusion.28 = f32[768,2304]{1,0:T(8,128)S(1)} fusion(bf16[4,128,2304]{2,1,0:T(8,128)(2,1)} %param.27, f32[2,768,128]{2,1,0:T(8,128)S(1)} %convolution_bitcast_fusion.3), kind=kOutput, calls=%fused_computation.42 | convolution fusion | flops 453574656 | bytes 8454144 | tf_op jit(solution)/shard_map/dot_general | solution.py:54
  151.7 1.1 fusion.26
  152.8 4.0 %fusion.24 = f32[768,2304]{1,0:T(8,128)} fusion(bf16[4,128,2304]{2,1,0:T(8,128)(2,1)S(1)} %copy-done.5, f32[2,768,128]{2,1,0:T(8,128)S(1)} %convolution_bitcast_fusion.1), kind=kOutput, calls=%fused_computation.38 | convolution fusion | flops 453574656 | bytes 8454144 | tf_op jit(solution)/shard_map/dot_general | solution.py:54
  156.8 6.2 %add_convert_fusion = bf16[768,2304]{1,0:T(8,128)(2,1)} fusion(f32[768,2304]{1,0:T(8,128)} %fusion.24, f32[768,2304]{1,0:T(8,128)S(1)} %fusion.26, f32[768,2304]{1,0:T(8,128)S(1)} %fusion.28, f32[768]{0:T(1024)S(1)} %mul.226, f32[768]{0:T(1024)S(1)} %mul.221, f32[768]{0:T(1024)S(1)} %mul.216, f32[768]{0:T(1024)S(1)} %mul.211, ...), kind=kOutput, calls=%fused_computation.3 | convolution fusion | flops 467730432 | bytes 26165248 | tf_op jit(solution)/shard_map/dot_general | solution.py:54
  163.1 43.4 %shard_map.139 = f32[24,2304]{1,0:T(8,128)} custom-call(bf16[2,4,4,24,2304]{4,3,2,1,0:T(8,128)(2,1)} %bitcast.127), custom_call_target="tpu_custom_call" | custom-call | tf_op jit(solution)/shard_map/pallas_call | solution.py:294
  206.5 1.6 fusion.43
  (88 shorter events, 3.5 us)
Async XLA Ops:
  0.0 59.0 %copy-start = (bf16[8,1,2048,64]{2,3,1,0:T(8,128)(2,1)S(1)}, bf16[8,1,2048,64]{2,3,1,0:T(8,128)(2,1)}, u32[]{:S(2)}) copy-start(bf16[8,1,2048,64]{2,3,1,0:T(8,128)(2,1)} %param.20) | copy-start | bytes 6291460
  0.0 65.4 %collective-permute-start.1 = (bf16[64,2304]{1,0:T(8,128)(2,1)}, bf16[64,2304]{1,0:T(8,128)(2,1)S(1)}, u32[]{:S(2)}, u32[]{:S(2)}) collective-permute-start(bf16[64,2304]{1,0:T(8,128)(2,1)} %param.19), channel_id=1, source_target_pairs={{0,1},{1,0},{2,3},{3,2},{4,5},{5,4},{6,7},{7,6},{8,9},{9,8},{10,11... | collective-permute-start | bytes 884744 | tf_op jit(solution)/shard_map/ppermute | solution.py:378
  46.5 4.7 %copy-start.7 = (bf16[2304,64]{0,1:T(8,128)(2,1)S(1)}, bf16[2304,64]{0,1:T(8,128)(2,1)}, u32[]{:S(2)}) copy-start(bf16[2304,64]{0,1:T(8,128)(2,1)} %param.18) | copy-start | bytes 884740
  49.5 1.8 copy-start.2
  51.2 1.4 copy-start.8
  52.4 3.6 %copy-start.9 = (bf16[2304,64]{0,1:T(8,128)(2,1)S(1)}, bf16[2304,64]{0,1:T(8,128)(2,1)}, u32[]{:S(2)}) copy-start(bf16[2304,64]{0,1:T(8,128)(2,1)} %param.16) | copy-start | bytes 884740
  52.6 3.4 %copy-start.3 = (bf16[768,2304]{1,0:T(8,128)(2,1)S(1)}, bf16[768,2304]{1,0:T(8,128)(2,1)}, u32[]{:S(2)}) copy-start(bf16[768,2304]{1,0:T(8,128)(2,1)} %copy-done.2) | copy-start | bytes 10616836
  60.1 1.6 copy-start.15
  61.7 2.7 %copy-start.13 = (s32[768,2]{0,1:T(2,128)S(1)}, s32[768,2]{0,1:T(2,128)}, u32[]{:S(2)}) copy-start(s32[768,2]{0,1:T(2,128)} %param.25) | copy-start | bytes 18436
  61.7 2.9 %copy-start.10 = (bf16[64,2304]{1,0:T(8,128)(2,1)S(1)}, bf16[64,2304]{1,0:T(8,128)(2,1)}, u32[]{:S(2)}) copy-start(bf16[64,2304]{1,0:T(8,128)(2,1)} %param.19) | copy-start | bytes 884740
  63.3 2.0 copy-start.14
  63.8 1.6 collective-permute-start
  65.3 34.8 %copy-start.6 = (bf16[24,2304]{1,0:T(8,128)(2,1)S(1)}, bf16[24,2304]{1,0:T(8,128)(2,1)}, u32[]{:S(2)}) copy-start(bf16[24,2304]{1,0:T(8,128)(2,1)} %own_ref.1) | copy-start | bytes 331780
  138.4 4.5 %copy-start.4 = (bf16[2,4,4,24,2304]{4,3,2,1,0:T(8,128)(2,1)S(1)}, bf16[2,4,4,24,2304]{4,3,2,1,0:T(8,128)(2,1)}, u32[]{:S(2)}) copy-start(bf16[2,4,4,24,2304]{4,3,2,1,0:T(8,128)(2,1)} %shard_map.138) | copy-start | bytes 10616836
  138.4 6.9 %slice-start = ((s8[4718592]{0:T(1024)(128)(4,1)}), s8[4194304]{0:T(1024)(128)(4,1)S(1)}, s32[]{:S(2)}) async-start(s8[4718592]{0:T(1024)(128)(4,1)} %bitcast.144), calls=%async_computation | async-start | bytes 8388608
  142.9 2.4 %slice-start.1 = ((s8[4718592]{0:T(1024)(128)(4,1)}), s8[524288]{0:T(1024)(128)(4,1)S(1)}, s32[]{:S(2)}) async-start(s8[4718592]{0:T(1024)(128)(4,1)} %bitcast.144), calls=%async_computation.1 | async-start | bytes 1048576
  146.4 1.1 copy-start.12
  149.4 2.3 %copy-start.5 = (bf16[4,128,2304]{2,1,0:T(8,128)(2,1)S(1)}, bf16[4,128,2304]{2,1,0:T(8,128)(2,1)}, u32[]{:S(2)}) copy-start(bf16[4,128,2304]{2,1,0:T(8,128)(2,1)} %param.27) | copy-start | bytes 7077892
  152.8 4.0 %copy-start.11 = (f32[2,768,128]{2,1,0:T(8,128)S(1)}, f32[2,768,128]{2,1,0:T(8,128)}, u32[]{:S(2)}) copy-start(f32[2,768,128]{2,1,0:T(8,128)} %convolution_bitcast_fusion) | copy-start | bytes 2359300
  156.8 51.3 %copy-start.1 = (bf16[8,1,2048,64]{2,3,1,0:T(8,128)(2,1)S(1)}, bf16[8,1,2048,64]{2,3,1,0:T(8,128)(2,1)}, u32[]{:S(2)}) copy-start(bf16[8,1,2048,64]{2,3,1,0:T(8,128)(2,1)} %param.20) | copy-start | bytes 6291460

commit v6 on v5

--- a/solution.py
+++ b/solution.py
@@ -350,6 +350,8 @@
     n_experts = w_gate_up.shape[0]
     whole_in = gather_rows(hidden_in)
     normed = rms_scale(whole_in, attn_gain)
+    w_down_later, _ = lax.optimization_barrier((w_down, whole_in))
+    w_down_sibling = lax.ppermute(w_down_later, "core", [(0, 1), (1, 0)])
     positions = (cache_len[:, None] + jnp.arange(NEW, dtype=jnp.int32)[None, :]).reshape(-1)
     positions = from_request_order(positions)
 
@@ -369,6 +371,7 @@
         by_request(query), by_request(key_new), by_request(value_new), cache_k, cache_v, cache_len
     )
     heads_flat = from_request_order(heads_out.transpose(0, 2, 1, 3).reshape(TOKENS, head_dev * HDIM))
+    heads_flat, w_down_sibling = lax.optimization_barrier((heads_flat, w_down_sibling))
     core = lax.axis_index("core")
     by_core = heads_flat.reshape(SIZE["core"], TOKENS // SIZE["core"], head_dev * HDIM)
     mine = lax.dynamic_index_in_dim(by_core, core, axis=0, keepdims=False)
@@ -388,14 +391,26 @@
     logits = jnp.dot(normed2, router, preferred_element_type=jnp.float32)
     routes = from_request_order(routes)
     pair_weights = route_weights(logits, routes)
-    running = jnp.zeros((TOKENS, width), jnp.float32)
+    half = TOKENS // SIZE["core"]
+    both = jnp.einsum("td,ekdf->ektf", normed2, w_gate_up, preferred_element_type=jnp.float32)
+    inner = (jax.nn.silu(both[:, 0]) * both[:, 1]).astype(jnp.bfloat16)
+    inner = inner.reshape(n_experts, SIZE["core"], half, -1)
+    inner_mine = lax.dynamic_index_in_dim(inner, core, axis=1, keepdims=False)
+    inner_theirs = lax.dynamic_index_in_dim(inner, 1 - core, axis=1, keepdims=False)
+    inner_sibling = lax.ppermute(inner_theirs, "core", swap)
+    running = jnp.zeros((half, width), jnp.float32)
     for expert in range(n_experts):
         dense_weight = jnp.sum(jnp.where(routes == expert, pair_weights, 0.0), axis=1)
-        running = (
-            running
-            + expert_apply(normed2, w_gate_up[expert], w_down[expert]) * dense_weight[:, None]
+        weight_mine = lax.dynamic_index_in_dim(
+            dense_weight.reshape(SIZE["core"], half), core, axis=0, keepdims=False
         )
-    expert_out = scatter_rows(running.astype(jnp.bfloat16))
+        running = running + (
+            jnp.dot(inner_mine[expert], w_down[expert], preferred_element_type=jnp.float32)
+            + jnp.dot(
+                inner_sibling[expert], w_down_sibling[expert], preferred_element_type=jnp.float32
+            )
+        ) * weight_mine[:, None]
+    expert_out = scatter_rows(running.astype(jnp.bfloat16), with_core=False)
     return (middle.astype(jnp.float32) + expert_out).astype(jnp.bfloat16)
 
 

time: 208 us -> 208 us (level)
  Pallas kernels: 154 us -> 147 us
  matrix products: 35 us -> 40.9 us
    pallas_call x2, Pallas kernels: 76.4 us -> 68.3 us  [scatter_rows(): pl.pallas_call(functools.partial(scatter_kernel, with_core), out_shape=ja...]
    dot_general x8 -> x9, matrix products: 22.7 us -> 28.7 us  [the longest x4 12.3 us: local(): jnp.dot(inner_mine[expert], w_down[expert], preferred_element_type=jnp.fl...]
  transfers between devices with their start and end apart: 2 -> 4, of which waited for: 0 -> 1; matrix products, arithmetic and copies ran while one was open for 10% -> 14% of each run, Pallas kernels for 20% -> 20%
where the time goes in v6:
time: 208 us
  Pallas kernels  147 us (71%)
  matrix products  40.9 us (20%)
  other arithmetic  12.8 us (6%)
  local copies, waits for them, and re-layouts  4.63 us (2%)
    pallas_call x2, Pallas kernels, gather_rows(): pl.pallas_call(gather_kernel, out_shape=jax.ShapeDtypeStruct((nc, nx, nz)...  78.4 us
    pallas_call x2, Pallas kernels, scatter_rows(): pl.pallas_call(functools.partial(scatter_kernel, with_core), out_shape=ja...  68.3 us
    dot_general x4, matrix products, local(): jnp.dot(inner_mine[expert], w_down[expert], preferred_element_type=jnp.fl...  12.3 us
    dot_general x4, matrix products, local(): jnp.dot(inner_sibling[expert], w_down_sibling[expert], preferred_element_...  9.69 us
    dot_general x1, matrix products, local(): jnp.einsum('td,ekdf->ektf', normed2, w_gate_up, preferred_element_type=jn...  6.74 us
    dot_general x3, matrix products, project(): jnp.dot(normed, weight, preferred_element_type=jnp.float32)  5.58 us
  transfers between devices with their start and end apart: 4, of which 1 were waited for; matrix products, arithmetic and copies ran while one was open for 14% of the time, Pallas kernels for 20%

profile of v6, /device:TPU:22, one launch (start us, length us, event | category | flops | bytes accessed | tf_op | source)
XLA Modules:
  0.0 207.7 jit_solution(3459743030653815930)
XLA Ops:
  0.0 0.5 collective-permute-start.2
  0.5 0.8 add.160
  1.4 0.7 iota_compare_fusion
  2.1 40.7 %shard_map.136 = bf16[2,4,4,24,2304]{4,3,2,1,0:T(8,128)(2,1)} custom-call(bf16[24,2304]{1,0:T(8,128)(2,1)} %own_ref.1), custom_call_target="tpu_custom_call" | custom-call | tf_op jit(solution)/shard_map/pallas_call | solution.py:204
  42.8 2.8 %multiply_reduce_fusion = f32[2,4,4,24]{3,2,1,0:T(4,128)S(1)} fusion(bf16[2,4,4,24,2304]{4,3,2,1,0:T(8,128)(2,1)} %shard_map.136), kind=kLoop, calls=%fused_computation.1 | loop fusion | flops 5307648 | bytes 3542016 | tf_op jit(solution)/shard_map/reduce_sum | solution.py:25
  45.7 2.9 %multiply_convert_fusion = bf16[768,2304]{1,0:T(8,128)(2,1)S(1)} fusion(f32[2304]{0:T(1024)S(1)} %convert_element_type.91, f32[768]{0:T(1024)S(1)} %rsqrt.20, bf16[2,4,4,24,2304]{4,3,2,1,0:T(8,128)(2,1)} %shard_map.136), kind=kLoop, calls=%fused_computation | loop fusion | flops 7077888 | bytes 7090176 | tf_op jit(solution)/shard_map/convert_element_type | solution.py:26
  48.7 1.2 convolution_bitcast_fusion.1
  49.9 0.5 copy-done.2
  50.4 1.2 convolution_bitcast_fusion.2
  53.5 3.2 %convolution_convert_fusion = bf16[768,64]{0,1:T(8,128)(2,1)S(1)} fusion(bf16[768,2304]{1,0:T(8,128)(2,1)} %copy-done.2, bf16[2304,64]{0,1:T(8,128)(2,1)S(1)} %copy-done.9), kind=kOutput, calls=%fused_computation.35 | convolution fusion | flops 226541568 | bytes 3932160 | tf_op jit(solution)/shard_map/dot_general | solution.py:359
  57.2 1.1 fusion
  58.4 1.5 fusion.1
  60.0 1.5 fusion.12
  62.3 0.7 collective-permute-start.1
  62.9 0.6 fusion.65
  63.9 1.8 fusion.10
  65.7 32.8 %shard_map.137 = f32[24,2304]{1,0:T(8,128)} custom-call(bf16[4,4,24,2304]{3,2,1,0:T(8,128)(2,1)} %bitcast.131), custom_call_target="tpu_custom_call" | custom-call | tf_op jit(solution)/shard_map/pallas_call | solution.py:294
  98.5 1.1 fusion.43
  99.6 0.7 fusion.45.own_ref
  100.3 37.7 %shard_map.138 = bf16[2,4,4,24,2304]{4,3,2,1,0:T(8,128)(2,1)} custom-call(bf16[24,2304]{1,0:T(8,128)(2,1)} %fusion.45.own_ref), custom_call_target="tpu_custom_call" | custom-call | tf_op jit(solution)/shard_map/pallas_call | solution.py:204
  138.0 6.7 %convolution_bitcast_fusion = f32[4,2,768,128]{3,2,1,0:T(8,128)S(1)} fusion(bf16[768,2304,1,1]{1,0,3,2:T(8,128)(2,1)} %bitcast.129, bf16[4,2,2304,128]{3,2,1,0:T(8,128)(2,1)} %param.26), kind=kOutput, calls=%fused_computation.26 | convolution fusion | flops 3623878656 | bytes 11403264 | tf_op jit(solution)/shard_map/td,ekdf->ektf/dot_general | solution.py:395
  145.4 3.7 %fusion.31 = f32[384,2304]{1,0:T(8,128)} fusion(bf16[4,128,2304]{2,1,0:T(8,128)(2,1)} %param.27, bf16[4,2,384,128]{3,2,1,0:T(8,128)(2,1)S(1)} %multiply_convert_fusion.1, s32[]{:T(128)S(6)} %select_n.51), kind=kOutput, calls=%fused_computation.46 | convolution fusion | flops 226492416 | bytes 4227076 | tf_op jit(solution)/shard_map/dot_general | solution.py:408
  149.1 1.1 select_reduce_fusion
  150.9 3.5 %fusion.28 = f32[384,2304]{1,0:T(8,128)} fusion(bf16[4,128,2304]{2,1,0:T(8,128)(2,1)} %param.27, bf16[4,2,384,128]{3,2,1,0:T(8,128)(2,1)S(1)} %multiply_convert_fusion.1, s32[]{:T(128)S(6)} %add.201, s32[]{:T(128)S(6)} %select_n.51), kind=kOutput, calls=%fused_computation.43 | convolution fusion | flops 226492416 | bytes 4227080 | tf_op jit(solution)/shard_map/dot_general | solution.py:408
  154.4 3.5 %fusion.25 = f32[384,2304]{1,0:T(8,128)} fusion(bf16[4,128,2304]{2,1,0:T(8,128)(2,1)} %param.27, bf16[4,2,384,128]{3,2,1,0:T(8,128)(2,1)S(1)} %multiply_convert_fusion.1, s32[]{:T(128)S(6)} %add.202, s32[]{:T(128)S(6)} %select_n.51), kind=kOutput, calls=%fused_computation.40 | convolution fusion | flops 226492416 | bytes 4227080 | tf_op jit(solution)/shard_map/dot_general | solution.py:408
  158.5 1.7 fusion.22
  160.2 3.0 %fusion.9 = f32[384,2304]{1,0:T(8,128)S(1)} fusion(f32[384,2304]{1,0:T(8,128)} %fusion.31, f32[384]{0:T(512)S(1)} %get-tuple-element.35, bf16[4,128,2304]{2,1,0:T(8,128)(2,1)} %collective-permute-done, bf16[4,384,128]{2,1,0:T(8,128)(2,1)S(1)} %collective-permute-done.3), kind=kOutput, calls=%fused_computation.17 | convolution fusion | flops 228261888 | bytes 7768064 | tf_op jit(solution)/shard_map/dot_general | solution.py:409
  163.5 1.9 fusion.8
  165.6 1.7 fusion.6
  167.4 3.1 %fusion.11 = bf16[384,2304]{1,0:T(8,128)(2,1)} fusion(f32[384,2304]{1,0:T(8,128)S(1)} %fusion.6, f32[384,2304]{1,0:T(8,128)S(1)} %fusion.22, f32[384]{0:T(512)S(1)} %get-tuple-element.38, bf16[4,128,2304]{2,1,0:T(8,128)(2,1)} %collective-permute-done, bf16[4,384,128]{2,1,0:T(8,128)(2,1)S(1)} %collective-permute-done.3), kind=kOutput, calls=%fused_computation.20 | convolution fusion | flops 230031360 | bytes 9537536 | tf_op jit(solution)/shard_map/dot_general | solution.py:409
  170.5 35.6 %shard_map.139 = f32[24,2304]{1,0:T(8,128)} custom-call(bf16[4,4,24,2304]{3,2,1,0:T(8,128)(2,1)} %bitcast.132), custom_call_target="tpu_custom_call" | custom-call | tf_op jit(solution)/shard_map/pallas_call | solution.py:294
  206.1 1.6 fusion.46
  (93 shorter events, 6.1 us)
Async XLA Ops:
  0.0 57.2 %copy-start = (bf16[8,1,2048,64]{2,3,1,0:T(8,128)(2,1)S(1)}, bf16[8,1,2048,64]{2,3,1,0:T(8,128)(2,1)}, u32[]{:S(2)}) copy-start(bf16[8,1,2048,64]{2,3,1,0:T(8,128)(2,1)} %param.20) | copy-start | bytes 6291460
  0.0 62.2 %collective-permute-start = (bf16[4,128,2304]{2,1,0:T(8,128)(2,1)}, bf16[4,128,2304]{2,1,0:T(8,128)(2,1)}, u32[]{:S(2)}, u32[]{:S(2)}) collective-permute-start(bf16[4,128,2304]{2,1,0:T(8,128)(2,1)} %param.27), channel_id=1, source_target_pairs={{0,1},{1,0},{2,3},{3,2},{4,5},{5,4},{6,7},{7,6},{8,9},{9,8},{10,11... | collective-permute-start | bytes 7077896 | tf_op jit(solution)/shard_map/ppermute | solution.py:354
  0.0 63.5 %collective-permute-start.2 = (bf16[64,2304]{1,0:T(8,128)(2,1)}, bf16[64,2304]{1,0:T(8,128)(2,1)S(1)}, u32[]{:S(2)}, u32[]{:S(2)}) collective-permute-start(bf16[64,2304]{1,0:T(8,128)(2,1)} %param.19), channel_id=1, source_target_pairs={{0,1},{1,0},{2,3},{3,2},{4,5},{5,4},{6,7},{7,6},{8,9},{9,8},{10,11... | collective-permute-start | bytes 884744 | tf_op jit(solution)/shard_map/ppermute | solution.py:381
  2.1 43.6 %copy-start.13 = (bf16[2304]{0:T(1024)(128)(2,1)S(1)}, bf16[2304]{0:T(1024)(128)(2,1)}, u32[]{:S(2)}) copy-start(bf16[2304]{0:T(1024)(128)(2,1)} %param.15) | copy-start | bytes 13828
  45.7 2.9 %copy-start.7 = (bf16[2304,64]{0,1:T(8,128)(2,1)S(1)}, bf16[2304,64]{0,1:T(8,128)(2,1)}, u32[]{:S(2)}) copy-start(bf16[2304,64]{0,1:T(8,128)(2,1)} %param.17) | copy-start | bytes 884740
  48.7 1.8 copy-start.2
  48.7 1.8 copy-start.8
  50.4 3.1 %copy-start.9 = (bf16[2304,64]{0,1:T(8,128)(2,1)S(1)}, bf16[2304,64]{0,1:T(8,128)(2,1)}, u32[]{:S(2)}) copy-start(bf16[2304,64]{0,1:T(8,128)(2,1)} %param.18) | copy-start | bytes 884740
  58.3 1.6 copy-start.15
  59.9 2.0 copy-start.14
  59.9 2.0 copy-start.12
  60.0 3.0 %copy-start.10 = (bf16[64,2304]{1,0:T(8,128)(2,1)S(1)}, bf16[64,2304]{1,0:T(8,128)(2,1)}, u32[]{:S(2)}) copy-start(bf16[64,2304]{1,0:T(8,128)(2,1)} %param.19) | copy-start | bytes 884740
  62.3 1.6 collective-permute-start.1
  63.5 35.0 %copy-start.6 = (bf16[24,2304]{1,0:T(8,128)(2,1)S(1)}, bf16[24,2304]{1,0:T(8,128)(2,1)}, u32[]{:S(2)}) copy-start(bf16[24,2304]{1,0:T(8,128)(2,1)} %own_ref.1) | copy-start | bytes 331780
  145.0 4.1 %copy-start.3 = (bf16[2,4,4,24,2304]{4,3,2,1,0:T(8,128)(2,1)S(1)}, bf16[2,4,4,24,2304]{4,3,2,1,0:T(8,128)(2,1)}, u32[]{:S(2)}) copy-start(bf16[2,4,4,24,2304]{4,3,2,1,0:T(8,128)(2,1)} %shard_map.138) | copy-start | bytes 10616836
  145.0 4.1 %copy-start.11 = (bf16[2304,4]{0,1:T(4,128)(2,1)S(1)}, bf16[2304,4]{0,1:T(4,128)(2,1)}, u32[]{:S(2)}) copy-start(bf16[2304,4]{0,1:T(4,128)(2,1)} %param.24) | copy-start | bytes 55300
  150.4 9.8 %collective-permute-start.3 = (bf16[4,384,128]{2,1,0:T(8,128)(2,1)S(1)}, bf16[4,384,128]{2,1,0:T(8,128)(2,1)S(1)}, u32[]{:S(2)}, u32[]{:S(2)}) collective-permute-start(bf16[4,384,128]{2,1,0:T(8,128)(2,1)S(1)} %dynamic-slice_bitcast_fusion), channel_id=1, source_target_pairs={{0,1},{1,0},{2,3},{3,2},{4,5},{5,4},{6,7},{7,6},{8,9},{9,8},{10,11... | collective-permute-start | bytes 1179656 | tf_op jit(solution)/shard_map/ppermute | solution.py:400
  160.2 3.2 %copy-start.5 = (f32[384,2304]{1,0:T(8,128)S(1)}, f32[384,2304]{1,0:T(8,128)}, u32[]{:S(2)}) copy-start(f32[384,2304]{1,0:T(8,128)} %fusion.28) | copy-start | bytes 10616836
  163.4 2.2 %copy-start.4 = (f32[384,2304]{1,0:T(8,128)S(1)}, f32[384,2304]{1,0:T(8,128)}, u32[]{:S(2)}) copy-start(f32[384,2304]{1,0:T(8,128)} %fusion.25) | copy-start | bytes 10616836
  167.4 40.3 %copy-start.1 = (bf16[8,1,2048,64]{2,3,1,0:T(8,128)(2,1)S(1)}, bf16[8,1,2048,64]{2,3,1,0:T(8,128)(2,1)}, u32[]{:S(2)}) copy-start(bf16[8,1,2048,64]{2,3,1,0:T(8,128)(2,1)} %param.20) | copy-start | bytes 6291460

commit v7 on v6

--- a/solution.py
+++ b/solution.py
@@ -398,18 +398,17 @@
     inner_mine = lax.dynamic_index_in_dim(inner, core, axis=1, keepdims=False)
     inner_theirs = lax.dynamic_index_in_dim(inner, 1 - core, axis=1, keepdims=False)
     inner_sibling = lax.ppermute(inner_theirs, "core", swap)
-    running = jnp.zeros((half, width), jnp.float32)
-    for expert in range(n_experts):
-        dense_weight = jnp.sum(jnp.where(routes == expert, pair_weights, 0.0), axis=1)
-        weight_mine = lax.dynamic_index_in_dim(
-            dense_weight.reshape(SIZE["core"], half), core, axis=0, keepdims=False
-        )
-        running = running + (
-            jnp.dot(inner_mine[expert], w_down[expert], preferred_element_type=jnp.float32)
-            + jnp.dot(
-                inner_sibling[expert], w_down_sibling[expert], preferred_element_type=jnp.float32
-            )
-        ) * weight_mine[:, None]
+    dense_weight = jnp.stack(
+        [jnp.sum(jnp.where(routes == expert, pair_weights, 0.0), axis=1) for expert in range(n_experts)]
+    )
+    weight_mine = lax.dynamic_index_in_dim(
+        dense_weight.reshape(n_experts, SIZE["core"], half), core, axis=1, keepdims=False
+    )[..., None]
+    scaled_mine = (inner_mine.astype(jnp.float32) * weight_mine).astype(jnp.bfloat16)
+    scaled_sibling = (inner_sibling.astype(jnp.float32) * weight_mine).astype(jnp.bfloat16)
+    running = jnp.einsum(
+        "etf,efd->td", scaled_mine, w_down, preferred_element_type=jnp.float32
+    ) + jnp.einsum("etf,efd->td", scaled_sibling, w_down_sibling, preferred_element_type=jnp.float32)
     expert_out = scatter_rows(running.astype(jnp.bfloat16), with_core=False)
     return (middle.astype(jnp.float32) + expert_out).astype(jnp.bfloat16)
 

time: 208 us -> 198 us (0.952)
  matrix products: 40.9 us -> 26.4 us
    dot_general x8 -> x2, matrix products: 22 us -> 5.33 us  [the longest x1 4.12 us: local(): jnp.einsum('etf,efd->td', scaled_sibling, w_down_sibling, preferred_eleme...]
  transfers between devices with their start and end apart: 4 -> 4, of which waited for: 1 -> 1; matrix products, arithmetic and copies ran while one was open for 14% -> 12% of each run, Pallas kernels for 20% -> 21%
where the time goes in v7:
time: 198 us; the launch traced here: 197 us
  Pallas kernels  147 us (74%)
  matrix products  26.4 us (13%)
  other arithmetic  14.2 us (7%)
  local copies, waits for them, and re-layouts  6.57 us (3%)
    pallas_call x2, Pallas kernels, gather_rows(): pl.pallas_call(gather_kernel, out_shape=jax.ShapeDtypeStruct((nc, nx, nz)...  78.3 us
    pallas_call x2, Pallas kernels, scatter_rows(): pl.pallas_call(functools.partial(scatter_kernel, with_core), out_shape=ja...  68.9 us
    dot_general x1, matrix products, local(): jnp.einsum('td,ekdf->ektf', normed2, w_gate_up, preferred_element_type=jn...  6.74 us
    dot_general x3, matrix products, project(): jnp.dot(normed, weight, preferred_element_type=jnp.float32)  5.73 us
    dot_general x1, matrix products, local(): jnp.einsum('etf,efd->td', scaled_sibling, w_down_sibling, preferred_eleme...  4.12 us
  transfers between devices with their start and end apart: 4, of which 1 were waited for; matrix products, arithmetic and copies ran while one was open for 12% of the time, Pallas kernels for 21%

profile of v7, /device:TPU:22, one launch (start us, length us, event | category | flops | bytes accessed | tf_op | source)
XLA Modules:
  0.0 196.9 jit_solution(15199684985028845193)
XLA Ops:
  0.0 0.5 collective-permute-start
  0.5 0.8 add.139
  1.4 0.7 iota_compare_fusion
  2.5 0.7 convert_element_type.106
  3.2 0.7 convert_element_type.117
  3.9 0.8 reshape.467
  4.8 40.7 %shard_map.136 = bf16[2,4,4,24,2304]{4,3,2,1,0:T(8,128)(2,1)} custom-call(bf16[24,2304]{1,0:T(8,128)(2,1)} %own_ref.1), custom_call_target="tpu_custom_call" | custom-call | tf_op jit(solution)/shard_map/pallas_call | solution.py:204
  45.5 2.8 %multiply_reduce_fusion = f32[2,4,4,24]{3,2,1,0:T(4,128)S(1)} fusion(bf16[2,4,4,24,2304]{4,3,2,1,0:T(8,128)(2,1)} %shard_map.136), kind=kLoop, calls=%fused_computation.1 | loop fusion | flops 5307648 | bytes 3542016 | tf_op jit(solution)/shard_map/reduce_sum | solution.py:25
  48.4 2.9 %multiply_convert_fusion = bf16[768,2304]{1,0:T(8,128)(2,1)S(1)} fusion(f32[2304]{0:T(1024)S(1)} %convert_element_type.106, f32[768]{0:T(1024)S(1)} %rsqrt.20, bf16[2,4,4,24,2304]{4,3,2,1,0:T(8,128)(2,1)} %shard_map.136), kind=kLoop, calls=%fused_computation | loop fusion | flops 7077888 | bytes 7090176 | tf_op jit(solution)/shard_map/convert_element_type | solution.py:26
  51.3 1.7 copy-done.1
  53.1 1.2 convolution_convert_fusion
  54.5 3.3 %convolution_bitcast_fusion.3 = f32[768,1,64]{0,2,1:T(8,128)S(1)} fusion(bf16[768,2304]{1,0:T(8,128)(2,1)} %copy-done.1, bf16[2304,64]{0,1:T(8,128)(2,1)S(1)} %copy-done.6), kind=kOutput, calls=%fused_computation.26 | convolution fusion | flops 226492416 | bytes 4030464 | tf_op jit(solution)/shard_map/dot_general | solution.py:359
  57.9 1.2 convolution_bitcast_fusion.4
  59.1 0.5 fusion.43
  60.9 1.1 fusion
  62.1 1.5 fusion.1
  63.6 1.5 fusion.6
  65.6 0.7 collective-permute-start.1
  66.3 0.6 fusion.46
  67.2 1.8 fusion.5
  69.0 32.8 %shard_map.137 = f32[24,2304]{1,0:T(8,128)} custom-call(bf16[4,4,24,2304]{3,2,1,0:T(8,128)(2,1)} %bitcast.102), custom_call_target="tpu_custom_call" | custom-call | tf_op jit(solution)/shard_map/pallas_call | solution.py:294
  101.9 1.1 fusion.24
  103.0 0.7 fusion.26.own_ref
  103.7 37.6 %shard_map.138 = bf16[2,4,4,24,2304]{4,3,2,1,0:T(8,128)(2,1)} custom-call(bf16[24,2304]{1,0:T(8,128)(2,1)} %fusion.26.own_ref), custom_call_target="tpu_custom_call" | custom-call | tf_op jit(solution)/shard_map/pallas_call | solution.py:204
  141.4 3.1 %select_reduce_fusion = (f32[768]{0:T(1024)S(1)}, f32[768]{0:T(1024)S(1)}) fusion(s32[768]{0:T(1024)S(1)} %get-tuple-element.17, s32[768]{0:T(1024)S(1)} %get-tuple-element.18, bf16[768,2304]{1,0:T(8,128)(2,1)} %bitcast.100, bf16[2304,4]{0,1:T(4,128)(2,1)S(1)} %copy-done.9), kind=kOutput, calls=%fused_computation.91 | convolution fusion | flops 14172672 | bytes 3569664 | tf_op jit(solution)/shard_map/dot_general | solution.py:391
  145.3 6.7 %convolution_bitcast_fusion.2 = f32[4,2,768,128]{3,2,1,0:T(8,128)S(1)} fusion(bf16[768,2304,1,1]{1,0,3,2:T(8,128)(2,1)} %bitcast.101, bf16[4,2,2304,128]{3,2,1,0:T(8,128)(2,1)} %param.26), kind=kOutput, calls=%fused_computation.18 | convolution fusion | flops 3623878656 | bytes 11403264 | tf_op jit(solution)/shard_map/td,ekdf->ektf/dot_general | solution.py:395
  152.7 0.5 collective-permute-start.3
  153.2 0.7 copy-done.3
  153.9 1.2 convolution_bitcast_fusion.1
  155.1 4.1 %fusion.4 = bf16[384,2304]{1,0:T(8,128)(2,1)} fusion(f32[384,2304]{1,0:T(8,128)S(1)} %convolution_bitcast_fusion.1, bf16[4,128,2304]{2,1,0:T(8,128)(2,1)} %collective-permute-done, bf16[4,384,128]{2,1,0:T(8,128)(2,1)S(1)} %collective-permute-done.3, f32[4,384]{1,0:T(4,128)S(1)} %bitcast.120), kind=kOutput, calls=%fused_computation.11 | convolution fusion | flops 908328960 | bytes 8067072 | tf_op jit(solution)/shard_map/etf,efd->td/dot_general | solution.py:411
  159.2 36.1 %shard_map.139 = f32[24,2304]{1,0:T(8,128)} custom-call(bf16[4,4,24,2304]{3,2,1,0:T(8,128)(2,1)} %bitcast.103), custom_call_target="tpu_custom_call" | custom-call | tf_op jit(solution)/shard_map/pallas_call | solution.py:294
  195.3 1.6 fusion.27
  (77 shorter events, 4.4 us)
Async XLA Ops:
  0.0 60.8 %copy-start = (bf16[8,1,2048,64]{2,3,1,0:T(8,128)(2,1)S(1)}, bf16[8,1,2048,64]{2,3,1,0:T(8,128)(2,1)}, u32[]{:S(2)}) copy-start(bf16[8,1,2048,64]{2,3,1,0:T(8,128)(2,1)} %param.20) | copy-start | bytes 6291460
  0.0 66.9 %collective-permute-start.2 = (bf16[64,2304]{1,0:T(8,128)(2,1)}, bf16[64,2304]{1,0:T(8,128)(2,1)S(1)}, u32[]{:S(2)}, u32[]{:S(2)}) collective-permute-start(bf16[64,2304]{1,0:T(8,128)(2,1)} %param.19), channel_id=1, source_target_pairs={{0,1},{1,0},{2,3},{3,2},{4,5},{5,4},{6,7},{7,6},{8,9},{9,8},{10,11... | collective-permute-start | bytes 884744 | tf_op jit(solution)/shard_map/ppermute | solution.py:381
  0.0 65.6 %collective-permute-start = (bf16[4,128,2304]{2,1,0:T(8,128)(2,1)}, bf16[4,128,2304]{2,1,0:T(8,128)(2,1)}, u32[]{:S(2)}, u32[]{:S(2)}) collective-permute-start(bf16[4,128,2304]{2,1,0:T(8,128)(2,1)} %param.27), channel_id=1, source_target_pairs={{0,1},{1,0},{2,3},{3,2},{4,5},{5,4},{6,7},{7,6},{8,9},{9,8},{10,11... | collective-permute-start | bytes 7077896 | tf_op jit(solution)/shard_map/ppermute | solution.py:354
  48.4 4.7 %copy-start.5 = (bf16[2304,64]{0,1:T(8,128)(2,1)S(1)}, bf16[2304,64]{0,1:T(8,128)(2,1)}, u32[]{:S(2)}) copy-start(bf16[2304,64]{0,1:T(8,128)(2,1)} %param.18) | copy-start | bytes 884740
  51.3 1.8 copy-start.1
  53.1 1.4 copy-start.6
  54.3 3.6 %copy-start.7 = (bf16[2304,64]{0,1:T(8,128)(2,1)S(1)}, bf16[2304,64]{0,1:T(8,128)(2,1)}, u32[]{:S(2)}) copy-start(bf16[2304,64]{0,1:T(8,128)(2,1)} %param.16) | copy-start | bytes 884740
  54.5 3.4 %copy-start.2 = (bf16[768,2304]{1,0:T(8,128)(2,1)S(1)}, bf16[768,2304]{1,0:T(8,128)(2,1)}, u32[]{:S(2)}) copy-start(bf16[768,2304]{1,0:T(8,128)(2,1)} %copy-done.1) | copy-start | bytes 10616836
  62.0 1.6 copy-start.10
  63.6 2.7 %copy-start.8 = (bf16[64,2304]{1,0:T(8,128)(2,1)S(1)}, bf16[64,2304]{1,0:T(8,128)(2,1)}, u32[]{:S(2)}) copy-start(bf16[64,2304]{1,0:T(8,128)(2,1)} %param.19) | copy-start | bytes 884740
  65.6 1.6 collective-permute-start.1
  66.9 35.0 %copy-start.4 = (bf16[24,2304]{1,0:T(8,128)(2,1)S(1)}, bf16[24,2304]{1,0:T(8,128)(2,1)}, u32[]{:S(2)}) copy-start(bf16[24,2304]{1,0:T(8,128)(2,1)} %own_ref.1) | copy-start | bytes 331780
  69.0 72.3 %copy-start.9 = (bf16[2304,4]{0,1:T(4,128)(2,1)S(1)}, bf16[2304,4]{0,1:T(4,128)(2,1)}, u32[]{:S(2)}) copy-start(bf16[2304,4]{0,1:T(4,128)(2,1)} %param.24) | copy-start | bytes 55300
  152.2 1.7 copy-start.3
  152.7 2.4 %collective-permute-start.3 = (bf16[4,384,128]{2,1,0:T(8,128)(2,1)S(1)}, bf16[4,384,128]{2,1,0:T(8,128)(2,1)S(1)}, u32[]{:S(2)}, u32[]{:S(2)}) collective-permute-start(bf16[4,384,128]{2,1,0:T(8,128)(2,1)S(1)} %dynamic-slice_bitcast_fusion), channel_id=1, source_target_pairs={{0,1},{1,0},{2,3},{3,2},{4,5},{5,4},{6,7},{7,6},{8,9},{9,8},{10,11... | collective-permute-start | bytes 1179656 | tf_op jit(solution)/shard_map/ppermute | solution.py:400

commit v8 on v7

--- a/solution.py
+++ b/solution.py
@@ -348,9 +348,8 @@
     width = hidden_in.shape[1]
     head_dev = cache_k.shape[1]
     n_experts = w_gate_up.shape[0]
-    whole_in = gather_rows(hidden_in)
-    normed = rms_scale(whole_in, attn_gain)
-    w_down_later, _ = lax.optimization_barrier((w_down, whole_in))
+    normed = gather_rows(rms_scale(hidden_in, attn_gain))
+    w_down_later, _ = lax.optimization_barrier((w_down, normed))
     w_down_sibling = lax.ppermute(w_down_later, "core", [(0, 1), (1, 0)])
     positions = (cache_len[:, None] + jnp.arange(NEW, dtype=jnp.int32)[None, :]).reshape(-1)
     positions = from_request_order(positions)

time: 198 us -> 191 us (0.965)
  other arithmetic: 14.2 us -> 10 us
  local copies, waits for them, and re-layouts: 6.57 us -> 3.3 us
  matrix products: 26.4 us -> 28.4 us
    pallas_call x2, Pallas kernels: 78.3 us -> 75 us  [gather_rows(): pl.pallas_call(gather_kernel, out_shape=jax.ShapeDtypeStruct((nc, nx, nz)...]
    pallas_call x2, Pallas kernels: 68.9 us -> 71.3 us  [scatter_rows(): pl.pallas_call(functools.partial(scatter_kernel, with_core), out_shape=ja...]
    dot_general x3, matrix products: 5.73 us -> 7.73 us  [project(): jnp.dot(normed, weight, preferred_element_type=jnp.float32)]
  transfers between devices with their start and end apart: 4 -> 4, of which waited for: 1 -> 1; matrix products, arithmetic and copies ran while one was open for 12% -> 11% of each run, Pallas kernels for 21% -> 21%
where the time goes in v8:
time: 191 us
  Pallas kernels  146 us (76%)
  matrix products  28.4 us (15%)
  other arithmetic  10 us (5%)
  local copies, waits for them, and re-layouts  3.3 us (2%)
    pallas_call x2, Pallas kernels, gather_rows(): pl.pallas_call(gather_kernel, out_shape=jax.ShapeDtypeStruct((nc, nx, nz)...  75 us
    pallas_call x2, Pallas kernels, scatter_rows(): pl.pallas_call(functools.partial(scatter_kernel, with_core), out_shape=ja...  71.3 us
    dot_general x3, matrix products, project(): jnp.dot(normed, weight, preferred_element_type=jnp.float32)  7.73 us
    dot_general x1, matrix products, local(): jnp.einsum('td,ekdf->ektf', normed2, w_gate_up, preferred_element_type=jn...  6.74 us
    dot_general x1, matrix products, local(): jnp.einsum('etf,efd->td', scaled_sibling, w_down_sibling, preferred_eleme...  4.12 us
  transfers between devices with their start and end apart: 4, of which 1 were waited for; matrix products, arithmetic and copies ran while one was open for 11% of the time, Pallas kernels for 21%

profile of v8, /device:TPU:22, one launch (start us, length us, event | category | flops | bytes accessed | tf_op | source)
XLA Modules:
  0.0 190.5 jit_solution(2902026482719467822)
XLA Ops:
  0.1 1.2 fusion.24
  1.3 0.7 convert_element_type.99
  2.0 1.6 fusion.26.own_ref
  3.6 40.9 %shard_map.136 = bf16[2,4,4,24,2304]{4,3,2,1,0:T(8,128)(2,1)} custom-call(bf16[24,2304]{1,0:T(8,128)(2,1)} %fusion.26.own_ref), custom_call_target="tpu_custom_call" | custom-call | tf_op jit(solution)/shard_map/pallas_call | solution.py:204
  44.6 0.5 collective-permute-start
  45.9 3.2 %convolution_convert_fusion = bf16[768,64]{0,1:T(8,128)(2,1)S(1)} fusion(bf16[768,2304]{1,0:T(8,128)(2,1)} %bitcast.99, bf16[2304,64]{0,1:T(8,128)(2,1)S(1)} %copy-done.4), kind=kOutput, calls=%fused_computation.26 | convolution fusion | flops 226541568 | bytes 3932160 | tf_op jit(solution)/shard_map/dot_general | solution.py:358
  49.3 3.3 %convolution_bitcast_fusion.3 = f32[768,1,64]{0,2,1:T(8,128)S(1)} fusion(bf16[768,2304]{1,0:T(8,128)(2,1)} %bitcast.100, bf16[2304,64]{0,1:T(8,128)(2,1)S(1)} %copy-done.5), kind=kOutput, calls=%fused_computation.24 | convolution fusion | flops 226492416 | bytes 4030464 | tf_op jit(solution)/shard_map/dot_general | solution.py:358
  52.7 1.2 convolution_bitcast_fusion.4
  53.9 0.5 fusion.47
  55.4 0.3 fusion.66
  55.7 1.1 fusion
  56.9 1.5 fusion.1
  58.4 1.5 fusion.6
  60.0 0.2 fusion.15
  60.5 0.4 collective-permute-start.1
  60.9 0.6 fusion.50
  61.5 0.6 collective-permute-done.1
  62.0 1.8 fusion.5
  63.9 33.2 %shard_map.137 = f32[24,2304]{1,0:T(8,128)} custom-call(bf16[4,4,24,2304]{3,2,1,0:T(8,128)(2,1)} %bitcast.104), custom_call_target="tpu_custom_call" | custom-call | tf_op jit(solution)/shard_map/pallas_call | solution.py:294
  97.1 1.1 fusion.28
  98.2 0.7 fusion.30.own_ref
  98.9 34.0 %shard_map.138 = bf16[2,4,4,24,2304]{4,3,2,1,0:T(8,128)(2,1)} custom-call(bf16[24,2304]{1,0:T(8,128)(2,1)} %fusion.30.own_ref), custom_call_target="tpu_custom_call" | custom-call | tf_op jit(solution)/shard_map/pallas_call | solution.py:204
  133.0 3.1 %select_reduce_fusion = (f32[768]{0:T(1024)S(1)}, f32[768]{0:T(1024)S(1)}) fusion(s32[768]{0:T(1024)S(1)} %get-tuple-element.17, s32[768]{0:T(1024)S(1)} %get-tuple-element.18, bf16[768,2304]{1,0:T(8,128)(2,1)} %bitcast.102, bf16[2304,4]{0,1:T(4,128)(2,1)S(1)} %copy-done.8), kind=kOutput, calls=%fused_computation.94 | convolution fusion | flops 14172672 | bytes 3569664 | tf_op jit(solution)/shard_map/dot_general | solution.py:390
  136.9 6.7 %convolution_bitcast_fusion.2 = f32[4,2,768,128]{3,2,1,0:T(8,128)S(1)} fusion(bf16[768,2304,1,1]{1,0,3,2:T(8,128)(2,1)} %bitcast.103, bf16[4,2,2304,128]{3,2,1,0:T(8,128)(2,1)} %param.26), kind=kOutput, calls=%fused_computation.16 | convolution fusion | flops 3623878656 | bytes 11403264 | tf_op jit(solution)/shard_map/td,ekdf->ektf/dot_general | solution.py:394
  143.6 0.2 fusion.65
  143.8 0.4 fusion.12
  144.3 0.5 collective-permute-start.3
  144.8 0.7 copy-done.2
  145.5 1.2 convolution_bitcast_fusion.1
  146.7 4.1 %fusion.4 = bf16[384,2304]{1,0:T(8,128)(2,1)} fusion(f32[384,2304]{1,0:T(8,128)S(1)} %convolution_bitcast_fusion.1, bf16[4,128,2304]{2,1,0:T(8,128)(2,1)} %collective-permute-done, bf16[4,384,128]{2,1,0:T(8,128)(2,1)S(1)} %collective-permute-done.3, f32[4,384]{1,0:T(4,128)S(1)} %bitcast.122), kind=kOutput, calls=%fused_computation.9 | convolution fusion | flops 908328960 | bytes 8067072 | tf_op jit(solution)/shard_map/etf,efd->td/dot_general | solution.py:410
  150.8 38.1 %shard_map.139 = f32[24,2304]{1,0:T(8,128)} custom-call(bf16[4,4,24,2304]{3,2,1,0:T(8,128)(2,1)} %bitcast.105), custom_call_target="tpu_custom_call" | custom-call | tf_op jit(solution)/shard_map/pallas_call | solution.py:294
  188.9 1.6 fusion.31
  (80 shorter events, 3.2 us)
Async XLA Ops:
  0.0 55.7 %copy-start = (bf16[8,1,2048,64]{2,3,1,0:T(8,128)(2,1)S(1)}, bf16[8,1,2048,64]{2,3,1,0:T(8,128)(2,1)}, u32[]{:S(2)}) copy-start(bf16[8,1,2048,64]{2,3,1,0:T(8,128)(2,1)} %param.20) | copy-start | bytes 6291460
  0.0 45.1 %copy-start.11 = (s32[8]{0:T(128)S(1)}, s32[8]{0:T(128)}, u32[]{:S(2)}) copy-start(s32[8]{0:T(128)} %param.22) | copy-start | bytes 100
  0.0 45.6 %copy-start.10 = (bf16[2304]{0:T(1024)(128)(2,1)S(1)}, bf16[2304]{0:T(1024)(128)(2,1)}, u32[]{:S(2)}) copy-start(bf16[2304]{0:T(1024)(128)(2,1)} %param.23) | copy-start | bytes 13828
  0.0 45.6 %copy-start.9 = (s32[768,2]{0,1:T(2,128)S(1)}, s32[768,2]{0,1:T(2,128)}, u32[]{:S(2)}) copy-start(s32[768,2]{0,1:T(2,128)} %param.25) | copy-start | bytes 18436
  0.0 45.9 %copy-start.4 = (bf16[2304,64]{0,1:T(8,128)(2,1)S(1)}, bf16[2304,64]{0,1:T(8,128)(2,1)}, u32[]{:S(2)}) copy-start(bf16[2304,64]{0,1:T(8,128)(2,1)} %param.18) | copy-start | bytes 884740
  0.0 61.4 %collective-permute-start.2 = (bf16[64,2304]{1,0:T(8,128)(2,1)}, bf16[64,2304]{1,0:T(8,128)(2,1)S(1)}, u32[]{:S(2)}, u32[]{:S(2)}) collective-permute-start(bf16[64,2304]{1,0:T(8,128)(2,1)} %param.19), channel_id=1, source_target_pairs={{0,1},{1,0},{2,3},{3,2},{4,5},{5,4},{6,7},{7,6},{8,9},{9,8},{10,11... | collective-permute-start | bytes 884744 | tf_op jit(solution)/shard_map/ppermute | solution.py:380
  44.6 4.8 %copy-start.5 = (bf16[2304,64]{0,1:T(8,128)(2,1)S(1)}, bf16[2304,64]{0,1:T(8,128)(2,1)}, u32[]{:S(2)}) copy-start(bf16[2304,64]{0,1:T(8,128)(2,1)} %param.17) | copy-start | bytes 884740
  44.6 15.8 %collective-permute-start = (bf16[4,128,2304]{2,1,0:T(8,128)(2,1)}, bf16[4,128,2304]{2,1,0:T(8,128)(2,1)}, u32[]{:S(2)}, u32[]{:S(2)}) collective-permute-start(bf16[4,128,2304]{2,1,0:T(8,128)(2,1)} %param.27), channel_id=1, source_target_pairs={{0,1},{1,0},{2,3},{3,2},{4,5},{5,4},{6,7},{7,6},{8,9},{9,8},{10,11... | collective-permute-start | bytes 7077896 | tf_op jit(solution)/shard_map/ppermute | solution.py:353
  49.1 3.6 %copy-start.6 = (bf16[2304,64]{0,1:T(8,128)(2,1)S(1)}, bf16[2304,64]{0,1:T(8,128)(2,1)}, u32[]{:S(2)}) copy-start(bf16[2304,64]{0,1:T(8,128)(2,1)} %param.16) | copy-start | bytes 884740
  49.3 3.4 %copy-start.1 = (bf16[2,4,4,24,2304]{4,3,2,1,0:T(8,128)(2,1)S(1)}, bf16[2,4,4,24,2304]{4,3,2,1,0:T(8,128)(2,1)}, u32[]{:S(2)}) copy-start(bf16[2,4,4,24,2304]{4,3,2,1,0:T(8,128)(2,1)} %shard_map.136) | copy-start | bytes 10616836
  56.8 1.6 copy-start.12
  58.4 2.4 %copy-start.7 = (bf16[64,2304]{1,0:T(8,128)(2,1)S(1)}, bf16[64,2304]{1,0:T(8,128)(2,1)}, u32[]{:S(2)}) copy-start(bf16[64,2304]{1,0:T(8,128)(2,1)} %param.19) | copy-start | bytes 884740
  60.5 1.6 collective-permute-start.1
  61.4 35.6 %copy-start.3 = (bf16[24,2304]{1,0:T(8,128)(2,1)S(1)}, bf16[24,2304]{1,0:T(8,128)(2,1)}, u32[]{:S(2)}) copy-start(bf16[24,2304]{1,0:T(8,128)(2,1)} %param.14) | copy-start | bytes 331780
  63.9 69.1 %copy-start.8 = (bf16[2304,4]{0,1:T(4,128)(2,1)S(1)}, bf16[2304,4]{0,1:T(4,128)(2,1)}, u32[]{:S(2)}) copy-start(bf16[2304,4]{0,1:T(4,128)(2,1)} %param.24) | copy-start | bytes 55300
  143.8 1.7 copy-start.2
  144.3 2.4 %collective-permute-start.3 = (bf16[4,384,128]{2,1,0:T(8,128)(2,1)S(1)}, bf16[4,384,128]{2,1,0:T(8,128)(2,1)S(1)}, u32[]{:S(2)}, u32[]{:S(2)}) collective-permute-start(bf16[4,384,128]{2,1,0:T(8,128)(2,1)S(1)} %dynamic-slice_bitcast_fusion), channel_id=1, source_target_pairs={{0,1},{1,0},{2,3},{3,2},{4,5},{5,4},{6,7},{7,6},{8,9},{9,8},{10,11... | collective-permute-start | bytes 1179656 | tf_op jit(solution)/shard_map/ppermute | solution.py:399

commit v9 on v8

--- a/solution.py
+++ b/solution.py
@@ -173,7 +173,7 @@
     remote(hi, hi, send_sem.at[3], recv_sem.at[3], right).wait_recv()
 
 
-def gather_kernel(own_ref, out_ref, send_sem, recv_sem, local_sem):
+def gather_kernel(with_core, own_ref, out_ref, send_sem, recv_sem, local_sem):
     x = lax.axis_index("x")
     z = lax.axis_index("zh")
     c = lax.axis_index("core")
@@ -181,29 +181,36 @@
     _, _, x_right, x_left = ring_peers("x")
     _, _, sibling, _ = ring_peers("core")
     barrier = pltpu.get_barrier_semaphore()
-    for peer in (z_right, z_left, x_right, x_left, sibling):
+    peers = (z_right, z_left, x_right, x_left) + ((sibling,) if with_core else ())
+    for peer in peers:
         pl.semaphore_signal(barrier, 1, device_id=peer, device_id_type=pl.DeviceIdType.MESH)
-    pl.semaphore_wait(barrier, 5)
-    local = pltpu.make_async_copy(own_ref, out_ref.at[c, x, z], local_sem.at[0])
+    pl.semaphore_wait(barrier, len(peers))
+
+    def view(*index):
+        return out_ref.at[((c,) if with_core else ()) + index]
+
+    local = pltpu.make_async_copy(own_ref, view(x, z), local_sem.at[0])
     local.start()
     sent = []
-    ring_gather(lambda i: out_ref.at[c, x, i], own_ref, "zh", send_sem.at[0:4], recv_sem.at[0:4], sent)
+    ring_gather(lambda i: view(x, i), own_ref, "zh", send_sem.at[0:4], recv_sem.at[0:4], sent)
     local.wait()
-    ring_gather(lambda i: out_ref.at[c, i], out_ref.at[c, x], "x", send_sem.at[4:8], recv_sem.at[4:8], sent)
-    copy = remote(out_ref.at[c], out_ref.at[c], send_sem.at[8], recv_sem.at[8], sibling)
-    copy.start()
-    sent.append(copy)
-    remote(out_ref.at[c], out_ref.at[1 - c], send_sem.at[8], recv_sem.at[8], sibling).wait_recv()
+    ring_gather(lambda i: view(i), view(x), "x", send_sem.at[4:8], recv_sem.at[4:8], sent)
+    if with_core:
+        copy = remote(out_ref.at[c], out_ref.at[c], send_sem.at[8], recv_sem.at[8], sibling)
+        copy.start()
+        sent.append(copy)
+        remote(out_ref.at[c], out_ref.at[1 - c], send_sem.at[8], recv_sem.at[8], sibling).wait_recv()
     for copy in sent:
         copy.wait_send()
 
 
-def gather_rows(rows):
+def gather_rows(rows, with_core=True):
     nx, nz, nc = SIZE["x"], SIZE["zh"], SIZE["core"]
     links = 9
+    lead = (nc, nx, nz) if with_core else (nx, nz)
     out = pl.pallas_call(
-        gather_kernel,
-        out_shape=jax.ShapeDtypeStruct((nc, nx, nz) + rows.shape, rows.dtype),
+        functools.partial(gather_kernel, with_core),
+        out_shape=jax.ShapeDtypeStruct(lead + rows.shape, rows.dtype),
         in_specs=[pl.BlockSpec(memory_space=pltpu.VMEM)],
         out_specs=pl.BlockSpec(memory_space=pltpu.VMEM),
         scratch_shapes=[
@@ -211,9 +218,11 @@
             pltpu.SemaphoreType.DMA((links,)),
             pltpu.SemaphoreType.DMA((1,)),
         ],
-        compiler_params=pltpu.CompilerParams(collective_id=0, has_side_effects=True),
+        compiler_params=pltpu.CompilerParams(
+            collective_id=0 if with_core else 3, has_side_effects=True
+        ),
     )(rows)
-    return out.reshape((nc * nx * nz * rows.shape[0],) + rows.shape[1:])
+    return out.reshape((-1,) + rows.shape[1:])
 
 
 def ring_scatter(chunk, axis, buffers, send_sem, recv_sem, sent):
@@ -348,34 +357,39 @@
     width = hidden_in.shape[1]
     head_dev = cache_k.shape[1]
     n_experts = w_gate_up.shape[0]
-    normed = gather_rows(rms_scale(hidden_in, attn_gain))
-    w_down_later, _ = lax.optimization_barrier((w_down, normed))
-    w_down_sibling = lax.ppermute(w_down_later, "core", [(0, 1), (1, 0)])
+    core = lax.axis_index("core")
+    swap = [(0, 1), (1, 0)]
+    w_qkv = jnp.concatenate([w_query, w_key, w_value], axis=1)
+    w_qkv_sibling = lax.ppermute(w_qkv, "core", swap)
+    normed_half = gather_rows(rms_scale(hidden_in, attn_gain), with_core=False)
+    w_down_later, _ = lax.optimization_barrier((w_down, normed_half))
+    w_down_sibling = lax.ppermute(w_down_later, "core", swap)
+    qkv_mine = jnp.dot(normed_half, w_qkv, preferred_element_type=jnp.float32)
+    qkv_for_sibling = jnp.dot(normed_half, w_qkv_sibling, preferred_element_type=jnp.float32)
+    qkv_other = lax.ppermute(qkv_for_sibling, "core", swap)
+    qkv = jnp.where(
+        core == 0,
+        jnp.concatenate([qkv_mine, qkv_other], axis=0),
+        jnp.concatenate([qkv_other, qkv_mine], axis=0),
+    ).reshape(TOKENS, 3, head_dev, HDIM)
     positions = (cache_len[:, None] + jnp.arange(NEW, dtype=jnp.int32)[None, :]).reshape(-1)
     positions = from_request_order(positions)
-
-    def project(weight):
-        return jnp.dot(normed, weight, preferred_element_type=jnp.float32).reshape(
-            TOKENS, head_dev, HDIM
-        )
 
     def by_request(values):
         values = to_request_order(values)
         return values.reshape(REQS, NEW, head_dev, HDIM).transpose(0, 2, 1, 3)
 
-    query = rotate(project(w_query), positions).astype(jnp.bfloat16)
-    key_new = rotate(project(w_key), positions).astype(jnp.bfloat16)
-    value_new = project(w_value).astype(jnp.bfloat16)
+    query = rotate(qkv[:, 0], positions).astype(jnp.bfloat16)
+    key_new = rotate(qkv[:, 1], positions).astype(jnp.bfloat16)
+    value_new = qkv[:, 2].astype(jnp.bfloat16)
     heads_out = attend(
         by_request(query), by_request(key_new), by_request(value_new), cache_k, cache_v, cache_len
     )
     heads_flat = from_request_order(heads_out.transpose(0, 2, 1, 3).reshape(TOKENS, head_dev * HDIM))
     heads_flat, w_down_sibling = lax.optimization_barrier((heads_flat, w_down_sibling))
-    core = lax.axis_index("core")
     by_core = heads_flat.reshape(SIZE["core"], TOKENS // SIZE["core"], head_dev * HDIM)
     mine = lax.dynamic_index_in_dim(by_core, core, axis=0, keepdims=False)
     theirs = lax.dynamic_index_in_dim(by_core, 1 - core, axis=0, keepdims=False)
-    swap = [(0, 1), (1, 0)]
     from_sibling = lax.ppermute(theirs, "core", swap)
     w_out_sibling = lax.ppermute(w_out, "core", swap)
     attn = scatter_rows(

time: 191 us -> 192 us (level)
  local copies, waits for them, and re-layouts: 3.3 us -> 8.64 us
  Pallas kernels: 146 us -> 143 us
    unnamed x28 -> x22, local copies, waits for them, and re-layouts: 0.77 us -> 4.37 us
    pallas_call x2, Pallas kernels: 75 us -> 71.4 us  [gather_rows(): pl.pallas_call(functools.partial(gather_kernel, with_core), out_shape=jax...]
    dot_general x3 -> x2, matrix products: 7.73 us -> 5.59 us  [the longest x1 3.15 us: local(): jnp.dot(normed_half, w_qkv_sibling, preferred_element_type=jnp.float32)]
  transfers between devices with their start and end apart: 4 -> 6, of which waited for: 1 -> 1; matrix products, arithmetic and copies ran while one was open for 11% -> 9% of each run, Pallas kernels for 21% -> 19%
where the time goes in v9:
time: 192 us; the launch traced here: 191 us
  Pallas kernels  143 us (74%)
  matrix products  27.2 us (14%)
  other arithmetic  9.91 us (5%)
  local copies, waits for them, and re-layouts  8.64 us (4%)
    pallas_call x2, Pallas kernels, scatter_rows(): pl.pallas_call(functools.partial(scatter_kernel, with_core), out_shape=ja...  71.5 us
    pallas_call x2, Pallas kernels, gather_rows(): pl.pallas_call(functools.partial(gather_kernel, with_core), out_shape=jax...  71.4 us
    dot_general x1, matrix products, local(): jnp.einsum('td,ekdf->ektf', normed2, w_gate_up, preferred_element_type=jn...  6.74 us
    unnamed x22, local copies, waits for them, and re-layouts  4.37 us
    dot_general x1, matrix products, local(): jnp.einsum('etf,efd->td', scaled_sibling, w_down_sibling, preferred_eleme...  4.12 us
  transfers between devices with their start and end apart: 6, of which 1 were waited for; matrix products, arithmetic and copies ran while one was open for 9% of the time, Pallas kernels for 19%

profile of v9, /device:TPU:22, one launch (start us, length us, event | category | flops | bytes accessed | tf_op | source)
XLA Modules:
  0.0 191.4 jit_solution(11393231021216478341)
XLA Ops:
  0.0 1.8 constant_dynamic-update-slice_fusion.2
  1.9 1.7 constant_dynamic-update-slice_fusion.1
  3.6 1.7 constant_dynamic-update-slice_fusion
  5.3 0.7 convert_element_type.108
  6.0 1.0 fusion.24
  7.0 1.6 fusion.26.own_ref
  8.6 37.0 %shard_map.136 = bf16[4,4,24,2304]{3,2,1,0:T(8,128)(2,1)} custom-call(bf16[24,2304]{1,0:T(8,128)(2,1)} %fusion.26.own_ref), custom_call_target="tpu_custom_call" | custom-call | tf_op jit(solution)/shard_map/pallas_call | solution.py:211
  45.7 0.5 collective-permute-start.4
  47.0 3.2 %fusion.67 = f32[384,192]{0,1:T(8,128)} fusion(bf16[384,2304]{1,0:T(8,128)(2,1)} %bitcast.113, bf16[2304,192]{0,1:T(8,128)(2,1)} %collective-permute-done), kind=kOutput, calls=%fused_computation.121 | convolution fusion | flops 339738624 | bytes 2949120 | tf_op jit(solution)/shard_map/dot_general | solution.py:368
  50.4 2.4 %convolution_bitcast_fusion.3 = f32[384,3,1,64]{0,3,1,2:T(8,128)S(1)} fusion(bf16[384,2304,1]{1,0,2:T(8,128)(2,1)} %bitcast.114, bf16[3,64,2304]{2,1,0:T(8,128)(2,1)} %bitcast.3), kind=kOutput, calls=%fused_computation.21 | convolution fusion | flops 339738624 | bytes 2949120 | tf_op jit(solution)/shard_map/dot_general | solution.py:367
  53.0 0.5 fusion.47
  54.6 0.3 fusion.66
  54.9 1.1 fusion
  56.1 1.5 fusion.1
  57.7 1.5 fusion.6
  59.7 0.7 collective-permute-start.3
  60.4 0.6 fusion.50
  61.0 0.3 collective-permute-done.3
  61.3 2.8 %fusion.5 = bf16[384,2304]{1,0:T(8,128)(2,1)} fusion(f32[384,2304]{1,0:T(8,128)S(1)} %fusion.50, bf16[384,64]{1,0:T(8,128)(2,1)S(1)} %collective-permute-done.3, bf16[64,2304]{1,0:T(8,128)(2,1)} %collective-permute-done.4), kind=kOutput, calls=%fused_computation.10 | convolution fusion | flops 115015680 | bytes 5652480 | tf_op jit(solution)/shard_map/dot_general | solution.py:398
  64.1 33.4 %shard_map.137 = f32[24,2304]{1,0:T(8,128)} custom-call(bf16[4,4,24,2304]{3,2,1,0:T(8,128)(2,1)} %bitcast.108), custom_call_target="tpu_custom_call" | custom-call | tf_op jit(solution)/shard_map/pallas_call | solution.py:303
  97.5 1.1 fusion.28
  98.6 0.7 fusion.30.own_ref
  99.3 34.4 %shard_map.138 = bf16[2,4,4,24,2304]{4,3,2,1,0:T(8,128)(2,1)} custom-call(bf16[24,2304]{1,0:T(8,128)(2,1)} %fusion.30.own_ref), custom_call_target="tpu_custom_call" | custom-call | tf_op jit(solution)/shard_map/pallas_call | solution.py:211
  133.8 3.1 %select_reduce_fusion = (f32[768]{0:T(1024)S(1)}, f32[768]{0:T(1024)S(1)}) fusion(s32[768]{0:T(1024)S(1)} %get-tuple-element.17, s32[768]{0:T(1024)S(1)} %get-tuple-element.18, bf16[768,2304]{1,0:T(8,128)(2,1)} %bitcast.106, bf16[2304,4]{0,1:T(4,128)(2,1)S(1)} %copy-done.4), kind=kOutput, calls=%fused_computation.96 | convolution fusion | flops 14172672 | bytes 3569664 | tf_op jit(solution)/shard_map/dot_general | solution.py:404
  137.7 6.7 %convolution_bitcast_fusion.2 = f32[4,2,768,128]{3,2,1,0:T(8,128)S(1)} fusion(bf16[768,2304,1,1]{1,0,3,2:T(8,128)(2,1)} %bitcast.107, bf16[4,2,2304,128]{3,2,1,0:T(8,128)(2,1)} %param.26), kind=kOutput, calls=%fused_computation.16 | convolution fusion | flops 3623878656 | bytes 11403264 | tf_op jit(solution)/shard_map/td,ekdf->ektf/dot_general | solution.py:408
  144.7 0.4 fusion.12
  145.1 0.5 collective-permute-start.5
  145.6 0.7 copy-done.1
  146.3 1.2 convolution_bitcast_fusion.1
  147.5 4.1 %fusion.4 = bf16[384,2304]{1,0:T(8,128)(2,1)} fusion(f32[384,2304]{1,0:T(8,128)S(1)} %convolution_bitcast_fusion.1, bf16[4,128,2304]{2,1,0:T(8,128)(2,1)} %collective-permute-done.2, bf16[4,384,128]{2,1,0:T(8,128)(2,1)S(1)} %collective-permute-done.5, f32[4,384]{1,0:T(4,128)S(1)} %bitcast.130), kind=kOutput, calls=%fused_computation.9 | convolution fusion | flops 908328960 | bytes 8067072 | tf_op jit(solution)/shard_map/etf,efd->td/dot_general | solution.py:424
  151.7 38.1 %shard_map.139 = f32[24,2304]{1,0:T(8,128)} custom-call(bf16[4,4,24,2304]{3,2,1,0:T(8,128)(2,1)} %bitcast.109), custom_call_target="tpu_custom_call" | custom-call | tf_op jit(solution)/shard_map/pallas_call | solution.py:303
  189.8 1.6 fusion.31
  (82 shorter events, 3.9 us)
Async XLA Ops:
  0.0 54.9 %copy-start = (bf16[8,1,2048,64]{2,3,1,0:T(8,128)(2,1)S(1)}, bf16[8,1,2048,64]{2,3,1,0:T(8,128)(2,1)}, u32[]{:S(2)}) copy-start(bf16[8,1,2048,64]{2,3,1,0:T(8,128)(2,1)} %param.20) | copy-start | bytes 6291460
  0.0 45.7 %copy-start.3 = (bf16[64,2304]{1,0:T(8,128)(2,1)S(1)}, bf16[64,2304]{1,0:T(8,128)(2,1)}, u32[]{:S(2)}) copy-start(bf16[64,2304]{1,0:T(8,128)(2,1)} %param.19) | copy-start | bytes 884740
  0.0 46.2 %copy-start.5 = (s32[768,2]{0,1:T(2,128)S(1)}, s32[768,2]{0,1:T(2,128)}, u32[]{:S(2)}) copy-start(s32[768,2]{0,1:T(2,128)} %param.25) | copy-start | bytes 18436
  0.0 46.5 %copy-start.7 = (s32[8]{0:T(128)S(1)}, s32[8]{0:T(128)}, u32[]{:S(2)}) copy-start(s32[8]{0:T(128)} %param.22) | copy-start | bytes 100
  5.3 45.1 %copy-start.6 = (bf16[2304]{0:T(1024)(128)(2,1)S(1)}, bf16[2304]{0:T(1024)(128)(2,1)}, u32[]{:S(2)}) copy-start(bf16[2304]{0:T(1024)(128)(2,1)} %param.23) | copy-start | bytes 13828
  5.3 41.7 %collective-permute-start = (bf16[2304,192]{0,1:T(8,128)(2,1)}, bf16[2304,192]{0,1:T(8,128)(2,1)}, u32[]{:S(2)}, u32[]{:S(2)}) collective-permute-start(bf16[2304,192]{0,1:T(8,128)(2,1)} %constant_dynamic-update-slice_fusion), channel_id=1, source_target_pairs={{0,1},{1,0},{2,3},{3,2},{4,5},{5,4},{6,7},{7,6},{8,9},{9,8},{10,11... | collective-permute-start | bytes 2654216 | tf_op jit(solution)/shard_map/ppermute | solution.py:363
  45.6 14.0 %collective-permute-start.2 = (bf16[4,128,2304]{2,1,0:T(8,128)(2,1)}, bf16[4,128,2304]{2,1,0:T(8,128)(2,1)}, u32[]{:S(2)}, u32[]{:S(2)}) collective-permute-start(bf16[4,128,2304]{2,1,0:T(8,128)(2,1)} %param.27), channel_id=1, source_target_pairs={{0,1},{1,0},{2,3},{3,2},{4,5},{5,4},{6,7},{7,6},{8,9},{9,8},{10,11... | collective-permute-start | bytes 7077896 | tf_op jit(solution)/shard_map/ppermute | solution.py:366
  45.7 15.2 %collective-permute-start.4 = (bf16[64,2304]{1,0:T(8,128)(2,1)S(1)}, bf16[64,2304]{1,0:T(8,128)(2,1)}, u32[]{:S(2)}, u32[]{:S(2)}) collective-permute-start(bf16[64,2304]{1,0:T(8,128)(2,1)S(1)} %copy-done.3), channel_id=1, source_target_pairs={{0,1},{1,0},{2,3},{3,2},{4,5},{5,4},{6,7},{7,6},{8,9},{9,8},{10,11... | collective-permute-start | bytes 884744 | tf_op jit(solution)/shard_map/ppermute | solution.py:394
  50.1 2.7 %collective-permute-start.1 = (f32[384,192]{0,1:T(8,128)}, f32[384,192]{0,1:T(8,128)S(1)}, u32[]{:S(2)}, u32[]{:S(2)}) collective-permute-start(f32[384,192]{0,1:T(8,128)} %fusion.67), channel_id=1, source_target_pairs={{0,1},{1,0},{2,3},{3,2},{4,5},{5,4},{6,7},{7,6},{8,9},{9,8},{10,11... | collective-permute-start | bytes 884744 | tf_op jit(solution)/shard_map/ppermute | solution.py:369
  56.1 1.6 copy-start.8
  59.7 1.6 collective-permute-start.3
  61.0 36.5 %copy-start.2 = (bf16[24,2304]{1,0:T(8,128)(2,1)S(1)}, bf16[24,2304]{1,0:T(8,128)(2,1)}, u32[]{:S(2)}) copy-start(bf16[24,2304]{1,0:T(8,128)(2,1)} %param.14) | copy-start | bytes 331780
  64.1 69.7 %copy-start.4 = (bf16[2304,4]{0,1:T(4,128)(2,1)S(1)}, bf16[2304,4]{0,1:T(4,128)(2,1)}, u32[]{:S(2)}) copy-start(bf16[2304,4]{0,1:T(4,128)(2,1)} %param.24) | copy-start | bytes 55300
  144.6 1.7 copy-start.1
  145.1 2.4 %collective-permute-start.5 = (bf16[4,384,128]{2,1,0:T(8,128)(2,1)S(1)}, bf16[4,384,128]{2,1,0:T(8,128)(2,1)S(1)}, u32[]{:S(2)}, u32[]{:S(2)}) collective-permute-start(bf16[4,384,128]{2,1,0:T(8,128)(2,1)S(1)} %dynamic-slice_bitcast_fusion), channel_id=1, source_target_pairs={{0,1},{1,0},{2,3},{3,2},{4,5},{5,4},{6,7},{7,6},{8,9},{9,8},{10,11... | collective-permute-start | bytes 1179656 | tf_op jit(solution)/shard_map/ppermute | solution.py:413

commit v10 on v9

--- a/solution.py
+++ b/solution.py
@@ -359,19 +359,21 @@
     n_experts = w_gate_up.shape[0]
     core = lax.axis_index("core")
     swap = [(0, 1), (1, 0)]
-    w_qkv = jnp.concatenate([w_query, w_key, w_value], axis=1)
+    w_qkv = jnp.stack([w_query, w_key, w_value])
     w_qkv_sibling = lax.ppermute(w_qkv, "core", swap)
     normed_half = gather_rows(rms_scale(hidden_in, attn_gain), with_core=False)
     w_down_later, _ = lax.optimization_barrier((w_down, normed_half))
     w_down_sibling = lax.ppermute(w_down_later, "core", swap)
-    qkv_mine = jnp.dot(normed_half, w_qkv, preferred_element_type=jnp.float32)
-    qkv_for_sibling = jnp.dot(normed_half, w_qkv_sibling, preferred_element_type=jnp.float32)
+    qkv_mine = jnp.einsum("td,kdf->ktf", normed_half, w_qkv, preferred_element_type=jnp.float32)
+    qkv_for_sibling = jnp.einsum(
+        "td,kdf->ktf", normed_half, w_qkv_sibling, preferred_element_type=jnp.float32
+    )
     qkv_other = lax.ppermute(qkv_for_sibling, "core", swap)
     qkv = jnp.where(
         core == 0,
-        jnp.concatenate([qkv_mine, qkv_other], axis=0),
-        jnp.concatenate([qkv_other, qkv_mine], axis=0),
-    ).reshape(TOKENS, 3, head_dev, HDIM)
+        jnp.concatenate([qkv_mine, qkv_other], axis=1),
+        jnp.concatenate([qkv_other, qkv_mine], axis=1),
+    ).reshape(3, TOKENS, head_dev, HDIM)
     positions = (cache_len[:, None] + jnp.arange(NEW, dtype=jnp.int32)[None, :]).reshape(-1)
     positions = from_request_order(positions)
 
@@ -379,9 +381,9 @@
         values = to_request_order(values)
         return values.reshape(REQS, NEW, head_dev, HDIM).transpose(0, 2, 1, 3)
 
-    query = rotate(qkv[:, 0], positions).astype(jnp.bfloat16)
-    key_new = rotate(qkv[:, 1], positions).astype(jnp.bfloat16)
-    value_new = qkv[:, 2].astype(jnp.bfloat16)
+    query = rotate(qkv[0], positions).astype(jnp.bfloat16)
+    key_new = rotate(qkv[1], positions).astype(jnp.bfloat16)
+    value_new = qkv[2].astype(jnp.bfloat16)
     heads_out = attend(
         by_request(query), by_request(key_new), by_request(value_new), cache_k, cache_v, cache_len
     )

time: 192 us -> 189 us (0.984)
  local copies, waits for them, and re-layouts: 8.64 us -> 4.08 us
  other arithmetic: 9.91 us -> 12.2 us
    unnamed x22 -> x18, local copies, waits for them, and re-layouts: 4.37 us -> 0.82 us
    another operation x1 -> x2, other arithmetic: 0.46 us -> 2.78 us  [the longest x1 2.32 us: local(): w_qkv = jnp.stack([w_query, w_key, w_value])]
  transfers between devices with their start and end apart: 6 -> 6, of which waited for: 1 -> 1; matrix products, arithmetic and copies ran while one was open for 9% -> 10% of each run, Pallas kernels for 19% -> 20%
where the time goes in v10:
time: 189 us
  Pallas kernels  144 us (76%)
  matrix products  26.1 us (14%)
  other arithmetic  12.2 us (6%)
  local copies, waits for them, and re-layouts  4.08 us (2%)
    pallas_call x2, Pallas kernels, scatter_rows(): pl.pallas_call(functools.partial(scatter_kernel, with_core), out_shape=ja...  72 us
    pallas_call x2, Pallas kernels, gather_rows(): pl.pallas_call(functools.partial(gather_kernel, with_core), out_shape=jax...  71.7 us
    dot_general x1, matrix products, local(): jnp.einsum('td,ekdf->ektf', normed2, w_gate_up, preferred_element_type=jn...  6.74 us
    dot_general x1, matrix products, local(): jnp.einsum('etf,efd->td', scaled_sibling, w_down_sibling, preferred_eleme...  4.12 us
  transfers between devices with their start and end apart: 6, of which 1 were waited for; matrix products, arithmetic and copies ran while one was open for 10% of the time, Pallas kernels for 20%

profile of v10, /device:TPU:22, one launch (start us, length us, event | category | flops | bytes accessed | tf_op | source)
XLA Modules:
  0.0 188.6 jit_solution(1033085526053401819)
XLA Ops:
  0.0 2.3 %pad_maximum_fusion = bf16[3,2304,64]{1,2,0:T(8,128)(2,1)} fusion(bf16[1,2304,64]{1,2,0:T(8,128)(2,1)} %bitcast.124, bf16[1,2304,64]{1,2,0:T(8,128)(2,1)} %bitcast.126, bf16[1,2304,64]{1,2,0:T(8,128)(2,1)} %bitcast.128), kind=kLoop, calls=%fused_computation.26 | loop fusion | flops 884736 | bytes 1769472 | tf_op jit(solution)/shard_map/stack | solution.py:362
  2.3 0.5 collective-permute-start.2
  2.9 0.8 reshape.465
  3.8 0.7 convert_element_type.108
  4.5 1.0 fusion.24
  5.5 1.6 fusion.26.own_ref
  7.2 37.0 %shard_map.136 = bf16[4,4,24,2304]{3,2,1,0:T(8,128)(2,1)} custom-call(bf16[24,2304]{1,0:T(8,128)(2,1)} %fusion.26.own_ref), custom_call_target="tpu_custom_call" | custom-call | tf_op jit(solution)/shard_map/pallas_call | solution.py:211
  44.7 2.9 %convolution_bitcast_fusion.3 = f32[3,384,64]{1,2,0:T(8,128)} fusion(bf16[3,2304,64]{1,2,0:T(8,128)(2,1)S(1)} %collective-permute-done, bf16[384,2304,1]{1,0,2:T(8,128)(2,1)} %bitcast.107), kind=kOutput, calls=%fused_computation.21 | convolution fusion | flops 339738624 | bytes 2949120 | tf_op jit(solution)/shard_map/td,kdf->ktf/dot_general | solution.py:368
  47.7 2.5 %convolution_bitcast_fusion.4 = f32[3,384,64]{1,2,0:T(8,128)S(1)} fusion(bf16[384,2304,1]{1,0,2:T(8,128)(2,1)} %bitcast.108, bf16[1,2304,64]{1,2,0:T(8,128)(2,1)} %bitcast.125, bf16[1,2304,64]{1,2,0:T(8,128)(2,1)} %bitcast.127, bf16[1,2304,64]{1,2,0:T(8,128)(2,1)} %bitcast.129), kind=kOutput, calls=%fused_computation.22 | convolution fusion | flops 340623360 | bytes 2949120 | tf_op jit(solution)/shard_map/td,kdf->ktf/dot_general | solution.py:367
  50.4 0.5 fusion.47
  52.0 0.3 fusion.66
  52.3 1.1 fusion
  53.5 1.5 fusion.1
  55.1 1.5 fusion.6
  56.6 0.2 fusion.15
  57.1 0.8 collective-permute-start.3
  57.9 0.6 fusion.50
  58.5 0.3 collective-permute-done.3
  58.8 1.8 fusion.5
  60.6 33.2 %shard_map.137 = f32[24,2304]{1,0:T(8,128)} custom-call(bf16[4,4,24,2304]{3,2,1,0:T(8,128)(2,1)} %bitcast.109), custom_call_target="tpu_custom_call" | custom-call | tf_op jit(solution)/shard_map/pallas_call | solution.py:303
  93.9 1.1 fusion.28
  95.0 0.7 fusion.30.own_ref
  95.7 34.7 %shard_map.138 = bf16[2,4,4,24,2304]{4,3,2,1,0:T(8,128)(2,1)} custom-call(bf16[24,2304]{1,0:T(8,128)(2,1)} %fusion.30.own_ref), custom_call_target="tpu_custom_call" | custom-call | tf_op jit(solution)/shard_map/pallas_call | solution.py:211
  130.4 3.1 %select_reduce_fusion = (f32[768]{0:T(1024)S(1)}, f32[768]{0:T(1024)S(1)}) fusion(s32[768]{0:T(1024)S(1)} %get-tuple-element.17, s32[768]{0:T(1024)S(1)} %get-tuple-element.18, bf16[768,2304]{1,0:T(8,128)(2,1)} %bitcast.105, bf16[2304,4]{0,1:T(4,128)(2,1)S(1)} %copy-done.4), kind=kOutput, calls=%fused_computation.98 | convolution fusion | flops 14172672 | bytes 3569664 | tf_op jit(solution)/shard_map/dot_general | solution.py:406
  134.3 6.7 %convolution_bitcast_fusion.2 = f32[4,2,768,128]{3,2,1,0:T(8,128)S(1)} fusion(bf16[768,2304,1,1]{1,0,3,2:T(8,128)(2,1)} %bitcast.106, bf16[4,2,2304,128]{3,2,1,0:T(8,128)(2,1)} %param.26), kind=kOutput, calls=%fused_computation.16 | convolution fusion | flops 3623878656 | bytes 11403264 | tf_op jit(solution)/shard_map/td,ekdf->ektf/dot_general | solution.py:410
  141.3 0.4 fusion.12
  141.8 0.5 collective-permute-start.5
  142.3 0.7 copy-done.1
  143.0 1.2 convolution_bitcast_fusion.1
  144.2 4.1 %fusion.4 = bf16[384,2304]{1,0:T(8,128)(2,1)} fusion(f32[384,2304]{1,0:T(8,128)S(1)} %convolution_bitcast_fusion.1, bf16[4,128,2304]{2,1,0:T(8,128)(2,1)} %collective-permute-done.2, bf16[4,384,128]{2,1,0:T(8,128)(2,1)S(1)} %collective-permute-done.5, f32[4,384]{1,0:T(4,128)S(1)} %bitcast.133), kind=kOutput, calls=%fused_computation.9 | convolution fusion | flops 908328960 | bytes 8067072 | tf_op jit(solution)/shard_map/etf,efd->td/dot_general | solution.py:426
  148.3 38.7 %shard_map.139 = f32[24,2304]{1,0:T(8,128)} custom-call(bf16[4,4,24,2304]{3,2,1,0:T(8,128)(2,1)} %bitcast.110), custom_call_target="tpu_custom_call" | custom-call | tf_op jit(solution)/shard_map/pallas_call | solution.py:303
  187.0 1.6 fusion.31
  (77 shorter events, 3.4 us)
Async XLA Ops:
  0.0 52.3 %copy-start = (bf16[8,1,2048,64]{2,3,1,0:T(8,128)(2,1)S(1)}, bf16[8,1,2048,64]{2,3,1,0:T(8,128)(2,1)}, u32[]{:S(2)}) copy-start(bf16[8,1,2048,64]{2,3,1,0:T(8,128)(2,1)} %param.20) | copy-start | bytes 6291460
  0.0 44.2 %copy-start.6 = (s32[8]{0:T(128)S(1)}, s32[8]{0:T(128)}, u32[]{:S(2)}) copy-start(s32[8]{0:T(128)} %param.22) | copy-start | bytes 100
  2.3 45.4 %copy-start.5 = (bf16[2304]{0:T(1024)(128)(2,1)S(1)}, bf16[2304]{0:T(1024)(128)(2,1)}, u32[]{:S(2)}) copy-start(bf16[2304]{0:T(1024)(128)(2,1)} %param.23) | copy-start | bytes 13828
  2.3 42.3 %collective-permute-start = (bf16[3,2304,64]{1,2,0:T(8,128)(2,1)}, bf16[3,2304,64]{1,2,0:T(8,128)(2,1)S(1)}, u32[]{:S(2)}, u32[]{:S(2)}) collective-permute-start(bf16[3,2304,64]{1,2,0:T(8,128)(2,1)} %pad_maximum_fusion), channel_id=1, source_target_pairs={{0,1},{1,0},{2,3},{3,2},{4,5},{5,4},{6,7},{7,6},{8,9},{9,8},{10,11... | collective-permute-start | bytes 2654216 | tf_op jit(solution)/shard_map/ppermute | solution.py:363
  2.3 54.7 %collective-permute-start.2 = (bf16[4,128,2304]{2,1,0:T(8,128)(2,1)}, bf16[4,128,2304]{2,1,0:T(8,128)(2,1)}, u32[]{:S(2)}, u32[]{:S(2)}) collective-permute-start(bf16[4,128,2304]{2,1,0:T(8,128)(2,1)} %param.27), channel_id=1, source_target_pairs={{0,1},{1,0},{2,3},{3,2},{4,5},{5,4},{6,7},{7,6},{8,9},{9,8},{10,11... | collective-permute-start | bytes 7077896 | tf_op jit(solution)/shard_map/ppermute | solution.py:366
  2.8 55.7 %collective-permute-start.4 = (bf16[64,2304]{1,0:T(8,128)(2,1)}, bf16[64,2304]{1,0:T(8,128)(2,1)S(1)}, u32[]{:S(2)}, u32[]{:S(2)}) collective-permute-start(bf16[64,2304]{1,0:T(8,128)(2,1)} %param.19), channel_id=1, source_target_pairs={{0,1},{1,0},{2,3},{3,2},{4,5},{5,4},{6,7},{7,6},{8,9},{9,8},{10,11... | collective-permute-start | bytes 884744 | tf_op jit(solution)/shard_map/ppermute | solution.py:396
  47.6 2.7 %collective-permute-start.1 = (f32[3,384,64]{1,2,0:T(8,128)}, f32[3,384,64]{1,2,0:T(8,128)S(1)}, u32[]{:S(2)}, u32[]{:S(2)}) collective-permute-start(f32[3,384,64]{1,2,0:T(8,128)} %convolution_bitcast_fusion.3), channel_id=1, source_target_pairs={{0,1},{1,0},{2,3},{3,2},{4,5},{5,4},{6,7},{7,6},{8,9},{9,8},{10,11... | collective-permute-start | bytes 884744 | tf_op jit(solution)/shard_map/ppermute | solution.py:371
  53.5 1.6 copy-start.7
  55.1 2.8 %copy-start.3 = (bf16[64,2304]{1,0:T(8,128)(2,1)S(1)}, bf16[64,2304]{1,0:T(8,128)(2,1)}, u32[]{:S(2)}) copy-start(bf16[64,2304]{1,0:T(8,128)(2,1)} %param.19) | copy-start | bytes 884740
  57.1 1.7 collective-permute-start.3
  58.5 35.4 %copy-start.2 = (bf16[24,2304]{1,0:T(8,128)(2,1)S(1)}, bf16[24,2304]{1,0:T(8,128)(2,1)}, u32[]{:S(2)}) copy-start(bf16[24,2304]{1,0:T(8,128)(2,1)} %param.14) | copy-start | bytes 331780
  60.6 69.8 %copy-start.4 = (bf16[2304,4]{0,1:T(4,128)(2,1)S(1)}, bf16[2304,4]{0,1:T(4,128)(2,1)}, u32[]{:S(2)}) copy-start(bf16[2304,4]{0,1:T(4,128)(2,1)} %param.24) | copy-start | bytes 55300
  141.3 1.7 copy-start.1
  141.8 2.4 %collective-permute-start.5 = (bf16[4,384,128]{2,1,0:T(8,128)(2,1)S(1)}, bf16[4,384,128]{2,1,0:T(8,128)(2,1)S(1)}, u32[]{:S(2)}, u32[]{:S(2)}) collective-permute-start(bf16[4,384,128]{2,1,0:T(8,128)(2,1)S(1)} %dynamic-slice_bitcast_fusion), channel_id=1, source_target_pairs={{0,1},{1,0},{2,3},{3,2},{4,5},{5,4},{6,7},{7,6},{8,9},{9,8},{10,11... | collective-permute-start | bytes 1179656 | tf_op jit(solution)/shard_map/ppermute | solution.py:415

commit v11 on v10

--- a/solution.py
+++ b/solution.py
@@ -361,6 +361,7 @@
     swap = [(0, 1), (1, 0)]
     w_qkv = jnp.stack([w_query, w_key, w_value])
     w_qkv_sibling = lax.ppermute(w_qkv, "core", swap)
+    w_gate_up_sibling = lax.ppermute(w_gate_up, "core", swap)
     normed_half = gather_rows(rms_scale(hidden_in, attn_gain), with_core=False)
     w_down_later, _ = lax.optimization_barrier((w_down, normed_half))
     w_down_sibling = lax.ppermute(w_down_later, "core", swap)
@@ -402,23 +403,24 @@
         with_core=False,
     )
     middle = (hidden_in.astype(jnp.float32) + attn).astype(jnp.bfloat16)
-    normed2 = gather_rows(rms_scale(middle, ffn_gain))
+    half = TOKENS // SIZE["core"]
+    normed2 = gather_rows(rms_scale(middle, ffn_gain), with_core=False)
     logits = jnp.dot(normed2, router, preferred_element_type=jnp.float32)
-    routes = from_request_order(routes)
+    routes = lax.dynamic_index_in_dim(
+        from_request_order(routes).reshape(SIZE["core"], half, -1), core, axis=0, keepdims=False
+    )
     pair_weights = route_weights(logits, routes)
-    half = TOKENS // SIZE["core"]
-    both = jnp.einsum("td,ekdf->ektf", normed2, w_gate_up, preferred_element_type=jnp.float32)
-    inner = (jax.nn.silu(both[:, 0]) * both[:, 1]).astype(jnp.bfloat16)
-    inner = inner.reshape(n_experts, SIZE["core"], half, -1)
-    inner_mine = lax.dynamic_index_in_dim(inner, core, axis=1, keepdims=False)
-    inner_theirs = lax.dynamic_index_in_dim(inner, 1 - core, axis=1, keepdims=False)
-    inner_sibling = lax.ppermute(inner_theirs, "core", swap)
+
+    def hidden_units(gate_up):
+        both = jnp.einsum("td,ekdf->ektf", normed2, gate_up, preferred_element_type=jnp.float32)
+        return (jax.nn.silu(both[:, 0]) * both[:, 1]).astype(jnp.bfloat16)
+
+    inner_mine = hidden_units(w_gate_up)
+    inner_sibling = hidden_units(w_gate_up_sibling)
     dense_weight = jnp.stack(
         [jnp.sum(jnp.where(routes == expert, pair_weights, 0.0), axis=1) for expert in range(n_experts)]
     )
-    weight_mine = lax.dynamic_index_in_dim(
-        dense_weight.reshape(n_experts, SIZE["core"], half), core, axis=1, keepdims=False
-    )[..., None]
+    weight_mine = dense_weight[..., None]
     scaled_mine = (inner_mine.astype(jnp.float32) * weight_mine).astype(jnp.bfloat16)
     scaled_sibling = (inner_sibling.astype(jnp.float32) * weight_mine).astype(jnp.bfloat16)
     running = jnp.einsum(

time: 189 us -> 177 us (0.937)
  Pallas kernels: 144 us -> 130 us
  local copies, waits for them, and re-layouts: 4.08 us -> 2.08 us
    pallas_call x2, Pallas kernels: 72 us -> 61.9 us  [scatter_rows(): pl.pallas_call(functools.partial(scatter_kernel, with_core), out_shape=ja...]
    pallas_call x2, Pallas kernels: 71.7 us -> 68.6 us  [gather_rows(): pl.pallas_call(functools.partial(gather_kernel, with_core), out_shape=jax...]
    dot_general x1 -> x2, matrix products: 6.74 us -> 9.35 us  [hidden_units(): jnp.einsum('td,ekdf->ektf', normed2, gate_up, preferred_element_type=jnp....]
  transfers between devices with their start and end apart: 6 -> 6, of which waited for: 1 -> 1; matrix products, arithmetic and copies ran while one was open for 10% -> 17% of each run, Pallas kernels for 20% -> 58%
where the time goes in v11:
time: 177 us; the launch traced here: 175 us
  Pallas kernels  130 us (73%)
  matrix products  27.9 us (16%)
  other arithmetic  11.8 us (7%)
  local copies, waits for them, and re-layouts  2.08 us (1%)
  starting transfers between devices  1.79 us (1%)
    pallas_call x2, Pallas kernels, gather_rows(): pl.pallas_call(functools.partial(gather_kernel, with_core), out_shape=jax...  68.6 us
    pallas_call x2, Pallas kernels, scatter_rows(): pl.pallas_call(functools.partial(scatter_kernel, with_core), out_shape=ja...  61.9 us
    dot_general x2, matrix products, hidden_units(): jnp.einsum('td,ekdf->ektf', normed2, gate_up, preferred_element_type=jnp....  9.35 us
    dot_general x1, matrix products, local(): jnp.einsum('etf,efd->td', scaled_sibling, w_down_sibling, preferred_eleme...  4.18 us
  transfers between devices with their start and end apart: 6, of which 1 were waited for; matrix products, arithmetic and copies ran while one was open for 17% of the time, Pallas kernels for 58%

profile of v11, /device:TPU:22, one launch (start us, length us, event | category | flops | bytes accessed | tf_op | source)
XLA Modules:
  0.0 174.9 jit_solution(17306585815532748606)
XLA Ops:
  0.0 2.4 %pad_maximum_fusion = bf16[3,2304,64]{1,2,0:T(8,128)(2,1)} fusion(bf16[1,2304,64]{1,2,0:T(8,128)(2,1)} %bitcast.149, bf16[1,2304,64]{1,2,0:T(8,128)(2,1)} %bitcast.151, bf16[1,2304,64]{1,2,0:T(8,128)(2,1)} %bitcast.153), kind=kLoop, calls=%fused_computation.27 | loop fusion | flops 884736 | bytes 1769472 | tf_op jit(solution)/shard_map/stack | solution.py:362
  2.4 0.5 collective-permute-start.2
  2.9 0.5 collective-permute-start.5
  3.4 0.7 convert_element_type.107
  4.1 1.0 fusion.30
  5.2 1.6 fusion.32.own_ref
  6.8 36.8 %shard_map.136 = bf16[4,4,24,2304]{3,2,1,0:T(8,128)(2,1)} custom-call(bf16[24,2304]{1,0:T(8,128)(2,1)} %fusion.32.own_ref), custom_call_target="tpu_custom_call" | custom-call | tf_op jit(solution)/shard_map/pallas_call | solution.py:211
  44.4 3.0 %convolution_bitcast_fusion.3 = f32[3,384,64]{1,2,0:T(8,128)} fusion(bf16[3,2304,64]{1,2,0:T(8,128)(2,1)S(1)} %collective-permute-done, bf16[384,2304,1]{1,0,2:T(8,128)(2,1)} %bitcast.131), kind=kOutput, calls=%fused_computation.22 | convolution fusion | flops 339738624 | bytes 2949120 | tf_op jit(solution)/shard_map/td,kdf->ktf/dot_general | solution.py:369
  47.5 2.5 %convolution_bitcast_fusion.4 = f32[3,384,64]{1,2,0:T(8,128)S(1)} fusion(bf16[384,2304,1]{1,0,2:T(8,128)(2,1)} %bitcast.132, bf16[1,2304,64]{1,2,0:T(8,128)(2,1)} %bitcast.150, bf16[1,2304,64]{1,2,0:T(8,128)(2,1)} %bitcast.152, bf16[1,2304,64]{1,2,0:T(8,128)(2,1)} %bitcast.154), kind=kOutput, calls=%fused_computation.23 | convolution fusion | flops 340623360 | bytes 2949120 | tf_op jit(solution)/shard_map/td,kdf->ktf/dot_general | solution.py:368
  50.1 0.5 fusion.53
  50.8 0.2 copy.65
  51.8 0.3 fusion.69
  52.1 1.1 fusion
  53.3 1.5 fusion.1
  54.9 1.5 fusion.8
  56.4 0.2 fusion.19
  56.9 0.8 collective-permute-start.3
  57.6 0.6 fusion.56
  58.3 0.3 collective-permute-done.3
  58.6 1.9 %fusion.7 = bf16[384,2304]{1,0:T(8,128)(2,1)} fusion(f32[384,2304]{1,0:T(8,128)S(1)} %fusion.56, bf16[384,64]{1,0:T(8,128)(2,1)S(1)} %collective-permute-done.3, bf16[64,2304]{1,0:T(8,128)(2,1)S(1)} %collective-permute-done.4), kind=kOutput, calls=%fused_computation.12 | convolution fusion | flops 115015680 | bytes 5652480 | tf_op jit(solution)/shard_map/dot_general | solution.py:401
  60.5 32.8 %shard_map.137 = f32[24,2304]{1,0:T(8,128)} custom-call(bf16[4,4,24,2304]{3,2,1,0:T(8,128)(2,1)} %bitcast.136), custom_call_target="tpu_custom_call" | custom-call | tf_op jit(solution)/shard_map/pallas_call | solution.py:303
  93.3 1.1 fusion.34
  94.4 0.7 fusion.36.own_ref
  95.2 31.8 %shard_map.138 = bf16[4,4,24,2304]{3,2,1,0:T(8,128)(2,1)} custom-call(bf16[24,2304]{1,0:T(8,128)(2,1)} %fusion.36.own_ref), custom_call_target="tpu_custom_call" | custom-call | tf_op jit(solution)/shard_map/pallas_call | solution.py:211
  127.0 2.1 %select_reduce_fusion.1 = (f32[384]{0:T(512)S(1)}, f32[384]{0:T(512)S(1)}) fusion(s32[384]{0:T(512)S(1)} %get-tuple-element.17, s32[384]{0:T(512)S(1)} %get-tuple-element.18, bf16[384,2304]{1,0:T(8,128)(2,1)} %bitcast.133, bf16[2304,4]{0,1:T(4,128)(2,1)S(1)} %copy-done.4), kind=kOutput, calls=%fused_computation.93 | convolution fusion | flops 7086336 | bytes 1794048 | tf_op jit(solution)/shard_map/dot_general | solution.py:408
  129.2 5.0 %convolution_bitcast_fusion.2 = f32[4,2,384,128]{3,2,1,0:T(8,128)S(1)} fusion(bf16[384,2304,1,1]{1,0,3,2:T(8,128)(2,1)} %bitcast.134, bf16[4,2,2304,128]{3,2,1,0:T(8,128)(2,1)} %param.26), kind=kOutput, calls=%fused_computation.19 | convolution fusion | flops 1811939328 | bytes 8060928 | tf_op jit(solution)/shard_map/td,ekdf->ektf/dot_general | solution.py:415
  134.2 1.3 convolution_bitcast_fusion.1
  135.5 0.2 copy-done.1
  135.7 4.3 %fusion.14 = f32[4,2,384,128]{3,2,0,1:T(8,128)S(1)} fusion(bf16[384,2304,1,1]{1,0,2,3:T(8,128)(2,1)S(1)} %bitcast.135, bf16[4,2,2304,128]{3,2,1,0:T(8,128)(2,1)} %collective-permute-done.5), kind=kOutput, calls=%fused_computation.18 | convolution fusion | flops 1811939328 | bytes 8060928 | tf_op jit(solution)/shard_map/td,ekdf->ektf/dot_general | solution.py:415
  140.0 4.2 %fusion.6 = bf16[384,2304]{1,0:T(8,128)(2,1)} fusion(f32[384,2304]{1,0:T(8,128)S(1)} %convolution_bitcast_fusion.1, bf16[4,128,2304]{2,1,0:T(8,128)(2,1)} %collective-permute-done.2, f32[4,384]{1,0:T(4,128)S(1)} %pad_maximum_fusion.1, f32[4,2,384,128]{3,2,0,1:T(8,128)S(1)} %fusion.14), kind=kOutput, calls=%fused_computation.11 | convolution fusion | flops 909508608 | bytes 9246720 | tf_op jit(solution)/shard_map/etf,efd->td/dot_general | solution.py:428
  144.2 29.1 %shard_map.139 = f32[24,2304]{1,0:T(8,128)} custom-call(bf16[4,4,24,2304]{3,2,1,0:T(8,128)(2,1)} %bitcast.137), custom_call_target="tpu_custom_call" | custom-call | tf_op jit(solution)/shard_map/pallas_call | solution.py:303
  173.3 1.6 fusion.37
  (73 shorter events, 2.4 us)
Async XLA Ops:
  0.0 52.0 %copy-start = (bf16[8,1,2048,64]{2,3,1,0:T(8,128)(2,1)S(1)}, bf16[8,1,2048,64]{2,3,1,0:T(8,128)(2,1)}, u32[]{:S(2)}) copy-start(bf16[8,1,2048,64]{2,3,1,0:T(8,128)(2,1)} %param.20) | copy-start | bytes 6291460
  0.0 43.6 %copy-start.7 = (s32[8]{0:T(128)S(1)}, s32[8]{0:T(128)}, u32[]{:S(2)}) copy-start(s32[8]{0:T(128)} %param.22) | copy-start | bytes 100
  0.0 43.9 %copy-start.5 = (s32[768,2]{0,1:T(2,128)S(1)}, s32[768,2]{0,1:T(2,128)}, u32[]{:S(2)}) copy-start(s32[768,2]{0,1:T(2,128)} %param.25) | copy-start | bytes 18436
  2.4 42.0 %collective-permute-start = (bf16[3,2304,64]{1,2,0:T(8,128)(2,1)}, bf16[3,2304,64]{1,2,0:T(8,128)(2,1)S(1)}, u32[]{:S(2)}, u32[]{:S(2)}) collective-permute-start(bf16[3,2304,64]{1,2,0:T(8,128)(2,1)} %pad_maximum_fusion), channel_id=1, source_target_pairs={{0,1},{1,0},{2,3},{3,2},{4,5},{5,4},{6,7},{7,6},{8,9},{9,8},{10,11... | collective-permute-start | bytes 2654216 | tf_op jit(solution)/shard_map/ppermute | solution.py:363
  2.4 54.4 %collective-permute-start.2 = (bf16[4,128,2304]{2,1,0:T(8,128)(2,1)}, bf16[4,128,2304]{2,1,0:T(8,128)(2,1)}, u32[]{:S(2)}, u32[]{:S(2)}) collective-permute-start(bf16[4,128,2304]{2,1,0:T(8,128)(2,1)} %param.27), channel_id=1, source_target_pairs={{0,1},{1,0},{2,3},{3,2},{4,5},{5,4},{6,7},{7,6},{8,9},{9,8},{10,11... | collective-permute-start | bytes 7077896 | tf_op jit(solution)/shard_map/ppermute | solution.py:367
  2.9 55.3 %collective-permute-start.4 = (bf16[64,2304]{1,0:T(8,128)(2,1)}, bf16[64,2304]{1,0:T(8,128)(2,1)S(1)}, u32[]{:S(2)}, u32[]{:S(2)}) collective-permute-start(bf16[64,2304]{1,0:T(8,128)(2,1)} %param.19), channel_id=1, source_target_pairs={{0,1},{1,0},{2,3},{3,2},{4,5},{5,4},{6,7},{7,6},{8,9},{9,8},{10,11... | collective-permute-start | bytes 884744 | tf_op jit(solution)/shard_map/ppermute | solution.py:397
  2.9 132.6 %collective-permute-start.5 = (bf16[4,2,2304,128]{3,2,1,0:T(8,128)(2,1)}, bf16[4,2,2304,128]{3,2,1,0:T(8,128)(2,1)}, u32[]{:S(2)}, u32[]{:S(2)}) collective-permute-start(bf16[4,2,2304,128]{3,2,1,0:T(8,128)(2,1)} %param.26), channel_id=1, source_target_pairs={{0,1},{1,0},{2,3},{3,2},{4,5},{5,4},{6,7},{7,6},{8,9},{9,8},{10,11... | collective-permute-start | bytes 14155784 | tf_op jit(solution)/shard_map/ppermute | solution.py:364
  6.8 40.7 %copy-start.6 = (bf16[2304]{0:T(1024)(128)(2,1)S(1)}, bf16[2304]{0:T(1024)(128)(2,1)}, u32[]{:S(2)}) copy-start(bf16[2304]{0:T(1024)(128)(2,1)} %param.23) | copy-start | bytes 13828
  47.3 2.7 %collective-permute-start.1 = (f32[3,384,64]{1,2,0:T(8,128)}, f32[3,384,64]{1,2,0:T(8,128)S(1)}, u32[]{:S(2)}, u32[]{:S(2)}) collective-permute-start(f32[3,384,64]{1,2,0:T(8,128)} %convolution_bitcast_fusion.3), channel_id=1, source_target_pairs={{0,1},{1,0},{2,3},{3,2},{4,5},{5,4},{6,7},{7,6},{8,9},{9,8},{10,11... | collective-permute-start | bytes 884744 | tf_op jit(solution)/shard_map/ppermute | solution.py:372
  53.3 1.6 copy-start.9
  56.4 1.3 copy-start.3
  56.9 1.7 collective-permute-start.3
  58.2 35.1 %copy-start.2 = (bf16[24,2304]{1,0:T(8,128)(2,1)S(1)}, bf16[24,2304]{1,0:T(8,128)(2,1)}, u32[]{:S(2)}) copy-start(bf16[24,2304]{1,0:T(8,128)(2,1)} %param.14) | copy-start | bytes 331780
  60.5 66.5 %copy-start.4 = (bf16[2304,4]{0,1:T(4,128)(2,1)S(1)}, bf16[2304,4]{0,1:T(4,128)(2,1)}, u32[]{:S(2)}) copy-start(bf16[2304,4]{0,1:T(4,128)(2,1)} %param.24) | copy-start | bytes 55300
  129.2 5.0 %copy-start.8 = (bf16[4,128,2304]{2,1,0:T(8,128)(2,1)S(1)}, bf16[4,128,2304]{2,1,0:T(8,128)(2,1)}, u32[]{:S(2)}) copy-start(bf16[4,128,2304]{2,1,0:T(8,128)(2,1)} %param.27) | copy-start | bytes 7077892
  134.2 1.5 copy-start.1

commit v12 on v11

--- a/solution.py
+++ b/solution.py
@@ -359,15 +359,17 @@
     n_experts = w_gate_up.shape[0]
     core = lax.axis_index("core")
     swap = [(0, 1), (1, 0)]
-    w_qkv = jnp.stack([w_query, w_key, w_value])
-    w_qkv_sibling = lax.ppermute(w_qkv, "core", swap)
+    weights = (w_query, w_key, w_value)
+    weights_sibling = [lax.ppermute(weight, "core", swap) for weight in weights]
     w_gate_up_sibling = lax.ppermute(w_gate_up, "core", swap)
     normed_half = gather_rows(rms_scale(hidden_in, attn_gain), with_core=False)
     w_down_later, _ = lax.optimization_barrier((w_down, normed_half))
     w_down_sibling = lax.ppermute(w_down_later, "core", swap)
-    qkv_mine = jnp.einsum("td,kdf->ktf", normed_half, w_qkv, preferred_element_type=jnp.float32)
-    qkv_for_sibling = jnp.einsum(
-        "td,kdf->ktf", normed_half, w_qkv_sibling, preferred_element_type=jnp.float32
+    qkv_mine = jnp.stack(
+        [jnp.dot(normed_half, weight, preferred_element_type=jnp.float32) for weight in weights]
+    )
+    qkv_for_sibling = jnp.stack(
+        [jnp.dot(normed_half, weight, preferred_element_type=jnp.float32) for weight in weights_sibling]
     )
     qkv_other = lax.ppermute(qkv_for_sibling, "core", swap)
     qkv = jnp.where(

time: 177 us -> 183 us (1.034)
  matrix products: 27.9 us -> 32.5 us
  other arithmetic: 11.8 us -> 9.48 us
  waiting for transfers between devices: 0.34 us -> 2.59 us
    dot_general x2 -> x6, matrix products: 5.46 us -> 10 us  [local(): jnp.dot(normed_half, weight, preferred_element_type=jnp.float32)]
    another operation x2, other arithmetic: 2.85 us -> 0.49 us  [the longest x1 2.38 us: local(): w_qkv = jnp.stack([w_query, w_key, w_value])]
    ppermute x1, waiting for transfers between devices: 0.01 us -> 2.06 us  [local(): qkv_other = lax.ppermute(qkv_for_sibling, 'core', swap)]
  transfers between devices with their start and end apart: 6 -> 8, of which waited for: 1 -> 2; matrix products, arithmetic and copies ran while one was open for 17% -> 19% of each run, Pallas kernels for 58% -> 57%
where the time goes in v12:
time: 183 us; the launch traced here: 180 us
  Pallas kernels  130 us (71%)
  matrix products  32.5 us (18%)
  other arithmetic  9.48 us (5%)
  starting transfers between devices  2.59 us (1%)
  waiting for transfers between devices  2.59 us (1%)
  local copies, waits for them, and re-layouts  2.13 us (1%)
    pallas_call x2, Pallas kernels, gather_rows(): pl.pallas_call(functools.partial(gather_kernel, with_core), out_shape=jax...  69.2 us
    pallas_call x2, Pallas kernels, scatter_rows(): pl.pallas_call(functools.partial(scatter_kernel, with_core), out_shape=ja...  61.3 us
    dot_general x6, matrix products, local(): jnp.dot(normed_half, weight, preferred_element_type=jnp.float32)  10 us
    dot_general x2, matrix products, hidden_units(): jnp.einsum('td,ekdf->ektf', normed2, gate_up, preferred_element_type=jnp....  9.35 us
    dot_general x1, matrix products, local(): jnp.einsum('etf,efd->td', scaled_sibling, w_down_sibling, preferred_eleme...  4.18 us
  transfers between devices with their start and end apart: 8, of which 2 were waited for; matrix products, arithmetic and copies ran while one was open for 19% of the time, Pallas kernels for 57%

profile of v12, /device:TPU:22, one launch (start us, length us, event | category | flops | bytes accessed | tf_op | source)
XLA Modules:
  0.0 180.4 jit_solution(14207057084764605750)
XLA Ops:
  0.1 0.5 collective-permute-start.1
  0.7 0.7 convert_element_type.107
  1.5 1.0 fusion.30
  2.5 1.6 fusion.32.own_ref
  4.2 37.2 %shard_map.136 = bf16[4,4,24,2304]{3,2,1,0:T(8,128)(2,1)} custom-call(bf16[24,2304]{1,0:T(8,128)(2,1)} %fusion.32.own_ref), custom_call_target="tpu_custom_call" | custom-call | tf_op jit(solution)/shard_map/pallas_call | solution.py:211
  41.4 0.5 collective-permute-start.6
  41.9 2.1 %convolution_bitcast_fusion.6 = f32[1,384,64]{1,2,0:T(8,128)S(1)} fusion(bf16[384,2304]{1,0:T(8,128)(2,1)} %bitcast.143, bf16[2304,64]{0,1:T(8,128)(2,1)S(1)} %copy-done.5), kind=kOutput, calls=%fused_computation.28 | convolution fusion | flops 113246208 | bytes 2162688 | tf_op jit(solution)/shard_map/dot_general | solution.py:369
  45.0 2.3 %convolution_bitcast_fusion.7 = f32[1,384,64]{1,2,0:T(8,128)S(1)} fusion(bf16[384,2304]{1,0:T(8,128)(2,1)} %bitcast.144, bf16[2304,64]{0,1:T(8,128)(2,1)S(1)} %copy-done.6), kind=kOutput, calls=%fused_computation.29 | convolution fusion | flops 113246208 | bytes 2162688 | tf_op jit(solution)/shard_map/dot_general | solution.py:369
  47.5 1.6 convolution_bitcast_fusion.3
  49.1 1.7 convolution_bitcast_fusion.4
  50.8 1.6 convolution_bitcast_fusion.5
  52.5 0.7 collective-permute-start.3
  53.2 0.7 convolution_bitcast_fusion.8
  53.9 2.1 %collective-permute-done.3 = f32[3,384,64]{1,2,0:T(8,128)S(1)} collective-permute-done((f32[3,384,64]{1,2,0:T(8,128)S(1)}, f32[3,384,64]{1,2,0:T(8,128)S(1)}, u32[]{:S(2)}, u32[]{:S(2)}) %collective-permute-start.3) | collective-permute-done | bytes 294944 | tf_op jit(solution)/shard_map/ppermute | solution.py:374
  56.0 0.5 fusion.53
  58.0 1.1 fusion
  59.2 1.5 fusion.1
  60.8 1.5 fusion.8
  63.3 0.6 fusion.56
  63.9 0.5 collective-permute-done.5
  64.4 1.9 %fusion.7 = bf16[384,2304]{1,0:T(8,128)(2,1)} fusion(f32[384,2304]{1,0:T(8,128)S(1)} %fusion.56, bf16[384,64]{1,0:T(8,128)(2,1)S(1)} %collective-permute-done.5, bf16[64,2304]{1,0:T(8,128)(2,1)S(1)} %collective-permute-done.6), kind=kOutput, calls=%fused_computation.12 | convolution fusion | flops 115015680 | bytes 5652480 | tf_op jit(solution)/shard_map/dot_general | solution.py:403
  66.3 33.2 %shard_map.137 = f32[24,2304]{1,0:T(8,128)} custom-call(bf16[4,4,24,2304]{3,2,1,0:T(8,128)(2,1)} %bitcast.152), custom_call_target="tpu_custom_call" | custom-call | tf_op jit(solution)/shard_map/pallas_call | solution.py:303
  99.5 1.1 fusion.34
  100.6 0.7 fusion.36.own_ref
  101.4 32.1 %shard_map.138 = bf16[4,4,24,2304]{3,2,1,0:T(8,128)(2,1)} custom-call(bf16[24,2304]{1,0:T(8,128)(2,1)} %fusion.36.own_ref), custom_call_target="tpu_custom_call" | custom-call | tf_op jit(solution)/shard_map/pallas_call | solution.py:211
  133.4 2.1 %select_reduce_fusion.1 = (f32[384]{0:T(512)S(1)}, f32[384]{0:T(512)S(1)}) fusion(s32[384]{0:T(512)S(1)} %get-tuple-element.17, s32[384]{0:T(512)S(1)} %get-tuple-element.18, bf16[384,2304]{1,0:T(8,128)(2,1)} %bitcast.149, bf16[2304,4]{0,1:T(4,128)(2,1)S(1)} %copy-done.8), kind=kOutput, calls=%fused_computation.97 | convolution fusion | flops 7086336 | bytes 1794048 | tf_op jit(solution)/shard_map/dot_general | solution.py:410
  135.7 5.0 %convolution_bitcast_fusion.2 = f32[4,2,384,128]{3,2,1,0:T(8,128)S(1)} fusion(bf16[384,2304,1,1]{1,0,3,2:T(8,128)(2,1)} %bitcast.150, bf16[4,2,2304,128]{3,2,1,0:T(8,128)(2,1)} %param.26), kind=kOutput, calls=%fused_computation.19 | convolution fusion | flops 1811939328 | bytes 8060928 | tf_op jit(solution)/shard_map/td,ekdf->ektf/dot_general | solution.py:417
  140.7 1.3 convolution_bitcast_fusion.1
  142.2 4.3 %fusion.14 = f32[4,2,384,128]{3,2,0,1:T(8,128)S(1)} fusion(bf16[384,2304,1,1]{1,0,2,3:T(8,128)(2,1)S(1)} %bitcast.151, bf16[4,2,2304,128]{3,2,1,0:T(8,128)(2,1)} %collective-permute-done.7), kind=kOutput, calls=%fused_computation.18 | convolution fusion | flops 1811939328 | bytes 8060928 | tf_op jit(solution)/shard_map/td,ekdf->ektf/dot_general | solution.py:417
  146.5 4.2 %fusion.6 = bf16[384,2304]{1,0:T(8,128)(2,1)} fusion(f32[384,2304]{1,0:T(8,128)S(1)} %convolution_bitcast_fusion.1, bf16[4,128,2304]{2,1,0:T(8,128)(2,1)} %collective-permute-done.4, f32[4,384]{1,0:T(4,128)S(1)} %pad_maximum_fusion.1, f32[4,2,384,128]{3,2,0,1:T(8,128)S(1)} %fusion.14), kind=kOutput, calls=%fused_computation.11 | convolution fusion | flops 909508608 | bytes 9246720 | tf_op jit(solution)/shard_map/etf,efd->td/dot_general | solution.py:430
  150.7 28.0 %shard_map.139 = f32[24,2304]{1,0:T(8,128)} custom-call(bf16[4,4,24,2304]{3,2,1,0:T(8,128)(2,1)} %bitcast.153), custom_call_target="tpu_custom_call" | custom-call | tf_op jit(solution)/shard_map/pallas_call | solution.py:303
  178.8 1.6 fusion.37
  (89 shorter events, 4.3 us)
Async XLA Ops:
  0.0 58.0 %copy-start = (bf16[8,1,2048,64]{2,3,1,0:T(8,128)(2,1)S(1)}, bf16[8,1,2048,64]{2,3,1,0:T(8,128)(2,1)}, u32[]{:S(2)}) copy-start(bf16[8,1,2048,64]{2,3,1,0:T(8,128)(2,1)} %param.20) | copy-start | bytes 6291460
  0.0 41.9 %copy-start.5 = (bf16[2304,64]{0,1:T(8,128)(2,1)S(1)}, bf16[2304,64]{0,1:T(8,128)(2,1)}, u32[]{:S(2)}) copy-start(bf16[2304,64]{0,1:T(8,128)(2,1)} %param.18) | copy-start | bytes 884740
  0.0 45.0 %copy-start.6 = (bf16[2304,64]{0,1:T(8,128)(2,1)S(1)}, bf16[2304,64]{0,1:T(8,128)(2,1)}, u32[]{:S(2)}) copy-start(bf16[2304,64]{0,1:T(8,128)(2,1)} %param.17) | copy-start | bytes 884740
  0.0 44.1 %copy-start.11 = (s32[8]{0:T(128)S(1)}, s32[8]{0:T(128)}, u32[]{:S(2)}) copy-start(s32[8]{0:T(128)} %param.22) | copy-start | bytes 100
  0.0 44.6 %copy-start.10 = (bf16[2304]{0:T(1024)(128)(2,1)S(1)}, bf16[2304]{0:T(1024)(128)(2,1)}, u32[]{:S(2)}) copy-start(bf16[2304]{0:T(1024)(128)(2,1)} %param.23) | copy-start | bytes 13828
  0.0 44.6 %copy-start.9 = (s32[768,2]{0,1:T(2,128)S(1)}, s32[768,2]{0,1:T(2,128)}, u32[]{:S(2)}) copy-start(s32[768,2]{0,1:T(2,128)} %param.25) | copy-start | bytes 18436
  0.0 47.2 %collective-permute-start.2 = (bf16[2304,64]{0,1:T(8,128)(2,1)}, bf16[2304,64]{0,1:T(8,128)(2,1)}, u32[]{:S(2)}, u32[]{:S(2)}) collective-permute-start(bf16[2304,64]{0,1:T(8,128)(2,1)} %param.18), channel_id=1, source_target_pairs={{0,1},{1,0},{2,3},{3,2},{4,5},{5,4},{6,7},{7,6},{8,9},{9,8},{10,11... | collective-permute-start | bytes 884744 | tf_op jit(solution)/shard_map/ppermute | solution.py:363
  0.1 49.0 %collective-permute-start.1 = (bf16[2304,64]{0,1:T(8,128)(2,1)}, bf16[2304,64]{0,1:T(8,128)(2,1)}, u32[]{:S(2)}, u32[]{:S(2)}) collective-permute-start(bf16[2304,64]{0,1:T(8,128)(2,1)} %param.17), channel_id=1, source_target_pairs={{0,1},{1,0},{2,3},{3,2},{4,5},{5,4},{6,7},{7,6},{8,9},{9,8},{10,11... | collective-permute-start | bytes 884744 | tf_op jit(solution)/shard_map/ppermute | solution.py:363
  0.6 50.2 %collective-permute-start = (bf16[2304,64]{0,1:T(8,128)(2,1)}, bf16[2304,64]{0,1:T(8,128)(2,1)}, u32[]{:S(2)}, u32[]{:S(2)}) collective-permute-start(bf16[2304,64]{0,1:T(8,128)(2,1)} %param.16), channel_id=1, source_target_pairs={{0,1},{1,0},{2,3},{3,2},{4,5},{5,4},{6,7},{7,6},{8,9},{9,8},{10,11... | collective-permute-start | bytes 884744 | tf_op jit(solution)/shard_map/ppermute | solution.py:363
  41.3 21.4 %collective-permute-start.4 = (bf16[4,128,2304]{2,1,0:T(8,128)(2,1)}, bf16[4,128,2304]{2,1,0:T(8,128)(2,1)}, u32[]{:S(2)}, u32[]{:S(2)}) collective-permute-start(bf16[4,128,2304]{2,1,0:T(8,128)(2,1)} %param.27), channel_id=1, source_target_pairs={{0,1},{1,0},{2,3},{3,2},{4,5},{5,4},{6,7},{7,6},{8,9},{9,8},{10,11... | collective-permute-start | bytes 7077896 | tf_op jit(solution)/shard_map/ppermute | solution.py:367
  41.4 22.4 %collective-permute-start.6 = (bf16[64,2304]{1,0:T(8,128)(2,1)}, bf16[64,2304]{1,0:T(8,128)(2,1)S(1)}, u32[]{:S(2)}, u32[]{:S(2)}) collective-permute-start(bf16[64,2304]{1,0:T(8,128)(2,1)} %param.19), channel_id=1, source_target_pairs={{0,1},{1,0},{2,3},{3,2},{4,5},{5,4},{6,7},{7,6},{8,9},{9,8},{10,11... | collective-permute-start | bytes 884744 | tf_op jit(solution)/shard_map/ppermute | solution.py:399
  45.0 2.5 %copy-start.1 = (bf16[4,4,24,2304]{3,2,1,0:T(8,128)(2,1)S(1)}, bf16[4,4,24,2304]{3,2,1,0:T(8,128)(2,1)}, u32[]{:S(2)}) copy-start(bf16[4,4,24,2304]{3,2,1,0:T(8,128)(2,1)} %shard_map.136) | copy-start | bytes 5308420
  47.3 94.7 %collective-permute-start.7 = (bf16[4,2,2304,128]{3,2,1,0:T(8,128)(2,1)}, bf16[4,2,2304,128]{3,2,1,0:T(8,128)(2,1)}, u32[]{:S(2)}, u32[]{:S(2)}) collective-permute-start(bf16[4,2,2304,128]{3,2,1,0:T(8,128)(2,1)} %param.26), channel_id=1, source_target_pairs={{0,1},{1,0},{2,3},{3,2},{4,5},{5,4},{6,7},{7,6},{8,9},{9,8},{10,11... | collective-permute-start | bytes 14155784 | tf_op jit(solution)/shard_map/ppermute | solution.py:364
  49.1 4.1 %copy-start.7 = (bf16[2304,64]{0,1:T(8,128)(2,1)S(1)}, bf16[2304,64]{0,1:T(8,128)(2,1)}, u32[]{:S(2)}) copy-start(bf16[2304,64]{0,1:T(8,128)(2,1)} %param.16) | copy-start | bytes 884740
  52.5 3.4 %collective-permute-start.3 = (f32[3,384,64]{1,2,0:T(8,128)S(1)}, f32[3,384,64]{1,2,0:T(8,128)S(1)}, u32[]{:S(2)}, u32[]{:S(2)}) collective-permute-start(f32[3,384,64]{1,2,0:T(8,128)S(1)} %pad_maximum_fusion), channel_id=1, source_target_pairs={{0,1},{1,0},{2,3},{3,2},{4,5},{5,4},{6,7},{7,6},{8,9},{9,8},{10,11... | collective-permute-start | bytes 884744 | tf_op jit(solution)/shard_map/ppermute | solution.py:374
  59.2 1.6 copy-start.13
  62.3 1.0 copy-start.4
  62.8 1.6 collective-permute-start.5
  63.8 35.7 %copy-start.3 = (bf16[24,2304]{1,0:T(8,128)(2,1)S(1)}, bf16[24,2304]{1,0:T(8,128)(2,1)}, u32[]{:S(2)}) copy-start(bf16[24,2304]{1,0:T(8,128)(2,1)} %param.14) | copy-start | bytes 331780
  66.3 67.1 %copy-start.8 = (bf16[2304,4]{0,1:T(4,128)(2,1)S(1)}, bf16[2304,4]{0,1:T(4,128)(2,1)}, u32[]{:S(2)}) copy-start(bf16[2304,4]{0,1:T(4,128)(2,1)} %param.24) | copy-start | bytes 55300
  135.7 5.0 %copy-start.12 = (bf16[4,128,2304]{2,1,0:T(8,128)(2,1)S(1)}, bf16[4,128,2304]{2,1,0:T(8,128)(2,1)}, u32[]{:S(2)}) copy-start(bf16[4,128,2304]{2,1,0:T(8,128)(2,1)} %param.27) | copy-start | bytes 7077892
  140.7 1.5 copy-start.2

commit v13 on v11

--- a/solution.py
+++ b/solution.py
@@ -389,7 +389,9 @@
         by_request(query), by_request(key_new), by_request(value_new), cache_k, cache_v, cache_len
     )
     heads_flat = from_request_order(heads_out.transpose(0, 2, 1, 3).reshape(TOKENS, head_dev * HDIM))
-    heads_flat, w_down_sibling = lax.optimization_barrier((heads_flat, w_down_sibling))
+    heads_flat, w_down_sibling, w_gate_up_sibling = lax.optimization_barrier(
+        (heads_flat, w_down_sibling, w_gate_up_sibling)
+    )
     by_core = heads_flat.reshape(SIZE["core"], TOKENS // SIZE["core"], head_dev * HDIM)
     mine = lax.dynamic_index_in_dim(by_core, core, axis=0, keepdims=False)
     theirs = lax.dynamic_index_in_dim(by_core, 1 - core, axis=0, keepdims=False)

time: 177 us -> 175 us (0.989)
  transfers between devices with their start and end apart: 6 -> 6, of which waited for: 1 -> 1; matrix products, arithmetic and copies ran while one was open for 17% -> 10% of each run, Pallas kernels for 58% -> 21%
where the time goes in v13:
time: 175 us; the launch traced here: 173 us
  Pallas kernels  130 us (74%)
  matrix products  26.6 us (15%)
  other arithmetic  11.8 us (7%)
  local copies, waits for them, and re-layouts  2.59 us (1%)
  starting transfers between devices  1.79 us (1%)
    pallas_call x2, Pallas kernels, gather_rows(): pl.pallas_call(functools.partial(gather_kernel, with_core), out_shape=jax...  68.6 us
    pallas_call x2, Pallas kernels, scatter_rows(): pl.pallas_call(functools.partial(scatter_kernel, with_core), out_shape=ja...  61.1 us
    dot_general x2, matrix products, hidden_units(): jnp.einsum('td,ekdf->ektf', normed2, gate_up, preferred_element_type=jnp....  9.48 us
    dot_general x1, matrix products, local(): jnp.einsum('etf,efd->td', scaled_sibling, w_down_sibling, preferred_eleme...  4.17 us
  transfers between devices with their start and end apart: 6, of which 1 were waited for; matrix products, arithmetic and copies ran while one was open for 10% of the time, Pallas kernels for 21%

profile of v13, /device:TPU:22, one launch (start us, length us, event | category | flops | bytes accessed | tf_op | source)
XLA Modules:
  0.0 173.3 jit_solution(8281309467649515358)
XLA Ops:
  0.0 2.4 %pad_maximum_fusion = bf16[3,2304,64]{1,2,0:T(8,128)(2,1)} fusion(bf16[1,2304,64]{1,2,0:T(8,128)(2,1)} %bitcast.149, bf16[1,2304,64]{1,2,0:T(8,128)(2,1)} %bitcast.151, bf16[1,2304,64]{1,2,0:T(8,128)(2,1)} %bitcast.153), kind=kLoop, calls=%fused_computation.27 | loop fusion | flops 884736 | bytes 1769472 | tf_op jit(solution)/shard_map/stack | solution.py:362
  2.4 0.5 collective-permute-start.3
  2.9 0.5 collective-permute-start.5
  3.4 0.7 convert_element_type.107
  4.1 1.0 fusion.30
  5.2 0.8 reshape.419
  6.1 1.6 fusion.32.own_ref
  7.7 36.8 %shard_map.136 = bf16[4,4,24,2304]{3,2,1,0:T(8,128)(2,1)} custom-call(bf16[24,2304]{1,0:T(8,128)(2,1)} %fusion.32.own_ref), custom_call_target="tpu_custom_call" | custom-call | tf_op jit(solution)/shard_map/pallas_call | solution.py:211
  45.1 3.0 %convolution_bitcast_fusion.3 = f32[3,384,64]{1,2,0:T(8,128)} fusion(bf16[3,2304,64]{1,2,0:T(8,128)(2,1)S(1)} %collective-permute-done, bf16[384,2304,1]{1,0,2:T(8,128)(2,1)} %bitcast.131), kind=kOutput, calls=%fused_computation.22 | convolution fusion | flops 339738624 | bytes 2949120 | tf_op jit(solution)/shard_map/td,kdf->ktf/dot_general | solution.py:369
  48.2 2.5 %convolution_bitcast_fusion.4 = f32[3,384,64]{1,2,0:T(8,128)S(1)} fusion(bf16[384,2304,1]{1,0,2:T(8,128)(2,1)} %bitcast.132, bf16[1,2304,64]{1,2,0:T(8,128)(2,1)} %bitcast.150, bf16[1,2304,64]{1,2,0:T(8,128)(2,1)} %bitcast.152, bf16[1,2304,64]{1,2,0:T(8,128)(2,1)} %bitcast.154), kind=kOutput, calls=%fused_computation.23 | convolution fusion | flops 340623360 | bytes 2949120 | tf_op jit(solution)/shard_map/td,kdf->ktf/dot_general | solution.py:368
  50.8 0.5 fusion.53
  51.4 0.2 copy.68
  52.5 0.3 fusion.69
  52.7 1.1 fusion
  54.0 1.5 fusion.1
  55.5 1.5 fusion.8
  57.1 0.2 fusion.19
  57.6 0.8 collective-permute-start.4
  58.3 0.6 fusion.56
  59.0 0.3 collective-permute-done.4
  59.3 1.9 %fusion.7 = bf16[384,2304]{1,0:T(8,128)(2,1)} fusion(f32[384,2304]{1,0:T(8,128)S(1)} %fusion.56, bf16[384,64]{1,0:T(8,128)(2,1)S(1)} %collective-permute-done.4, bf16[64,2304]{1,0:T(8,128)(2,1)S(1)} %collective-permute-done.5), kind=kOutput, calls=%fused_computation.12 | convolution fusion | flops 115015680 | bytes 5652480 | tf_op jit(solution)/shard_map/dot_general | solution.py:403
  61.2 32.8 %shard_map.137 = f32[24,2304]{1,0:T(8,128)} custom-call(bf16[4,4,24,2304]{3,2,1,0:T(8,128)(2,1)} %bitcast.136), custom_call_target="tpu_custom_call" | custom-call | tf_op jit(solution)/shard_map/pallas_call | solution.py:303
  94.0 1.1 fusion.34
  95.1 0.7 fusion.36.own_ref
  95.8 31.8 %shard_map.138 = bf16[4,4,24,2304]{3,2,1,0:T(8,128)(2,1)} custom-call(bf16[24,2304]{1,0:T(8,128)(2,1)} %fusion.36.own_ref), custom_call_target="tpu_custom_call" | custom-call | tf_op jit(solution)/shard_map/pallas_call | solution.py:211
  127.7 5.0 %convolution_bitcast_fusion.2 = f32[4,2,384,128]{3,2,1,0:T(8,128)S(1)} fusion(bf16[384,2304,1,1]{1,0,3,2:T(8,128)(2,1)} %bitcast.133, bf16[4,2,2304,128]{3,2,1,0:T(8,128)(2,1)} %param.26), kind=kOutput, calls=%fused_computation.19 | convolution fusion | flops 1811939328 | bytes 8060928 | tf_op jit(solution)/shard_map/td,ekdf->ektf/dot_general | solution.py:417
  132.7 0.6 select_reduce_fusion.1
  133.5 4.5 %fusion.14 = f32[4,2,384,128]{3,2,0,1:T(8,128)S(1)} fusion(bf16[384,2304,1,1]{1,0,2,3:T(8,128)(2,1)S(1)} %bitcast.135, bf16[4,2,2304,128]{3,2,1,0:T(8,128)(2,1)} %collective-permute-done.3), kind=kOutput, calls=%fused_computation.18 | convolution fusion | flops 1811939328 | bytes 8060928 | tf_op jit(solution)/shard_map/td,ekdf->ektf/dot_general | solution.py:417
  138.0 1.2 convolution_bitcast_fusion.1
  139.2 4.2 %fusion.6 = bf16[384,2304]{1,0:T(8,128)(2,1)} fusion(f32[384,2304]{1,0:T(8,128)S(1)} %convolution_bitcast_fusion.1, bf16[4,128,2304]{2,1,0:T(8,128)(2,1)} %collective-permute-done.2, f32[4,384]{1,0:T(4,128)S(1)} %pad_maximum_fusion.1, f32[4,2,384,128]{3,2,0,1:T(8,128)S(1)} %fusion.14), kind=kOutput, calls=%fused_computation.11 | convolution fusion | flops 909508608 | bytes 9246720 | tf_op jit(solution)/shard_map/etf,efd->td/dot_general | solution.py:430
  143.4 28.3 %shard_map.139 = f32[24,2304]{1,0:T(8,128)} custom-call(bf16[4,4,24,2304]{3,2,1,0:T(8,128)(2,1)} %bitcast.137), custom_call_target="tpu_custom_call" | custom-call | tf_op jit(solution)/shard_map/pallas_call | solution.py:303
  171.7 1.6 fusion.37
  (71 shorter events, 2.3 us)
Async XLA Ops:
  0.0 52.7 %copy-start = (bf16[8,1,2048,64]{2,3,1,0:T(8,128)(2,1)S(1)}, bf16[8,1,2048,64]{2,3,1,0:T(8,128)(2,1)}, u32[]{:S(2)}) copy-start(bf16[8,1,2048,64]{2,3,1,0:T(8,128)(2,1)} %param.20) | copy-start | bytes 6291460
  0.0 44.5 %copy-start.6 = (s32[8]{0:T(128)S(1)}, s32[8]{0:T(128)}, u32[]{:S(2)}) copy-start(s32[8]{0:T(128)} %param.22) | copy-start | bytes 100
  2.4 42.7 %collective-permute-start = (bf16[3,2304,64]{1,2,0:T(8,128)(2,1)}, bf16[3,2304,64]{1,2,0:T(8,128)(2,1)S(1)}, u32[]{:S(2)}, u32[]{:S(2)}) collective-permute-start(bf16[3,2304,64]{1,2,0:T(8,128)(2,1)} %pad_maximum_fusion), channel_id=1, source_target_pairs={{0,1},{1,0},{2,3},{3,2},{4,5},{5,4},{6,7},{7,6},{8,9},{9,8},{10,11... | collective-permute-start | bytes 2654216 | tf_op jit(solution)/shard_map/ppermute | solution.py:363
  2.4 55.1 %collective-permute-start.3 = (bf16[4,2,2304,128]{3,2,1,0:T(8,128)(2,1)}, bf16[4,2,2304,128]{3,2,1,0:T(8,128)(2,1)}, u32[]{:S(2)}, u32[]{:S(2)}) collective-permute-start(bf16[4,2,2304,128]{3,2,1,0:T(8,128)(2,1)} %param.26), channel_id=1, source_target_pairs={{0,1},{1,0},{2,3},{3,2},{4,5},{5,4},{6,7},{7,6},{8,9},{9,8},{10,11... | collective-permute-start | bytes 14155784 | tf_op jit(solution)/shard_map/ppermute | solution.py:364
  2.9 54.6 %collective-permute-start.2 = (bf16[4,128,2304]{2,1,0:T(8,128)(2,1)}, bf16[4,128,2304]{2,1,0:T(8,128)(2,1)}, u32[]{:S(2)}, u32[]{:S(2)}) collective-permute-start(bf16[4,128,2304]{2,1,0:T(8,128)(2,1)} %param.27), channel_id=1, source_target_pairs={{0,1},{1,0},{2,3},{3,2},{4,5},{5,4},{6,7},{7,6},{8,9},{9,8},{10,11... | collective-permute-start | bytes 7077896 | tf_op jit(solution)/shard_map/ppermute | solution.py:367
  2.9 56.0 %collective-permute-start.5 = (bf16[64,2304]{1,0:T(8,128)(2,1)}, bf16[64,2304]{1,0:T(8,128)(2,1)S(1)}, u32[]{:S(2)}, u32[]{:S(2)}) collective-permute-start(bf16[64,2304]{1,0:T(8,128)(2,1)} %param.19), channel_id=1, source_target_pairs={{0,1},{1,0},{2,3},{3,2},{4,5},{5,4},{6,7},{7,6},{8,9},{9,8},{10,11... | collective-permute-start | bytes 884744 | tf_op jit(solution)/shard_map/ppermute | solution.py:399
  7.7 40.4 %copy-start.5 = (bf16[2304]{0:T(1024)(128)(2,1)S(1)}, bf16[2304]{0:T(1024)(128)(2,1)}, u32[]{:S(2)}) copy-start(bf16[2304]{0:T(1024)(128)(2,1)} %param.23) | copy-start | bytes 13828
  48.0 2.7 %collective-permute-start.1 = (f32[3,384,64]{1,2,0:T(8,128)}, f32[3,384,64]{1,2,0:T(8,128)S(1)}, u32[]{:S(2)}, u32[]{:S(2)}) collective-permute-start(f32[3,384,64]{1,2,0:T(8,128)} %convolution_bitcast_fusion.3), channel_id=1, source_target_pairs={{0,1},{1,0},{2,3},{3,2},{4,5},{5,4},{6,7},{7,6},{8,9},{9,8},{10,11... | collective-permute-start | bytes 884744 | tf_op jit(solution)/shard_map/ppermute | solution.py:372
  53.9 1.6 copy-start.8
  57.1 1.3 copy-start.3
  57.6 1.7 collective-permute-start.4
  58.9 35.1 %copy-start.2 = (bf16[24,2304]{1,0:T(8,128)(2,1)S(1)}, bf16[24,2304]{1,0:T(8,128)(2,1)}, u32[]{:S(2)}) copy-start(bf16[24,2304]{1,0:T(8,128)(2,1)} %param.14) | copy-start | bytes 331780
  127.7 5.0 %copy-start.1 = (bf16[4,4,24,2304]{3,2,1,0:T(8,128)(2,1)S(1)}, bf16[4,4,24,2304]{3,2,1,0:T(8,128)(2,1)}, u32[]{:S(2)}) copy-start(bf16[4,4,24,2304]{3,2,1,0:T(8,128)(2,1)} %shard_map.138) | copy-start | bytes 5308420
  127.7 5.0 %copy-start.4 = (bf16[2304,4]{0,1:T(4,128)(2,1)S(1)}, bf16[2304,4]{0,1:T(4,128)(2,1)}, u32[]{:S(2)}) copy-start(bf16[2304,4]{0,1:T(4,128)(2,1)} %param.24) | copy-start | bytes 55300
  133.4 4.5 %copy-start.7 = (bf16[4,128,2304]{2,1,0:T(8,128)(2,1)S(1)}, bf16[4,128,2304]{2,1,0:T(8,128)(2,1)}, u32[]{:S(2)}) copy-start(bf16[4,128,2304]{2,1,0:T(8,128)(2,1)} %param.27) | copy-start | bytes 7077892
